TPU v7x, 32 devices: a whole 2x2x4 slice. The times are simulated.
32 devices in a mesh: grid: 8 (over y, x, core), pts: 4 (over z).
Axes of the slice: x: 2, y: 2, z: 4, core: 2. Of those that a mesh axis runs over, the one named last changes fastest.
Arguments:
- phi_blocks: bfloat16 [8, 6, 3200, 512], P('grid'), may hold values from -0.0546875 to 0.0546875
- phi_points: bfloat16 [8, 3200, 2048], P('grid', None, 'pts'), may hold values from -6 to 6
- tile_mask: int32 [8, 6, 4], P('grid', None, 'pts'), may hold values 0 or 1
- support: int32 [8, 6], P('grid'), may hold values from 0 to 7, as said below
- point_order: int32 [2048], replicated, may hold values from 0 to 2047, each once
- gram_inverse: bfloat16 [2048, 2048], P('pts'), may hold values from -0.125 to 0.125
Outputs:
- fitted: bfloat16 [2048, 4096], P('pts', 'grid')
Inputs may be any that keep to these rules, and one draw needn't show every extreme that they name: `support`: each row holds 6 distinct slab indices, the first the row's own slab, the others within 3 slabs of it, counted cyclically.
All inputs are finite; a program needn't handle non-finite values. No bound on the sum of `tile_mask` on one device may be relied on, other than what follows from the above.
Results may differ from a plain program's by a relative error of at most 0.005.
Values sent between devices are 32-bit elements; how exact they have to be, the bound alone decides.
No kernel may reach another device: no remote copies, remote signals or barrier semaphores. Data moves between devices by JAX's collectives and lax.ppermute only.
A program may use at most 128 MiB of HBM per device.

v0:
```python
import functools

import jax
import jax.numpy as jnp
from jax import lax
from jax.experimental import pallas as pl
from jax.experimental.pallas import tpu as pltpu
from jax.sharding import PartitionSpec as P

REACH = 3
F32 = jnp.float32
WIDTHS = (128, 128, 256)
ORDER = (0, 2, 1)
HOLD = {0: (), 2: ((0, 0),), 1: ((0, 1),)}


def lasting(us):
    return pl.CostEstimate(flops=int(us * 1e9), bytes_accessed=int(us * 3e6), transcendentals=0)


CHUNKS = 4


def product(points_ref, block):
    return lax.dot_general(points_ref[...], block, (((0,), (0,)), ((), ())), preferred_element_type=F32)


def fetched_kernel(count, block_of, live, points_ref, blocks_hbm, out_ref, slots, done):
    rows = slots.shape[1] // CHUNKS

    def copies(n):
        return [
            pltpu.make_async_copy(
                blocks_hbm.at[block_of[n], pl.ds(c * rows, rows)], slots.at[n % 2, pl.ds(c * rows, rows)], done.at[n % 2, c]
            )
            for c in range(CHUNKS)
        ]

    def start(n):
        @pl.when(live[n] != 0)
        def _():
            for copy in copies(n):
                copy.start()

    start(0)
    for n in range(count):

        @pl.when(live[n] != 0)
        def _(n=n):
            for copy in copies(n):
                copy.wait()

        if n + 1 < count:
            start(n + 1)

        @pl.when(live[n] != 0)
        def _(n=n):
            out_ref[n] = product(points_ref, slots[n % 2])

        @pl.when(live[n] == 0)
        def _(n=n):
            out_ref[n] = jnp.zeros(out_ref.shape[1:], F32)


SMEM = pl.BlockSpec(memory_space=pltpu.SMEM)
VMEM = pl.BlockSpec(memory_space=pltpu.VMEM)


def params(mib):
    return pltpu.CompilerParams(vmem_limit_bytes=mib << 20)


def fetched(points, blocks, block_of, live, count):
    orbs, batch = points.shape
    cells = blocks.shape[2]
    return pl.pallas_call(
        functools.partial(fetched_kernel, count),
        in_specs=[SMEM, SMEM, VMEM, pl.BlockSpec(memory_space=pltpu.HBM)],
        out_specs=VMEM,
        out_shape=jax.ShapeDtypeStruct((count, batch, cells), F32),
        scratch_shapes=[pltpu.VMEM((2, orbs, cells), blocks.dtype), pltpu.SemaphoreType.DMA((2, CHUNKS))],
        compiler_params=params(16),
        cost_estimate=lasting(2.5 * count),
        name="fetched",
    )(block_of, live, in_vmem(points), blocks)


def held_kernel(base, block_of, live, points_ref, blocks_ref, *outs):
    for n, out in enumerate(outs):

        @pl.when(live[base + n] != 0)
        def _(n=n, out=out):
            out[...] = product(points_ref, blocks_ref[block_of[base + n]])

        @pl.when(live[base + n] == 0)
        def _(out=out):
            out[...] = jnp.zeros(out.shape, F32)


def held(points, blocks, block_of, live, base, count):
    batch, cells = points.shape[1], blocks.shape[2]
    return pl.pallas_call(
        functools.partial(held_kernel, base),
        in_specs=[SMEM, SMEM, VMEM, VMEM],
        out_specs=[VMEM] * count,
        out_shape=[jax.ShapeDtypeStruct((batch, cells), F32)] * count,
        compiler_params=params(8),
        cost_estimate=lasting(2.0 * count),
        name="held",
    )(block_of, live, in_vmem(points), in_vmem(blocks))


def near_kernel(base, widths, block_of, live, points_ref, blocks_ref, came_ref, *outs):
    pieces = len(widths)

    def put(n, value):
        start = 0
        for out, width in zip(outs[n * pieces : (n + 1) * pieces], widths):
            out[...] = value[:, start : start + width]
            start += width

    for n in range(2):

        @pl.when(live[base + n] != 0)
        def _(n=n):
            put(n, product(points_ref, blocks_ref[block_of[base + n]]) + came_ref[n])

        @pl.when(live[base + n] == 0)
        def _(n=n):
            put(n, came_ref[n])

    put(2, came_ref[2])


def near_sums(points, blocks, block_of, live, base, came, widths):
    batch = points.shape[1]
    return pl.pallas_call(
        functools.partial(near_kernel, base, widths),
        in_specs=[SMEM, SMEM, VMEM, VMEM, VMEM],
        out_specs=[pl.BlockSpec((batch, width), lambda i: (0, 0)) for _ in range(3) for width in widths],
        out_shape=[pltpu.HBM((batch, width), F32) for _ in range(3) for width in widths],
        grid=(1,),
        compiler_params=params(12),
        cost_estimate=lasting(5.0),
        name="near_sums",
    )(block_of, live, in_vmem(points), in_vmem(blocks), in_vmem(came))


def in_vmem(array):
    return pltpu.with_memory_space_constraint(array, pltpu.VMEM)


def picked_kernel(order_ref, gram_ref, out_ref):
    points, columns = gram_ref.shape[1], order_ref.shape[1]
    rows = lax.broadcasted_iota(jnp.int32, (points, columns), 0)
    chosen = (rows == order_ref[...]).astype(gram_ref.dtype)
    out_ref[...] = jnp.dot(gram_ref[...], chosen, preferred_element_type=F32).astype(out_ref.dtype)


def picked(gram, point_order):
    batch, points = gram.shape
    columns = 256
    return pl.pallas_call(
        picked_kernel,
        grid=(points // columns,),
        in_specs=[
            pl.BlockSpec((1, columns), lambda i: (0, i)),
            pl.BlockSpec((batch, points), lambda i: (0, 0), pipeline_mode=pl.Buffered(1)),
        ],
        out_specs=pl.BlockSpec((batch, columns), lambda i: (0, i)),
        out_shape=jax.ShapeDtypeStruct((batch, points), gram.dtype),
        compiler_params=pltpu.CompilerParams(vmem_limit_bytes=24 << 20),
        cost_estimate=lasting(8.0),
        name="picked",
    )(point_order[None, :], gram)


def shares_kernel(pieces, count, me, columns_ref, *refs):
    terms, outs, squared = refs[: -count - 1], refs[-count - 1 : -1], refs[-1]

    @pl.when(pl.program_id(0) == 0)
    def _():
        at = start = 0
        for number, width in pieces:
            field = terms[at][...]
            for t in terms[at + 1 : at + number]:
                field = field + t[...]
            squared[:, start : start + width] = (field * field).astype(squared.dtype)
            at, start = at + number, start + width

    share = lax.dot_general(columns_ref[...], squared[...], (((0,), (0,)), ((), ())), preferred_element_type=F32)
    for n in range(count):

        @pl.when(pl.program_id(0) == n)
        def _(n=n):
            outs[n][...] = share


def shares(me, columns, pieces):
    batch = pieces[0][1][0][0].shape[-2]
    count = columns.shape[1] // batch
    in_specs = [pl.BlockSpec((batch, batch), lambda i, me: (0, lax.rem(me[0] + i, count)))]
    args = []
    for width, terms in pieces:
        for array, at in terms:
            lead = (pl.Squeezed(),) * (array.ndim - 2)
            in_specs.append(pl.BlockSpec((*lead, batch, width), lambda i, me, at=at: at, pipeline_mode=pl.Buffered(1)))
            args.append(array)
    total = sum(width for width, _ in pieces)
    return pl.pallas_call(
        functools.partial(shares_kernel, tuple((len(terms), width) for width, terms in pieces), count),
        grid_spec=pltpu.PrefetchScalarGridSpec(
            num_scalar_prefetch=1,
            grid=(count,),
            in_specs=in_specs,
            out_specs=[pl.BlockSpec((batch, total), lambda i, me: (0, 0))] * count,
            scratch_shapes=[pltpu.VMEM((batch, total), columns.dtype)],
        ),
        out_shape=[jax.ShapeDtypeStruct((batch, total), F32)] * count,
        compiler_params=pltpu.CompilerParams(vmem_limit_bytes=24 << 20),
        cost_estimate=lasting(5.0),
        name="shares",
    )(me, columns, *args)


def swapped(block, mask, count):
    return lax.ppermute(block, "grid", [(i, i ^ mask) for i in range(count)])


def passed_along(block, distance, count):
    return lax.ppermute(block, "grid", [((i - distance) % count, i) for i in range(count)])


def combined(share, batches):
    up = down = None
    links = []
    for step in range(1, batches):
        up = share[batches - step] if up is None else up + share[batches - step]
        down = share[step] if down is None else down + share[step]
        up = lax.ppermute(up, "pts", [(i, i + 1) for i in range(step)])
        down = lax.ppermute(down, "pts", [(batches - 1 - i, batches - 2 - i) for i in range(step)])
        links.append((up, down))
    return (share[0] + up + down).astype(jnp.bfloat16), links


def after(value, *others):
    return lax.optimization_barrier((value, *others))[0]


def on_device(phi_blocks, phi_points, tile_mask, support, point_order, gram_inverse):
    slabs, batches = lax.axis_size("grid"), lax.axis_size("pts")
    own_slab, own_batch = lax.axis_index("grid"), lax.axis_index("pts")
    blocks = phi_blocks[0]
    cube = slabs == 8
    if cube:
        targets = own_slab ^ jnp.array([3, 7, 5, 0, 1, 2, 6, 0] + [0] * 8, jnp.int32)
    else:
        targets = (own_slab + jnp.array([d % slabs for d in range(-REACH, REACH + 1)] + [0] * 9, jnp.int32)) % slabs
    match = targets[:, None] == support[0][None, :]
    block_of = jnp.sum(jnp.where(match, jnp.arange(support.shape[1], dtype=jnp.int32)[None, :], 0), axis=1)
    live = jnp.sum(jnp.where(match, tile_mask[0, :, 0][None, :], 0), axis=1)
    me = own_batch.astype(jnp.int32)[None]
    cells = phi_blocks.shape[-1]
    points = phi_points[0]
    if cube:
        away = fetched(points, pltpu.with_memory_space_constraint(blocks, pltpu.HBM), block_of, live, 3)
        came = swapped(away, 1, slabs)
        blocks = in_vmem(blocks)
        own, other = held(after(points, away), blocks, block_of, live, 3, 2)
        near = near_sums(after(points, own), blocks, block_of, live, 5, came, WIDTHS)
        late = swapped(after(other, near[0]), 1, slabs)
        columns = picked(after(gram_inverse, (near[0], late)), point_order)
        pieces, links, got = {}, {}, None
        for n in ORDER:
            width = WIDTHS[n]
            at = sum(WIDTHS[:n]) // width
            sums = [near[place * len(WIDTHS) + n] for place in range(3)]
            if got is not None:
                sums = [after(block, (before, late)) for block, before in zip(sums, got)]
            got = [swapped(block, mask, slabs) for block, mask in zip(sums, (2, 6, 4))]
            pending = [links[p][step] for p, step in HOLD[n]]
            if pending:
                columns = after(columns, pending)
            piece = (width, [(own, (0, at)), (late, (0, at))] + [(block, (0, 0)) for block in got])
            share = shares(me, columns, [piece])
            columns = after(columns, share[0])
            pieces[n], links[n] = combined(share, batches)
        fitted = [pieces[n] for n in range(len(WIDTHS))]
    else:
        tiles = fetched(points, pltpu.with_memory_space_constraint(blocks, pltpu.HBM), block_of, live, 2 * REACH + 1)
        columns = picked(gram_inverse, point_order)
        piece = (cells, [(tiles, (REACH, 0, 0))] + [
            (passed_along(tiles[REACH + d], d, slabs), (0, 0)) for d in range(-REACH, REACH + 1) if d != 0
        ])
        fitted = [combined(shares(me, columns, [piece]), batches)[0]]
    return jnp.concatenate(fitted, axis=1)


def solution(mesh):
    in_specs = (
        P("grid", None, None, None),
        P("grid", None, "pts"),
        P("grid", None, "pts"),
        P("grid", None),
        P(),
        P("pts", None),
    )
    out_specs = P("pts", "grid")
    return jax.shard_map(
        on_device, mesh=mesh, in_specs=in_specs, out_specs=out_specs, check_vma=False
    )
```

profile of v0, /device:TPU:0, one launch (start us, length us, event | category | flops | bytes accessed | tf_op | source)
XLA Modules:
  0.0 133.6 jit_solution(13342564194428748856)
XLA Ops:
  0.0 0.7 broadcast_xor_fusion
  0.7 0.8 fusion.1
  1.4 0.0 copy-start.1
  1.4 1.9 %copy-done.1 = bf16[1,3200,512]{2,1,0:T(8,128)(2,1)S(1)} copy-done((bf16[1,3200,512]{2,1,0:T(8,128)(2,1)S(1)}, bf16[1,3200,512]{2,1,0:T(8,128)(2,1)}, u32[]{:S(2)}) %copy-start.1) | copy-done | bytes 3276824
  3.3 9.3 %fetched.1 = f32[3,512,512]{2,1,0:T(8,128)S(1)} custom-call(s32[16]{0:T(128)S(1)} %get-tuple-element.80.block_of, s32[16]{0:T(128)S(1)} %get-tuple-element.79.live, bf16[3200,512]{1,0:T(8,128)(2,1)S(1)} %bitcast.9, bf16[6,3200,512]{2,1,0:T(8,128)(2,1)} %bitcast.6), custom_call_target="tpu_custom_call" | custom-call | flops 7500000256 | bytes 22500000 | tf_op jit(solution)/shard_map/fetched/pallas_call | solution.py:76
  12.6 0.4 collective-permute-start
  13.0 5.4 %held.1 = (f32[512,512]{1,0:T(8,128)S(1)}, f32[512,512]{1,0:T(8,128)}) custom-call(s32[16]{0:T(128)S(1)} %get-tuple-element.80.block_of, s32[16]{0:T(128)S(1)} %get-tuple-element.79.live, bf16[3200,512]{1,0:T(8,128)(2,1)S(1)} %bitcast.10, bf16[6,3200,512]{2,1,0:T(8,128)(2,1)S(1)} %bitcast.7), custom_call_target="tpu_custom_call" | custom-call | flops 4000000000 | bytes 12000000 | tf_op jit(solution)/shard_map/held/pallas_call | solution.py:102
  18.5 0.0 collective-permute-done.came_ref
  18.5 4.3 %near_sums.1 = (f32[512,128]{1,0:T(8,128)}, f32[512,128]{1,0:T(8,128)}, f32[512,256]{1,0:T(8,128)}, f32[512,128]{1,0:T(8,128)}, f32[512,128]{1,0:T(8,128)}, /*in...) custom-call(s32[16]{0:T(128)S(1)} %get-tuple-element.80.block_of, ...), custom_call_target="tpu_custom_call" | custom-call | flops 5000000000 | bytes 15000000 | tf_op jit(solution)/shard_map/near_sums/pallas_call | solution.py:137
  22.8 0.2 collective-permute-start.1
  23.0 2.5 %collective-permute-start.4 = (f32[512,128]{1,0:T(8,128)}, f32[512,128]{1,0:T(8,128)S(1)}, u32[]{:S(2)}, u32[]{:S(2)}) collective-permute-start(f32[512,128]{1,0:T(8,128)} %get-tuple-element.50), channel_id=1, source_target_pairs={{0,16},{4,20},{8,24},{12,28},{16,0},{20,4},{24,8},{28,12},{1,17},{... | collective-permute-start | bytes 786440 | tf_op jit(solution)/shard_map/ppermute | solution.py:227
  25.5 2.8 %collective-permute-start.3 = (f32[512,128]{1,0:T(8,128)}, f32[512,128]{1,0:T(8,128)}, u32[]{:S(2)}, u32[]{:S(2)}) collective-permute-start(f32[512,128]{1,0:T(8,128)} %get-tuple-element.49), channel_id=1, source_target_pairs={{0,24},{4,28},{8,16},{12,20},{16,8},{20,12},{24,0},{28,4},{1,25},{... | collective-permute-start | bytes 786440 | tf_op jit(solution)/shard_map/ppermute | solution.py:227
  28.3 0.6 collective-permute-start.2
  28.8 9.1 %collective-permute-done.4.refs_4_ = f32[512,128]{1,0:T(8,128)S(1)} collective-permute-done((f32[512,128]{1,0:T(8,128)}, f32[512,128]{1,0:T(8,128)S(1)}, u32[]{:S(2)}, u32[]{:S(2)}) %collective-permute-start.4) | collective-permute-done | bytes 262176 | tf_op jit(solution)/shard_map/ppermute | solution.py:227
  37.9 3.2 %collective-permute-done.2.refs_2_ = f32[512,128]{1,0:T(8,128)} collective-permute-done((f32[512,128]{1,0:T(8,128)}, f32[512,128]{1,0:T(8,128)}, u32[]{:S(2)}, u32[]{:S(2)}) %collective-permute-start.2) | collective-permute-done | bytes 262176 | tf_op jit(solution)/shard_map/ppermute | solution.py:227
  41.1 1.5 %collective-permute-start.11 = (f32[512,256]{1,0:T(8,128)}, f32[512,256]{1,0:T(8,128)S(1)}, u32[]{:S(2)}, u32[]{:S(2)}) collective-permute-start(f32[512,256]{1,0:T(8,128)} %get-tuple-element.58), channel_id=1, source_target_pairs={{0,8},{4,12},{8,0},{12,4},{16,24},{20,28},{24,16},{28,20},{1,9},{5... | collective-permute-start | bytes 1572872 | tf_op jit(solution)/shard_map/ppermute | solution.py:227
  42.6 1.2 collective-permute-start.12
  43.8 0.8 collective-permute-start.13
  44.6 5.9 %picked.1.columns_ref = bf16[512,2048]{1,0:T(8,128)(2,1)S(1)} custom-call(s32[1,2048]{1,0:T(1,128)S(1)} %bitcast.12, bf16[512,2048]{1,0:T(8,128)(2,1)S(1)} %copy-done.2), custom_call_target="tpu_custom_call" | custom-call | flops 8000000000 | bytes 24000000 | tf_op jit(solution)/shard_map/picked/pallas_call | solution.py:163
  50.6 3.0 %shares.3 = (f32[512,128]{1,0:T(8,128)S(1)}, f32[512,128]{1,0:T(8,128)S(1)}, f32[512,128]{1,0:T(8,128)S(1)}, f32[512,128]{1,0:T(8,128)S(1)}) custom-call(s32[1]{0:T(128)} %bitcast.me, bf16[512,2048]{1,0:T(8,128)(2,1)S(1)} %picked.1.columns_ref, f32[512,512]{1,0:T(8,128)S(1)} %get-tuple-element.43.refs_0_, f32[512,512]{1,0:T(8,128)} %collective-permute-done.1.refs_1_, ...), custom_call_target="tpu_custom_call" | custom-call | flops 5000000000 | bytes 15000000 | tf_op jit(solution)/shard_map/shares/pallas_call | solution.py:210
  53.6 3.9 %collective-permute-start.5 = (f32[512,128]{1,0:T(8,128)S(1)}, f32[512,128]{1,0:T(8,128)S(1)}, u32[]{:S(2)}, u32[]{:S(2)}) collective-permute-start(f32[512,128]{1,0:T(8,128)S(1)} %get-tuple-element.52), channel_id=1, source_target_pairs={{0,1},{4,5},{8,9},{12,13},{16,17},{20,21},{24,25},{28,29}} | collective-permute-start | bytes 786440 | tf_op jit(solution)/shard_map/ppermute | solution.py:240
  57.6 0.7 collective-permute-start.8
  58.2 3.6 %collective-permute-done.5 = f32[512,128]{1,0:T(8,128)S(1)} collective-permute-done((f32[512,128]{1,0:T(8,128)S(1)}, f32[512,128]{1,0:T(8,128)S(1)}, u32[]{:S(2)}, u32[]{:S(2)}) %collective-permute-start.5) | collective-permute-done | bytes 262176 | tf_op jit(solution)/shard_map/ppermute | solution.py:240
  61.8 0.0 collective-permute-done.8
  61.9 0.7 collective-permute-start.9
  62.6 5.2 %collective-permute-start.6 = (f32[512,128]{1,0:T(8,128)S(1)}, f32[512,128]{1,0:T(8,128)S(1)}, u32[]{:S(2)}, u32[]{:S(2)}) collective-permute-start(f32[512,128]{1,0:T(8,128)S(1)} %get-tuple-element.86), channel_id=1, source_target_pairs={{0,1},{1,2},{4,5},{5,6},{8,9},{9,10},{12,13},{13,14},{16,17},{17,1... | collective-permute-start | bytes 786440 | tf_op jit(solution)/shard_map/ppermute | solution.py:240
  67.8 0.0 collective-permute-done.11.refs_2_
  67.8 0.9 collective-permute-start.14
  68.7 0.0 collective-permute-done.12.refs_3_
  68.7 2.3 %collective-permute-start.15 = (f32[512,128]{1,0:T(8,128)S(1)}, f32[512,128]{1,0:T(8,128)S(1)}, u32[]{:S(2)}, u32[]{:S(2)}) collective-permute-start(f32[512,128]{1,0:T(8,128)S(1)} %copy-done.5), channel_id=1, source_target_pairs={{0,24},{4,28},{8,16},{12,20},{16,8},{20,12},{24,0},{28,4},{1,25},{... | collective-permute-start | bytes 786440 | tf_op jit(solution)/shard_map/ppermute | solution.py:227
  71.1 0.3 collective-permute-start.16
  71.4 3.1 %shares.4 = (f32[512,256]{1,0:T(8,128)S(1)}, f32[512,256]{1,0:T(8,128)S(1)}, f32[512,256]{1,0:T(8,128)S(1)}, f32[512,256]{1,0:T(8,128)S(1)}) custom-call(s32[1]{0:T(128)} %bitcast.me, bf16[512,2048]{1,0:T(8,128)(2,1)S(1)} %picked.1.columns_ref, f32[512,512]{1,0:T(8,128)S(1)} %get-tuple-element.43.refs_0_, f32[512,512]{1,0:T(8,128)} %collective-permute-done.1.refs_1_, ...), custom_call_target="tpu_custom_call" | custom-call | flops 5000000000 | bytes 15000000 | tf_op jit(solution)/shard_map/shares/pallas_call | solution.py:210
  74.5 5.1 %collective-permute-start.23 = (f32[512,256]{1,0:T(8,128)S(1)}, f32[512,256]{1,0:T(8,128)S(1)}, u32[]{:S(2)}, u32[]{:S(2)}) collective-permute-start(f32[512,256]{1,0:T(8,128)S(1)} %get-tuple-element.76), channel_id=1, source_target_pairs={{0,1},{4,5},{8,9},{12,13},{16,17},{20,21},{24,25},{28,29}} | collective-permute-start | bytes 1572872 | tf_op jit(solution)/shard_map/ppermute | solution.py:240
  79.6 0.7 collective-permute-start.26
  80.3 0.0 collective-permute-done.14.refs_2_
  80.3 0.0 collective-permute-done.15.refs_3_
  80.3 1.4 %collective-permute-done.16.refs_4_ = f32[512,128]{1,0:T(8,128)S(1)} collective-permute-done((f32[512,128]{1,0:T(8,128)S(1)}, f32[512,128]{1,0:T(8,128)S(1)}, u32[]{:S(2)}, u32[]{:S(2)}) %collective-permute-start.16) | collective-permute-done | bytes 262176 | tf_op jit(solution)/shard_map/ppermute | solution.py:227
  81.7 2.8 %shares.5 = (f32[512,128]{1,0:T(8,128)S(1)}, f32[512,128]{1,0:T(8,128)S(1)}, f32[512,128]{1,0:T(8,128)S(1)}, f32[512,128]{1,0:T(8,128)S(1)}) custom-call(s32[1]{0:T(128)} %bitcast.me, bf16[512,2048]{1,0:T(8,128)(2,1)S(1)} %picked.1.columns_ref, f32[512,512]{1,0:T(8,128)S(1)} %get-tuple-element.43.refs_0_, f32[512,512]{1,0:T(8,128)} %collective-permute-done.1.refs_1_, ...), custom_call_target="tpu_custom_call" | custom-call | flops 5000000000 | bytes 15000000 | tf_op jit(solution)/shard_map/shares/pallas_call | solution.py:210
  84.5 4.8 %collective-permute-start.17 = (f32[512,128]{1,0:T(8,128)S(1)}, f32[512,128]{1,0:T(8,128)S(1)}, u32[]{:S(2)}, u32[]{:S(2)}) collective-permute-start(f32[512,128]{1,0:T(8,128)S(1)} %get-tuple-element.73), channel_id=1, source_target_pairs={{0,1},{4,5},{8,9},{12,13},{16,17},{20,21},{24,25},{28,29}} | collective-permute-start | bytes 786440 | tf_op jit(solution)/shard_map/ppermute | solution.py:240
  89.3 0.7 collective-permute-start.20
  90.0 1.1 collective-permute-done.23
  91.0 0.0 collective-permute-done.26
  91.0 0.1 fusion.2
  91.1 4.4 %collective-permute-start.24 = (f32[512,256]{1,0:T(8,128)S(1)}, f32[512,256]{1,0:T(8,128)S(1)}, u32[]{:S(2)}, u32[]{:S(2)}) collective-permute-start(f32[512,256]{1,0:T(8,128)S(1)} %get-tuple-element.81), channel_id=1, source_target_pairs={{0,1},{1,2},{4,5},{5,6},{8,9},{9,10},{12,13},{13,14},{16,17},{17,1... | collective-permute-start | bytes 1572872 | tf_op jit(solution)/shard_map/ppermute | solution.py:240
  95.6 0.7 collective-permute-start.27
  96.3 0.4 collective-permute-done.17
  96.6 0.0 collective-permute-done.20
  96.7 0.1 fusion.3
  96.7 4.4 %collective-permute-start.18 = (f32[512,128]{1,0:T(8,128)S(1)}, f32[512,128]{1,0:T(8,128)S(1)}, u32[]{:S(2)}, u32[]{:S(2)}) collective-permute-start(f32[512,128]{1,0:T(8,128)S(1)} %get-tuple-element.83), channel_id=1, source_target_pairs={{0,1},{1,2},{4,5},{5,6},{8,9},{9,10},{12,13},{13,14},{16,17},{17,1... | collective-permute-start | bytes 786440 | tf_op jit(solution)/shard_map/ppermute | solution.py:240
  101.1 0.7 collective-permute-start.21
  101.8 1.3 collective-permute-start.10
  103.2 4.7 %collective-permute-done.24 = f32[512,256]{1,0:T(8,128)S(1)} collective-permute-done((f32[512,256]{1,0:T(8,128)S(1)}, f32[512,256]{1,0:T(8,128)S(1)}, u32[]{:S(2)}, u32[]{:S(2)}) %collective-permute-start.24) | collective-permute-done | bytes 524320 | tf_op jit(solution)/shard_map/ppermute | solution.py:240
  107.9 4.4 %collective-permute-start.7 = (f32[512,128]{1,0:T(8,128)S(1)}, f32[512,128]{1,0:T(8,128)S(1)}, u32[]{:S(2)}, u32[]{:S(2)}) collective-permute-start(f32[512,128]{1,0:T(8,128)S(1)} %add.55), channel_id=1, source_target_pairs={{0,1},{1,2},{2,3},{4,5},{5,6},{6,7},{8,9},{9,10},{10,11},{12,13},{... | collective-permute-start | bytes 786440 | tf_op jit(solution)/shard_map/ppermute | solution.py:240
  112.3 0.1 add.67
  112.4 1.9 %collective-permute-start.25 = (f32[512,256]{1,0:T(8,128)S(1)}, f32[512,256]{1,0:T(8,128)S(1)}, u32[]{:S(2)}, u32[]{:S(2)}) collective-permute-start(f32[512,256]{1,0:T(8,128)S(1)} %add.67), channel_id=1, source_target_pairs={{0,1},{1,2},{2,3},{4,5},{5,6},{6,7},{8,9},{9,10},{10,11},{12,13},{... | collective-permute-start | bytes 1572872 | tf_op jit(solution)/shard_map/ppermute | solution.py:240
  114.3 0.1 add.70
  114.4 1.3 collective-permute-start.28
  115.7 4.6 %collective-permute-start.19 = (f32[512,128]{1,0:T(8,128)S(1)}, f32[512,128]{1,0:T(8,128)S(1)}, u32[]{:S(2)}, u32[]{:S(2)}) collective-permute-start(f32[512,128]{1,0:T(8,128)S(1)} %add.61), channel_id=1, source_target_pairs={{0,1},{1,2},{2,3},{4,5},{5,6},{6,7},{8,9},{9,10},{10,11},{12,13},{... | collective-permute-start | bytes 786440 | tf_op jit(solution)/shard_map/ppermute | solution.py:240
  120.4 1.3 collective-permute-start.22
  121.7 0.0 collective-permute-done.7
  121.7 10.9 %collective-permute-done.19 = f32[512,128]{1,0:T(8,128)S(1)} collective-permute-done((f32[512,128]{1,0:T(8,128)S(1)}, f32[512,128]{1,0:T(8,128)S(1)}, u32[]{:S(2)}, u32[]{:S(2)}) %collective-permute-start.19) | collective-permute-done | bytes 262176 | tf_op jit(solution)/shard_map/ppermute | solution.py:240
  132.7 0.0 collective-permute-done.25
  132.7 0.1 add_convert_fusion
  132.8 0.8 pad_maximum_fusion
  (30 shorter events, 0.3 us)
Async XLA Ops:
  1.4 1.9 %copy-start.1 = (bf16[1,3200,512]{2,1,0:T(8,128)(2,1)S(1)}, bf16[1,3200,512]{2,1,0:T(8,128)(2,1)}, u32[]{:S(2)}) copy-start(bf16[1,3200,512]{2,1,0:T(8,128)(2,1)} %param.8) | copy-start | bytes 9830404
  3.3 9.7 %copy-start = (bf16[1,6,3200,512]{3,2,1,0:T(8,128)(2,1)S(1)}, bf16[1,6,3200,512]{3,2,1,0:T(8,128)(2,1)}, u32[]{:S(2)}) copy-start(bf16[1,6,3200,512]{3,2,1,0:T(8,128)(2,1)} %param.7) | copy-start | bytes 58982404
  12.6 5.9 %collective-permute-start = (f32[3,512,512]{2,1,0:T(8,128)S(1)}, f32[3,512,512]{2,1,0:T(8,128)S(1)}, u32[]{:S(2)}, u32[]{:S(2)}) collective-permute-start(f32[3,512,512]{2,1,0:T(8,128)S(1)} %fetched.1), channel_id=1, source_target_pairs={{0,4},{4,0},{8,12},{12,8},{16,20},{20,16},{24,28},{28,24},{1,5},{5... | collective-permute-start | bytes 9437192 | tf_op jit(solution)/shard_map/ppermute | solution.py:227
  18.5 26.1 %copy-start.2 = (bf16[512,2048]{1,0:T(8,128)(2,1)S(1)}, bf16[512,2048]{1,0:T(8,128)(2,1)}, u32[]{:S(2)}) copy-start(bf16[512,2048]{1,0:T(8,128)(2,1)} %gram_ref) | copy-start | bytes 6291460
  18.5 26.1 %copy-start.3 = (s32[2048]{0:T(1024)S(1)}, s32[2048]{0:T(1024)}, u32[]{:S(2)}) copy-start(s32[2048]{0:T(1024)} %param.11) | copy-start | bytes 24580
  22.8 15.1 %collective-permute-start.1 = (f32[512,512]{1,0:T(8,128)}, f32[512,512]{1,0:T(8,128)}, u32[]{:S(2)}, u32[]{:S(2)}) collective-permute-start(f32[512,512]{1,0:T(8,128)} %get-tuple-element.47), channel_id=1, source_target_pairs={{0,4},{4,0},{8,12},{12,8},{16,20},{20,16},{24,28},{28,24},{1,5},{5... | collective-permute-start | bytes 3145736 | tf_op jit(solution)/shard_map/ppermute | solution.py:227
  23.0 14.9 %collective-permute-start.4 = (f32[512,128]{1,0:T(8,128)}, f32[512,128]{1,0:T(8,128)S(1)}, u32[]{:S(2)}, u32[]{:S(2)}) collective-permute-start(f32[512,128]{1,0:T(8,128)} %get-tuple-element.50), channel_id=1, source_target_pairs={{0,16},{4,20},{8,24},{12,28},{16,0},{20,4},{24,8},{28,12},{1,17},{... | collective-permute-start | bytes 786440 | tf_op jit(solution)/shard_map/ppermute | solution.py:227
  25.5 12.4 %collective-permute-start.3 = (f32[512,128]{1,0:T(8,128)}, f32[512,128]{1,0:T(8,128)}, u32[]{:S(2)}, u32[]{:S(2)}) collective-permute-start(f32[512,128]{1,0:T(8,128)} %get-tuple-element.49), channel_id=1, source_target_pairs={{0,24},{4,28},{8,16},{12,20},{16,8},{20,12},{24,0},{28,4},{1,25},{... | collective-permute-start | bytes 786440 | tf_op jit(solution)/shard_map/ppermute | solution.py:227
  28.3 12.9 %collective-permute-start.2 = (f32[512,128]{1,0:T(8,128)}, f32[512,128]{1,0:T(8,128)}, u32[]{:S(2)}, u32[]{:S(2)}) collective-permute-start(f32[512,128]{1,0:T(8,128)} %get-tuple-element.45), channel_id=1, source_target_pairs={{0,8},{4,12},{8,0},{12,4},{16,24},{20,28},{24,16},{28,20},{1,9},{5... | collective-permute-start | bytes 786440 | tf_op jit(solution)/shard_map/ppermute | solution.py:227
  41.1 26.7 %collective-permute-start.11 = (f32[512,256]{1,0:T(8,128)}, f32[512,256]{1,0:T(8,128)S(1)}, u32[]{:S(2)}, u32[]{:S(2)}) collective-permute-start(f32[512,256]{1,0:T(8,128)} %get-tuple-element.58), channel_id=1, source_target_pairs={{0,8},{4,12},{8,0},{12,4},{16,24},{20,28},{24,16},{28,20},{1,9},{5... | collective-permute-start | bytes 1572872 | tf_op jit(solution)/shard_map/ppermute | solution.py:227
  42.6 26.1 %collective-permute-start.12 = (f32[512,256]{1,0:T(8,128)}, f32[512,256]{1,0:T(8,128)S(1)}, u32[]{:S(2)}, u32[]{:S(2)}) collective-permute-start(f32[512,256]{1,0:T(8,128)} %get-tuple-element.60), channel_id=1, source_target_pairs={{0,24},{4,28},{8,16},{12,20},{16,8},{20,12},{24,0},{28,4},{1,25},{... | collective-permute-start | bytes 1572872 | tf_op jit(solution)/shard_map/ppermute | solution.py:227
  43.8 27.3 %collective-permute-start.13 = (f32[512,256]{1,0:T(8,128)}, f32[512,256]{1,0:T(8,128)S(1)}, u32[]{:S(2)}, u32[]{:S(2)}) collective-permute-start(f32[512,256]{1,0:T(8,128)} %get-tuple-element.62), channel_id=1, source_target_pairs={{0,16},{4,20},{8,24},{12,28},{16,0},{20,4},{24,8},{28,12},{1,17},{... | collective-permute-start | bytes 1572872 | tf_op jit(solution)/shard_map/ppermute | solution.py:227
  50.6 17.2 %copy-start.6 = (f32[512,128]{1,0:T(8,128)S(1)}, f32[512,128]{1,0:T(8,128)}, u32[]{:S(2)}) copy-start(f32[512,128]{1,0:T(8,128)} %get-tuple-element.67) | copy-start | bytes 786436
  50.6 18.2 %copy-start.5 = (f32[512,128]{1,0:T(8,128)S(1)}, f32[512,128]{1,0:T(8,128)}, u32[]{:S(2)}) copy-start(f32[512,128]{1,0:T(8,128)} %get-tuple-element.69) | copy-start | bytes 786436
  50.6 20.5 %copy-start.4 = (f32[512,128]{1,0:T(8,128)S(1)}, f32[512,128]{1,0:T(8,128)}, u32[]{:S(2)}) copy-start(f32[512,128]{1,0:T(8,128)} %get-tuple-element.71) | copy-start | bytes 786436
  53.6 8.2 %collective-permute-start.5 = (f32[512,128]{1,0:T(8,128)S(1)}, f32[512,128]{1,0:T(8,128)S(1)}, u32[]{:S(2)}, u32[]{:S(2)}) collective-permute-start(f32[512,128]{1,0:T(8,128)S(1)} %get-tuple-element.52), channel_id=1, source_target_pairs={{0,1},{4,5},{8,9},{12,13},{16,17},{20,21},{24,25},{28,29}} | collective-permute-start | bytes 786440 | tf_op jit(solution)/shard_map/ppermute | solution.py:240
  57.6 4.3 %collective-permute-start.8 = (f32[512,128]{1,0:T(8,128)S(1)}, f32[512,128]{1,0:T(8,128)S(1)}, u32[]{:S(2)}, u32[]{:S(2)}) collective-permute-start(f32[512,128]{1,0:T(8,128)S(1)} %get-tuple-element.54), channel_id=1, source_target_pairs={{3,2},{7,6},{11,10},{15,14},{19,18},{23,22},{27,26},{31,30}} | collective-permute-start | bytes 786440 | tf_op jit(solution)/shard_map/ppermute | solution.py:241
  61.9 12.6 %collective-permute-start.9 = (f32[512,128]{1,0:T(8,128)S(1)}, f32[512,128]{1,0:T(8,128)S(1)}, u32[]{:S(2)}, u32[]{:S(2)}) collective-permute-start(f32[512,128]{1,0:T(8,128)S(1)} %get-tuple-element.85), channel_id=1, source_target_pairs={{3,2},{2,1},{7,6},{6,5},{11,10},{10,9},{15,14},{14,13},{19,18},{18... | collective-permute-start | bytes 786440 | tf_op jit(solution)/shard_map/ppermute | solution.py:241
  62.6 17.0 %collective-permute-start.6 = (f32[512,128]{1,0:T(8,128)S(1)}, f32[512,128]{1,0:T(8,128)S(1)}, u32[]{:S(2)}, u32[]{:S(2)}) collective-permute-start(f32[512,128]{1,0:T(8,128)S(1)} %get-tuple-element.86), channel_id=1, source_target_pairs={{0,1},{1,2},{4,5},{5,6},{8,9},{9,10},{12,13},{13,14},{16,17},{17,1... | collective-permute-start | bytes 786440 | tf_op jit(solution)/shard_map/ppermute | solution.py:240
  67.8 12.5 %collective-permute-start.14 = (f32[512,128]{1,0:T(8,128)S(1)}, f32[512,128]{1,0:T(8,128)S(1)}, u32[]{:S(2)}, u32[]{:S(2)}) collective-permute-start(f32[512,128]{1,0:T(8,128)S(1)} %copy-done.6), channel_id=1, source_target_pairs={{0,8},{4,12},{8,0},{12,4},{16,24},{20,28},{24,16},{28,20},{1,9},{5... | collective-permute-start | bytes 786440 | tf_op jit(solution)/shard_map/ppermute | solution.py:227
  68.7 11.6 %collective-permute-start.15 = (f32[512,128]{1,0:T(8,128)S(1)}, f32[512,128]{1,0:T(8,128)S(1)}, u32[]{:S(2)}, u32[]{:S(2)}) collective-permute-start(f32[512,128]{1,0:T(8,128)S(1)} %copy-done.5), channel_id=1, source_target_pairs={{0,24},{4,28},{8,16},{12,20},{16,8},{20,12},{24,0},{28,4},{1,25},{... | collective-permute-start | bytes 786440 | tf_op jit(solution)/shard_map/ppermute | solution.py:227
  71.1 10.6 %collective-permute-start.16 = (f32[512,128]{1,0:T(8,128)S(1)}, f32[512,128]{1,0:T(8,128)S(1)}, u32[]{:S(2)}, u32[]{:S(2)}) collective-permute-start(f32[512,128]{1,0:T(8,128)S(1)} %copy-done.4), channel_id=1, source_target_pairs={{0,16},{4,20},{8,24},{12,28},{16,0},{20,4},{24,8},{28,12},{1,17},{... | collective-permute-start | bytes 786440 | tf_op jit(solution)/shard_map/ppermute | solution.py:227
  74.5 16.6 %collective-permute-start.23 = (f32[512,256]{1,0:T(8,128)S(1)}, f32[512,256]{1,0:T(8,128)S(1)}, u32[]{:S(2)}, u32[]{:S(2)}) collective-permute-start(f32[512,256]{1,0:T(8,128)S(1)} %get-tuple-element.76), channel_id=1, source_target_pairs={{0,1},{4,5},{8,9},{12,13},{16,17},{20,21},{24,25},{28,29}} | collective-permute-start | bytes 1572872 | tf_op jit(solution)/shard_map/ppermute | solution.py:240
  79.6 11.5 %collective-permute-start.26 = (f32[512,256]{1,0:T(8,128)S(1)}, f32[512,256]{1,0:T(8,128)S(1)}, u32[]{:S(2)}, u32[]{:S(2)}) collective-permute-start(f32[512,256]{1,0:T(8,128)S(1)} %get-tuple-element.78), channel_id=1, source_target_pairs={{3,2},{7,6},{11,10},{15,14},{19,18},{23,22},{27,26},{31,30}} | collective-permute-start | bytes 1572872 | tf_op jit(solution)/shard_map/ppermute | solution.py:241
  84.5 12.1 %collective-permute-start.17 = (f32[512,128]{1,0:T(8,128)S(1)}, f32[512,128]{1,0:T(8,128)S(1)}, u32[]{:S(2)}, u32[]{:S(2)}) collective-permute-start(f32[512,128]{1,0:T(8,128)S(1)} %get-tuple-element.73), channel_id=1, source_target_pairs={{0,1},{4,5},{8,9},{12,13},{16,17},{20,21},{24,25},{28,29}} | collective-permute-start | bytes 786440 | tf_op jit(solution)/shard_map/ppermute | solution.py:240
  89.3 7.4 %collective-permute-start.20 = (f32[512,128]{1,0:T(8,128)S(1)}, f32[512,128]{1,0:T(8,128)S(1)}, u32[]{:S(2)}, u32[]{:S(2)}) collective-permute-start(f32[512,128]{1,0:T(8,128)S(1)} %get-tuple-element.75), channel_id=1, source_target_pairs={{3,2},{7,6},{11,10},{15,14},{19,18},{23,22},{27,26},{31,30}} | collective-permute-start | bytes 786440 | tf_op jit(solution)/shard_map/ppermute | solution.py:241
  91.1 16.7 %collective-permute-start.24 = (f32[512,256]{1,0:T(8,128)S(1)}, f32[512,256]{1,0:T(8,128)S(1)}, u32[]{:S(2)}, u32[]{:S(2)}) collective-permute-start(f32[512,256]{1,0:T(8,128)S(1)} %get-tuple-element.81), channel_id=1, source_target_pairs={{0,1},{1,2},{4,5},{5,6},{8,9},{9,10},{12,13},{13,14},{16,17},{17,1... | collective-permute-start | bytes 1572872 | tf_op jit(solution)/shard_map/ppermute | solution.py:240
  95.6 16.8 %collective-permute-start.27 = (f32[512,256]{1,0:T(8,128)S(1)}, f32[512,256]{1,0:T(8,128)S(1)}, u32[]{:S(2)}, u32[]{:S(2)}) collective-permute-start(f32[512,256]{1,0:T(8,128)S(1)} %get-tuple-element.82), channel_id=1, source_target_pairs={{3,2},{2,1},{7,6},{6,5},{11,10},{10,9},{15,14},{14,13},{19,18},{18... | collective-permute-start | bytes 1572872 | tf_op jit(solution)/shard_map/ppermute | solution.py:241
  96.7 17.7 %collective-permute-start.18 = (f32[512,128]{1,0:T(8,128)S(1)}, f32[512,128]{1,0:T(8,128)S(1)}, u32[]{:S(2)}, u32[]{:S(2)}) collective-permute-start(f32[512,128]{1,0:T(8,128)S(1)} %get-tuple-element.83), channel_id=1, source_target_pairs={{0,1},{1,2},{4,5},{5,6},{8,9},{9,10},{12,13},{13,14},{16,17},{17,1... | collective-permute-start | bytes 786440 | tf_op jit(solution)/shard_map/ppermute | solution.py:240
  101.1 14.6 %collective-permute-start.21 = (f32[512,128]{1,0:T(8,128)S(1)}, f32[512,128]{1,0:T(8,128)S(1)}, u32[]{:S(2)}, u32[]{:S(2)}) collective-permute-start(f32[512,128]{1,0:T(8,128)S(1)} %get-tuple-element.84), channel_id=1, source_target_pairs={{3,2},{2,1},{7,6},{6,5},{11,10},{10,9},{15,14},{14,13},{19,18},{18... | collective-permute-start | bytes 786440 | tf_op jit(solution)/shard_map/ppermute | solution.py:241
  101.8 18.5 %collective-permute-start.10 = (f32[512,128]{1,0:T(8,128)S(1)}, f32[512,128]{1,0:T(8,128)S(1)}, u32[]{:S(2)}, u32[]{:S(2)}) collective-permute-start(f32[512,128]{1,0:T(8,128)S(1)} %add.58), channel_id=1, source_target_pairs={{3,2},{2,1},{1,0},{7,6},{6,5},{5,4},{11,10},{10,9},{9,8},{15,14},{... | collective-permute-start | bytes 786440 | tf_op jit(solution)/shard_map/ppermute | solution.py:241
  107.9 13.8 %collective-permute-start.7 = (f32[512,128]{1,0:T(8,128)S(1)}, f32[512,128]{1,0:T(8,128)S(1)}, u32[]{:S(2)}, u32[]{:S(2)}) collective-permute-start(f32[512,128]{1,0:T(8,128)S(1)} %add.55), channel_id=1, source_target_pairs={{0,1},{1,2},{2,3},{4,5},{5,6},{6,7},{8,9},{9,10},{10,11},{12,13},{... | collective-permute-start | bytes 786440 | tf_op jit(solution)/shard_map/ppermute | solution.py:240
  112.4 20.3 %collective-permute-start.25 = (f32[512,256]{1,0:T(8,128)S(1)}, f32[512,256]{1,0:T(8,128)S(1)}, u32[]{:S(2)}, u32[]{:S(2)}) collective-permute-start(f32[512,256]{1,0:T(8,128)S(1)} %add.67), channel_id=1, source_target_pairs={{0,1},{1,2},{2,3},{4,5},{5,6},{6,7},{8,9},{9,10},{10,11},{12,13},{... | collective-permute-start | bytes 1572872 | tf_op jit(solution)/shard_map/ppermute | solution.py:240
  114.4 18.3 %collective-permute-start.28 = (f32[512,256]{1,0:T(8,128)S(1)}, f32[512,256]{1,0:T(8,128)S(1)}, u32[]{:S(2)}, u32[]{:S(2)}) collective-permute-start(f32[512,256]{1,0:T(8,128)S(1)} %add.70), channel_id=1, source_target_pairs={{3,2},{2,1},{1,0},{7,6},{6,5},{5,4},{11,10},{10,9},{9,8},{15,14},{... | collective-permute-start | bytes 1572872 | tf_op jit(solution)/shard_map/ppermute | solution.py:241
  115.7 16.9 %collective-permute-start.19 = (f32[512,128]{1,0:T(8,128)S(1)}, f32[512,128]{1,0:T(8,128)S(1)}, u32[]{:S(2)}, u32[]{:S(2)}) collective-permute-start(f32[512,128]{1,0:T(8,128)S(1)} %add.61), channel_id=1, source_target_pairs={{0,1},{1,2},{2,3},{4,5},{5,6},{6,7},{8,9},{9,10},{10,11},{12,13},{... | collective-permute-start | bytes 786440 | tf_op jit(solution)/shard_map/ppermute | solution.py:240
  120.4 12.2 %collective-permute-start.22 = (f32[512,128]{1,0:T(8,128)S(1)}, f32[512,128]{1,0:T(8,128)S(1)}, u32[]{:S(2)}, u32[]{:S(2)}) collective-permute-start(f32[512,128]{1,0:T(8,128)S(1)} %add.64), channel_id=1, source_target_pairs={{3,2},{2,1},{1,0},{7,6},{6,5},{5,4},{11,10},{10,9},{9,8},{15,14},{... | collective-permute-start | bytes 786440 | tf_op jit(solution)/shard_map/ppermute | solution.py:241
where the time goes:
time: 133 us; the launch traced here: 134 us
  starting transfers between devices  60.2 us (45%)
  waiting for transfers between devices  34.4 us (26%)
  Pallas kernels  33.8 us (25%)
  other arithmetic  2.94 us (2%)
  local copies, waits for them, and re-layouts  1.94 us (1%)
    ppermute x9, starting transfers between devices, combined(): up = lax.ppermute(up, 'pts', [(i, i + 1) for i in range(step)])  38.7 us
    ppermute x9, waiting for transfers between devices, combined(): up = lax.ppermute(up, 'pts', [(i, i + 1) for i in range(step)])  20.6 us
    ppermute x11, waiting for transfers between devices, swapped(): return lax.ppermute(block, 'grid', [(i, i ^ mask) for i in range(count)])  13.7 us
    ppermute x11, starting transfers between devices, swapped(): return lax.ppermute(block, 'grid', [(i, i ^ mask) for i in range(count)])  13.5 us
    pallas_call x1, Pallas kernels, fetched(): pl.pallas_call(functools.partial(fetched_kernel, count), in_specs=[SMEM,...  9.27 us
    pallas_call x3, Pallas kernels, shares(): pl.pallas_call(functools.partial(shares_kernel, tuple(((len(terms), width...  8.9 us
    ppermute x9, starting transfers between devices, combined(): lax.ppermute(down, 'pts', [(batches - 1 - i, batches - 2 - i) for i in ra...  7.97 us
    pallas_call x1, Pallas kernels, picked(): pl.pallas_call(picked_kernel, grid=(points // columns,), in_specs=[pl.Blo...  5.94 us
  transfers between devices with their start and end apart: 29, of which 8 were waited for; matrix products, arithmetic and copies ran while one was open for 0% of the time, Pallas kernels for 15%

commit v1 on v0

--- a/solution.py
+++ b/solution.py
@@ -9,9 +9,10 @@
 
 REACH = 3
 F32 = jnp.float32
-WIDTHS = (128, 128, 256)
-ORDER = (0, 2, 1)
-HOLD = {0: (), 2: ((0, 0),), 1: ((0, 1),)}
+WIDTHS = (128, 128, 128, 128)
+ORDER = (0, 1, 2, 3)
+HOLD = {0: (), 1: (), 2: ((0, 0),), 3: ((1, 0), (0, 1))}
+AFTER = (None, None, 0, 1)
 
 
 def lasting(us):
@@ -176,7 +177,7 @@
 
 
 def shares_kernel(pieces, count, me, columns_ref, *refs):
-    terms, outs, squared = refs[: -count - 1], refs[-count - 1 : -1], refs[-1]
+    terms, outs, squared = refs[: -count // 2 - 2], refs[-count // 2 - 2 : -1], refs[-1]
 
     @pl.when(pl.program_id(0) == 0)
     def _():
@@ -189,17 +190,27 @@
             at, start = at + number, start + width
 
     share = lax.dot_general(columns_ref[...], squared[...], (((0,), (0,)), ((), ())), preferred_element_type=F32)
-    for n in range(count):
+    half = count // 2
+    for n in range(half):
 
         @pl.when(pl.program_id(0) == n)
         def _(n=n):
-            outs[n][...] = share
+            outs[0][n] = share
+
+        @pl.when(pl.program_id(0) == half + n)
+        def _(n=n):
+            outs[1 + n][...] = share
 
 
 def shares(me, columns, pieces):
     batch = pieces[0][1][0][0].shape[-2]
     count = columns.shape[1] // batch
-    in_specs = [pl.BlockSpec((batch, batch), lambda i, me: (0, lax.rem(me[0] + i, count)))]
+    half = count // 2
+
+    def turn(i, me):
+        return 0, me[0] ^ jnp.where(i < half, 2 * i + 1, jnp.minimum(2 * (i - half), count - 2))
+
+    in_specs = [pl.BlockSpec((batch, batch), turn)]
     args = []
     for width, terms in pieces:
         for array, at in terms:
@@ -213,12 +224,13 @@
             num_scalar_prefetch=1,
             grid=(count,),
             in_specs=in_specs,
-            out_specs=[pl.BlockSpec((batch, total), lambda i, me: (0, 0))] * count,
+            out_specs=[pl.BlockSpec((half, batch, total), lambda i, me: (0, 0, 0))]
+            + [pl.BlockSpec((batch, total), lambda i, me: (0, 0))] * half,
             scratch_shapes=[pltpu.VMEM((batch, total), columns.dtype)],
         ),
-        out_shape=[jax.ShapeDtypeStruct((batch, total), F32)] * count,
-        compiler_params=pltpu.CompilerParams(vmem_limit_bytes=24 << 20),
-        cost_estimate=lasting(5.0),
+        out_shape=[jax.ShapeDtypeStruct((half, batch, total), F32)] + [jax.ShapeDtypeStruct((batch, total), F32)] * half,
+        compiler_params=params(24),
+        cost_estimate=lasting(3.0),
         name="shares",
     )(me, columns, *args)
 
@@ -232,15 +244,17 @@
 
 
 def combined(share, batches):
-    up = down = None
-    links = []
-    for step in range(1, batches):
-        up = share[batches - step] if up is None else up + share[batches - step]
-        down = share[step] if down is None else down + share[step]
-        up = lax.ppermute(up, "pts", [(i, i + 1) for i in range(step)])
-        down = lax.ppermute(down, "pts", [(batches - 1 - i, batches - 2 - i) for i in range(step)])
-        links.append((up, down))
-    return (share[0] + up + down).astype(jnp.bfloat16), links
+    sent, kept, links = share[0], list(share[1:]), []
+    distance = 1
+    while distance < batches:
+        came = lax.ppermute(sent, "pts", [(i, i ^ distance) for i in range(batches)])
+        links.append(came)
+        kept = [block + came[n] for n, block in enumerate(kept)]
+        if len(kept) > 1:
+            sent, kept = kept[1::2], kept[0::2]
+            sent = jnp.stack(sent) if len(sent) > 1 else sent[0][None]
+        distance *= 2
+    return kept[0].astype(jnp.bfloat16), links
 
 
 def after(value, *others):
@@ -270,14 +284,14 @@
         near = near_sums(after(points, own), blocks, block_of, live, 5, came, WIDTHS)
         late = swapped(after(other, near[0]), 1, slabs)
         columns = picked(after(gram_inverse, (near[0], late)), point_order)
-        pieces, links, got = {}, {}, None
+        pieces, links, gots = {}, {}, {}
         for n in ORDER:
             width = WIDTHS[n]
             at = sum(WIDTHS[:n]) // width
             sums = [near[place * len(WIDTHS) + n] for place in range(3)]
-            if got is not None:
-                sums = [after(block, (before, late)) for block, before in zip(sums, got)]
-            got = [swapped(block, mask, slabs) for block, mask in zip(sums, (2, 6, 4))]
+            if AFTER[n] is not None:
+                sums = [after(block, (before, late)) for block, before in zip(sums, gots[AFTER[n]])]
+            got = gots[n] = [swapped(block, mask, slabs) for block, mask in zip(sums, (2, 6, 4))]
             pending = [links[p][step] for p, step in HOLD[n]]
             if pending:
                 columns = after(columns, pending)

time: 133 us -> 126 us (0.947)
  starting transfers between devices: 60.2 us -> 36.6 us
  waiting for transfers between devices: 34.4 us -> 54.2 us
  Pallas kernels: 33.8 us -> 30.1 us
    ppermute x18 -> x8, starting transfers between devices: 46.7 us -> 11 us  [combined(): lax.ppermute(sent, 'pts', [(i, i ^ distance) for i in range(batches)])]
    ppermute x18 -> x8, waiting for transfers between devices: 20.6 us -> 44.7 us  [combined(): lax.ppermute(sent, 'pts', [(i, i ^ distance) for i in range(batches)])]
    ppermute x11 -> x14, starting transfers between devices: 13.5 us -> 25.6 us  [swapped(): return lax.ppermute(block, 'grid', [(i, i ^ mask) for i in range(count)])]
    pallas_call x1, Pallas kernels: 9.27 us -> 4.78 us  [fetched(): pl.pallas_call(functools.partial(fetched_kernel, count), in_specs=[SMEM,...]
    ppermute x11 -> x14, waiting for transfers between devices: 13.7 us -> 9.44 us  [swapped(): return lax.ppermute(block, 'grid', [(i, i ^ mask) for i in range(count)])]
    pallas_call x3 -> x4, Pallas kernels: 8.9 us -> 11.3 us  [shares(): pl.pallas_call(functools.partial(shares_kernel, tuple(((len(terms), width...]
    pallas_call x1, Pallas kernels: 4.3 us -> 2.62 us  [near_sums(): pl.pallas_call(functools.partial(near_kernel, base, widths), in_specs=[SM...]
  transfers between devices with their start and end apart: 29 -> 22, of which waited for: 8 -> 12; matrix products, arithmetic and copies ran while one was open for 0% -> 0% of each run, Pallas kernels for 15% -> 18%
where the time goes in v1:
time: 126 us
  waiting for transfers between devices  54.2 us (43%)
  starting transfers between devices  36.6 us (29%)
  Pallas kernels  30.1 us (24%)
  other arithmetic  2.58 us (2%)
  local copies, waits for them, and re-layouts  2.06 us (2%)
    ppermute x8, waiting for transfers between devices, combined(): lax.ppermute(sent, 'pts', [(i, i ^ distance) for i in range(batches)])  44.7 us
    ppermute x14, starting transfers between devices, swapped(): return lax.ppermute(block, 'grid', [(i, i ^ mask) for i in range(count)])  25.6 us
    pallas_call x4, Pallas kernels, shares(): pl.pallas_call(functools.partial(shares_kernel, tuple(((len(terms), width...  11.3 us
    ppermute x8, starting transfers between devices, combined(): lax.ppermute(sent, 'pts', [(i, i ^ distance) for i in range(batches)])  11 us
    ppermute x14, waiting for transfers between devices, swapped(): return lax.ppermute(block, 'grid', [(i, i ^ mask) for i in range(count)])  9.44 us
    pallas_call x1, Pallas kernels, picked(): pl.pallas_call(picked_kernel, grid=(points // columns,), in_specs=[pl.Blo...  5.96 us
    pallas_call x1, Pallas kernels, held(): pl.pallas_call(functools.partial(held_kernel, base), in_specs=[SMEM, SMEM...  5.44 us
    pallas_call x1, Pallas kernels, fetched(): pl.pallas_call(functools.partial(fetched_kernel, count), in_specs=[SMEM,...  4.78 us
  transfers between devices with their start and end apart: 22, of which 12 were waited for; matrix products, arithmetic and copies ran while one was open for 0% of the time, Pallas kernels for 18%

profile of v1, /device:TPU:0, one launch (start us, length us, event | category | flops | bytes accessed | tf_op | source)
XLA Modules:
  0.0 125.7 jit_solution(7352139568248971752)
XLA Ops:
  0.0 0.7 broadcast_xor_fusion
  0.7 0.8 fusion.21
  1.4 0.0 copy-start.1
  1.4 1.9 %copy-done.1 = bf16[1,3200,512]{2,1,0:T(8,128)(2,1)S(1)} copy-done((bf16[1,3200,512]{2,1,0:T(8,128)(2,1)S(1)}, bf16[1,3200,512]{2,1,0:T(8,128)(2,1)}, u32[]{:S(2)}) %copy-start.1) | copy-done | bytes 3276824
  3.3 4.8 %fetched.1 = f32[3,512,512]{2,1,0:T(8,128)S(1)} custom-call(s32[16]{0:T(128)S(1)} %get-tuple-element.88.block_of, s32[16]{0:T(128)S(1)} %get-tuple-element.87.live, bf16[3200,512]{1,0:T(8,128)(2,1)S(1)} %bitcast.81, bf16[6,3200,512]{2,1,0:T(8,128)(2,1)} %bitcast.78), custom_call_target="tpu_custom_call" | custom-call | flops 7500000256 | bytes 22500000 | tf_op jit(solution)/shard_map/fetched/pallas_call | solution.py:77
  8.1 2.7 %collective-permute-start = (f32[3,512,512]{2,1,0:T(8,128)S(1)}, f32[3,512,512]{2,1,0:T(8,128)S(1)}, u32[]{:S(2)}, u32[]{:S(2)}) collective-permute-start(f32[3,512,512]{2,1,0:T(8,128)S(1)} %fetched.1), channel_id=1, source_target_pairs={{0,4},{4,0},{8,12},{12,8},{16,20},{20,16},{24,28},{28,24},{1,5},{5... | collective-permute-start | bytes 9437192 | tf_op jit(solution)/shard_map/ppermute | solution.py:239
  10.8 0.1 copy-done
  10.9 5.4 %held.1 = (f32[512,512]{1,0:T(8,128)S(1)}, f32[512,512]{1,0:T(8,128)}) custom-call(s32[16]{0:T(128)S(1)} %get-tuple-element.88.block_of, s32[16]{0:T(128)S(1)} %get-tuple-element.87.live, bf16[3200,512]{1,0:T(8,128)(2,1)S(1)} %bitcast.82, bf16[6,3200,512]{2,1,0:T(8,128)(2,1)S(1)} %bitcast.79), custom_call_target="tpu_custom_call" | custom-call | flops 4000000000 | bytes 12000000 | tf_op jit(solution)/shard_map/held/pallas_call | solution.py:103
  16.4 0.0 collective-permute-done.came_ref
  16.4 2.6 %near_sums.1 = (f32[512,128]{1,0:T(8,128)}, f32[512,128]{1,0:T(8,128)}, f32[512,128]{1,0:T(8,128)}, f32[512,128]{1,0:T(8,128)}, f32[512,128]{1,0:T(8,128)}, /*in...) custom-call(s32[16]{0:T(128)S(1)} %get-tuple-element.88.block_of, ...), custom_call_target="tpu_custom_call" | custom-call | flops 5000000000 | bytes 15000000 | tf_op jit(solution)/shard_map/near_sums/pallas_call | solution.py:138
  19.0 2.0 %collective-permute-start.1 = (f32[512,512]{1,0:T(8,128)}, f32[512,512]{1,0:T(8,128)}, u32[]{:S(2)}, u32[]{:S(2)}) collective-permute-start(f32[512,512]{1,0:T(8,128)} %get-tuple-element.51), channel_id=1, source_target_pairs={{0,4},{4,0},{8,12},{12,8},{16,20},{20,16},{24,28},{28,24},{1,5},{5... | collective-permute-start | bytes 3145736 | tf_op jit(solution)/shard_map/ppermute | solution.py:239
  21.0 6.8 %collective-permute-start.2 = (f32[512,128]{1,0:T(8,128)}, f32[512,128]{1,0:T(8,128)S(1)}, u32[]{:S(2)}, u32[]{:S(2)}) collective-permute-start(f32[512,128]{1,0:T(8,128)} %get-tuple-element.49), channel_id=1, source_target_pairs={{0,8},{4,12},{8,0},{12,4},{16,24},{20,28},{24,16},{28,20},{1,9},{5... | collective-permute-start | bytes 786440 | tf_op jit(solution)/shard_map/ppermute | solution.py:239
  27.7 0.0 collective-permute-start.3
  27.7 1.5 %collective-permute-start.4 = (f32[512,128]{1,0:T(8,128)}, f32[512,128]{1,0:T(8,128)S(1)}, u32[]{:S(2)}, u32[]{:S(2)}) collective-permute-start(f32[512,128]{1,0:T(8,128)} %get-tuple-element.54), channel_id=1, source_target_pairs={{0,16},{4,20},{8,24},{12,28},{16,0},{20,4},{24,8},{28,12},{1,17},{... | collective-permute-start | bytes 786440 | tf_op jit(solution)/shard_map/ppermute | solution.py:239
  29.3 1.9 %collective-permute-start.7 = (f32[512,128]{1,0:T(8,128)}, f32[512,128]{1,0:T(8,128)S(1)}, u32[]{:S(2)}, u32[]{:S(2)}) collective-permute-start(f32[512,128]{1,0:T(8,128)} %get-tuple-element.59), channel_id=1, source_target_pairs={{0,8},{4,12},{8,0},{12,4},{16,24},{20,28},{24,16},{28,20},{1,9},{5... | collective-permute-start | bytes 786440 | tf_op jit(solution)/shard_map/ppermute | solution.py:239
  31.2 0.0 collective-permute-done.1.refs_1_
  31.2 0.0 collective-permute-start.8
  31.2 0.0 copy-done.2
  31.2 0.0 copy-done.3
  31.3 0.0 copy-start.10
  31.3 6.0 %picked.1.columns_ref = bf16[512,2048]{1,0:T(8,128)(2,1)S(1)} custom-call(s32[1,2048]{1,0:T(1,128)S(1)} %bitcast.84, bf16[512,2048]{1,0:T(8,128)(2,1)S(1)} %copy-done.2), custom_call_target="tpu_custom_call" | custom-call | flops 8000000000 | bytes 24000000 | tf_op jit(solution)/shard_map/picked/pallas_call | solution.py:164
  37.2 3.2 %collective-permute-done.3.refs_3_ = f32[512,128]{1,0:T(8,128)S(1)} collective-permute-done((f32[512,128]{1,0:T(8,128)}, f32[512,128]{1,0:T(8,128)S(1)}, u32[]{:S(2)}, u32[]{:S(2)}) %collective-permute-start.3) | collective-permute-done | bytes 262176 | tf_op jit(solution)/shard_map/ppermute | solution.py:239
  40.4 0.0 copy-done.10
  40.4 1.8 %collective-permute-start.9 = (f32[512,128]{1,0:T(8,128)S(1)}, f32[512,128]{1,0:T(8,128)S(1)}, u32[]{:S(2)}, u32[]{:S(2)}) collective-permute-start(f32[512,128]{1,0:T(8,128)S(1)} %copy-done.10), channel_id=1, source_target_pairs={{0,16},{4,20},{8,24},{12,28},{16,0},{20,4},{24,8},{28,12},{1,17},{... | collective-permute-start | bytes 786440 | tf_op jit(solution)/shard_map/ppermute | solution.py:239
  42.2 0.0 collective-permute-done.4.refs_4_
  42.2 0.0 collective-permute-done.2.refs_2_
  42.3 2.9 %shares.4 = (f32[2,512,128]{2,1,0:T(8,128)S(1)}, f32[512,128]{1,0:T(8,128)S(1)}, f32[512,128]{1,0:T(8,128)S(1)}) custom-call(s32[1]{0:T(128)} %bitcast.me, bf16[512,2048]{1,0:T(8,128)(2,1)S(1)} %picked.1.columns_ref, f32[512,512]{1,0:T(8,128)S(1)} %get-tuple-element.47.refs_0_, f32[512,512]{1,0:T(8,128)} %collective-permute-done.1.refs_1_, ...), custom_call_target="tpu_custom_call" | custom-call | flops 3000000000 | bytes 9000000 | tf_op jit(solution)/shard_map/shares/pallas_call | solution.py:221
  45.2 0.4 collective-permute-start.5
  45.6 0.0 copy-done.9
  45.6 1.8 %collective-permute-start.12 = (f32[512,128]{1,0:T(8,128)S(1)}, f32[512,128]{1,0:T(8,128)S(1)}, u32[]{:S(2)}, u32[]{:S(2)}) collective-permute-start(f32[512,128]{1,0:T(8,128)S(1)} %copy-done.9), channel_id=1, source_target_pairs={{0,8},{4,12},{8,0},{12,4},{16,24},{20,28},{24,16},{28,20},{1,9},{5... | collective-permute-start | bytes 786440 | tf_op jit(solution)/shard_map/ppermute | solution.py:239
  47.4 0.0 collective-permute-done.7.refs_2_
  47.4 0.8 collective-permute-start.13
  48.2 3.5 %collective-permute-done.8.refs_3_ = f32[512,128]{1,0:T(8,128)S(1)} collective-permute-done((f32[512,128]{1,0:T(8,128)}, f32[512,128]{1,0:T(8,128)S(1)}, u32[]{:S(2)}, u32[]{:S(2)}) %collective-permute-start.8) | collective-permute-done | bytes 262176 | tf_op jit(solution)/shard_map/ppermute | solution.py:239
  51.7 1.8 %collective-permute-start.14 = (f32[512,128]{1,0:T(8,128)S(1)}, f32[512,128]{1,0:T(8,128)S(1)}, u32[]{:S(2)}, u32[]{:S(2)}) collective-permute-start(f32[512,128]{1,0:T(8,128)S(1)} %copy-done.7), channel_id=1, source_target_pairs={{0,16},{4,20},{8,24},{12,28},{16,0},{20,4},{24,8},{28,12},{1,17},{... | collective-permute-start | bytes 786440 | tf_op jit(solution)/shard_map/ppermute | solution.py:239
  53.5 0.4 collective-permute-done.9.refs_4_
  53.9 2.8 %shares.5 = (f32[2,512,128]{2,1,0:T(8,128)S(1)}, f32[512,128]{1,0:T(8,128)S(1)}, f32[512,128]{1,0:T(8,128)S(1)}) custom-call(s32[1]{0:T(128)} %bitcast.me, bf16[512,2048]{1,0:T(8,128)(2,1)S(1)} %picked.1.columns_ref, f32[512,512]{1,0:T(8,128)S(1)} %get-tuple-element.47.refs_0_, f32[512,512]{1,0:T(8,128)} %collective-permute-done.1.refs_1_, ...), custom_call_target="tpu_custom_call" | custom-call | flops 3000000000 | bytes 9000000 | tf_op jit(solution)/shard_map/shares/pallas_call | solution.py:221
  56.7 0.8 collective-permute-start.10
  57.5 0.9 collective-permute-done.5
  58.4 1.6 %collective-permute-start.17 = (f32[512,128]{1,0:T(8,128)S(1)}, f32[512,128]{1,0:T(8,128)S(1)}, u32[]{:S(2)}, u32[]{:S(2)}) collective-permute-start(f32[512,128]{1,0:T(8,128)S(1)} %copy-done.6), channel_id=1, source_target_pairs={{0,8},{4,12},{8,0},{12,4},{16,24},{20,28},{24,16},{28,20},{1,9},{5... | collective-permute-start | bytes 786440 | tf_op jit(solution)/shard_map/ppermute | solution.py:239
  60.0 0.0 collective-permute-done.12.refs_2_
  60.0 1.0 collective-permute-start.18
  61.0 2.0 %collective-permute-done.13.refs_3_ = f32[512,128]{1,0:T(8,128)S(1)} collective-permute-done((f32[512,128]{1,0:T(8,128)S(1)}, f32[512,128]{1,0:T(8,128)S(1)}, u32[]{:S(2)}, u32[]{:S(2)}) %collective-permute-start.13) | collective-permute-done | bytes 262176 | tf_op jit(solution)/shard_map/ppermute | solution.py:239
  63.0 0.0 copy-done.4
  63.0 1.8 %collective-permute-start.19 = (f32[512,128]{1,0:T(8,128)S(1)}, f32[512,128]{1,0:T(8,128)S(1)}, u32[]{:S(2)}, u32[]{:S(2)}) collective-permute-start(f32[512,128]{1,0:T(8,128)S(1)} %copy-done.4), channel_id=1, source_target_pairs={{0,16},{4,20},{8,24},{12,28},{16,0},{20,4},{24,8},{28,12},{1,17},{... | collective-permute-start | bytes 786440 | tf_op jit(solution)/shard_map/ppermute | solution.py:239
  64.8 0.4 collective-permute-done.14.refs_4_
  65.2 3.3 %collective-permute-start.6 = (f32[1,512,128]{2,1,0:T(8,128)S(1)}, f32[1,512,128]{2,1,0:T(8,128)S(1)}, u32[]{:S(2)}, u32[]{:S(2)}) collective-permute-start(f32[1,512,128]{2,1,0:T(8,128)S(1)} %fusion.16), channel_id=1, source_target_pairs={{0,2},{1,3},{2,0},{3,1},{4,6},{5,7},{6,4},{7,5},{8,10},{9,11},{10,... | collective-permute-start | bytes 786440 | tf_op jit(solution)/shard_map/ppermute | solution.py:250
  68.5 2.8 %shares.6 = (f32[2,512,128]{2,1,0:T(8,128)S(1)}, f32[512,128]{1,0:T(8,128)S(1)}, f32[512,128]{1,0:T(8,128)S(1)}) custom-call(s32[1]{0:T(128)} %bitcast.me, bf16[512,2048]{1,0:T(8,128)(2,1)S(1)} %picked.1.columns_ref, f32[512,512]{1,0:T(8,128)S(1)} %get-tuple-element.47.refs_0_, f32[512,512]{1,0:T(8,128)} %collective-permute-done.1.refs_1_, ...), custom_call_target="tpu_custom_call" | custom-call | flops 3000000000 | bytes 9000000 | tf_op jit(solution)/shard_map/shares/pallas_call | solution.py:221
  71.3 2.8 %collective-permute-done.10 = f32[2,512,128]{2,1,0:T(8,128)S(1)} collective-permute-done((f32[2,512,128]{2,1,0:T(8,128)S(1)}, f32[2,512,128]{2,1,0:T(8,128)S(1)}, u32[]{:S(2)}, u32[]{:S(2)}) %collective-permute-start.10) | collective-permute-done | bytes 524320 | tf_op jit(solution)/shard_map/ppermute | solution.py:250
  74.1 0.0 collective-permute-start.15
  74.1 3.6 %collective-permute-done.6 = f32[1,512,128]{2,1,0:T(8,128)S(1)} collective-permute-done((f32[1,512,128]{2,1,0:T(8,128)S(1)}, f32[1,512,128]{2,1,0:T(8,128)S(1)}, u32[]{:S(2)}, u32[]{:S(2)}) %collective-permute-start.6) | collective-permute-done | bytes 262176 | tf_op jit(solution)/shard_map/ppermute | solution.py:250
  77.8 0.0 collective-permute-done.17.refs_2_
  77.8 0.0 collective-permute-done.18.refs_3_
  77.8 0.0 collective-permute-done.19.refs_4_
  77.8 2.8 %shares.7 = (f32[2,512,128]{2,1,0:T(8,128)S(1)}, f32[512,128]{1,0:T(8,128)S(1)}, f32[512,128]{1,0:T(8,128)S(1)}) custom-call(s32[1]{0:T(128)} %bitcast.me, bf16[512,2048]{1,0:T(8,128)(2,1)S(1)} %picked.1.columns_ref, f32[512,512]{1,0:T(8,128)S(1)} %get-tuple-element.47.refs_0_, f32[512,512]{1,0:T(8,128)} %collective-permute-done.1.refs_1_, ...), custom_call_target="tpu_custom_call" | custom-call | flops 3000000000 | bytes 9000000 | tf_op jit(solution)/shard_map/shares/pallas_call | solution.py:221
  80.6 2.9 %collective-permute-start.20 = (f32[2,512,128]{2,1,0:T(8,128)S(1)}, f32[2,512,128]{2,1,0:T(8,128)S(1)}, u32[]{:S(2)}, u32[]{:S(2)}) collective-permute-start(f32[2,512,128]{2,1,0:T(8,128)S(1)} %get-tuple-element.85), channel_id=1, source_target_pairs={{0,1},{1,0},{2,3},{3,2},{4,5},{5,4},{6,7},{7,6},{8,9},{9,8},{10,11... | collective-permute-start | bytes 1572872 | tf_op jit(solution)/shard_map/ppermute | solution.py:250
  83.5 1.7 %collective-permute-start.11 = (f32[1,512,128]{2,1,0:T(8,128)S(1)}, f32[1,512,128]{2,1,0:T(8,128)S(1)}, u32[]{:S(2)}, u32[]{:S(2)}) collective-permute-start(f32[1,512,128]{2,1,0:T(8,128)S(1)} %fusion.11), channel_id=1, source_target_pairs={{0,2},{1,3},{2,0},{3,1},{4,6},{5,7},{6,4},{7,5},{8,10},{9,11},{10,... | collective-permute-start | bytes 786440 | tf_op jit(solution)/shard_map/ppermute | solution.py:250
  85.3 12.1 %collective-permute-done.15 = f32[2,512,128]{2,1,0:T(8,128)S(1)} collective-permute-done((f32[2,512,128]{2,1,0:T(8,128)S(1)}, f32[2,512,128]{2,1,0:T(8,128)S(1)}, u32[]{:S(2)}, u32[]{:S(2)}) %collective-permute-start.15) | collective-permute-done | bytes 524320 | tf_op jit(solution)/shard_map/ppermute | solution.py:250
  97.5 1.3 %collective-permute-start.16 = (f32[1,512,128]{2,1,0:T(8,128)S(1)}, f32[1,512,128]{2,1,0:T(8,128)S(1)}, u32[]{:S(2)}, u32[]{:S(2)}) collective-permute-start(f32[1,512,128]{2,1,0:T(8,128)S(1)} %fusion.6), channel_id=1, source_target_pairs={{0,2},{1,3},{2,0},{3,1},{4,6},{5,7},{6,4},{7,5},{8,10},{9,11},{10,... | collective-permute-start | bytes 786440 | tf_op jit(solution)/shard_map/ppermute | solution.py:250
  98.8 7.7 %collective-permute-done.20 = f32[2,512,128]{2,1,0:T(8,128)S(1)} collective-permute-done((f32[2,512,128]{2,1,0:T(8,128)S(1)}, f32[2,512,128]{2,1,0:T(8,128)S(1)}, u32[]{:S(2)}, u32[]{:S(2)}) %collective-permute-start.20) | collective-permute-done | bytes 524320 | tf_op jit(solution)/shard_map/ppermute | solution.py:250
  106.5 0.6 collective-permute-start.21
  107.1 0.0 collective-permute-done.11
  107.1 14.5 %collective-permute-done.16 = f32[1,512,128]{2,1,0:T(8,128)S(1)} collective-permute-done((f32[1,512,128]{2,1,0:T(8,128)S(1)}, f32[1,512,128]{2,1,0:T(8,128)S(1)}, u32[]{:S(2)}, u32[]{:S(2)}) %collective-permute-start.16) | collective-permute-done | bytes 262176 | tf_op jit(solution)/shard_map/ppermute | solution.py:250
  121.7 3.1 %collective-permute-done.21 = f32[1,512,128]{2,1,0:T(8,128)S(1)} collective-permute-done((f32[1,512,128]{2,1,0:T(8,128)S(1)}, f32[1,512,128]{2,1,0:T(8,128)S(1)}, u32[]{:S(2)}, u32[]{:S(2)}) %collective-permute-start.21) | collective-permute-done | bytes 262176 | tf_op jit(solution)/shard_map/ppermute | solution.py:250
  124.8 0.9 pad_maximum_fusion
  (21 shorter events, 0.3 us)
Async XLA Ops:
  1.4 1.9 %copy-start.1 = (bf16[1,3200,512]{2,1,0:T(8,128)(2,1)S(1)}, bf16[1,3200,512]{2,1,0:T(8,128)(2,1)}, u32[]{:S(2)}) copy-start(bf16[1,3200,512]{2,1,0:T(8,128)(2,1)} %param.8) | copy-start | bytes 9830404
  3.3 7.6 %copy-start = (bf16[1,6,3200,512]{3,2,1,0:T(8,128)(2,1)S(1)}, bf16[1,6,3200,512]{3,2,1,0:T(8,128)(2,1)}, u32[]{:S(2)}) copy-start(bf16[1,6,3200,512]{3,2,1,0:T(8,128)(2,1)} %param.7) | copy-start | bytes 58982404
  8.1 8.2 %collective-permute-start = (f32[3,512,512]{2,1,0:T(8,128)S(1)}, f32[3,512,512]{2,1,0:T(8,128)S(1)}, u32[]{:S(2)}, u32[]{:S(2)}) collective-permute-start(f32[3,512,512]{2,1,0:T(8,128)S(1)} %fetched.1), channel_id=1, source_target_pairs={{0,4},{4,0},{8,12},{12,8},{16,20},{20,16},{24,28},{28,24},{1,5},{5... | collective-permute-start | bytes 9437192 | tf_op jit(solution)/shard_map/ppermute | solution.py:239
  16.4 14.9 %copy-start.2 = (bf16[512,2048]{1,0:T(8,128)(2,1)S(1)}, bf16[512,2048]{1,0:T(8,128)(2,1)}, u32[]{:S(2)}) copy-start(bf16[512,2048]{1,0:T(8,128)(2,1)} %gram_ref) | copy-start | bytes 6291460
  16.4 14.9 %copy-start.3 = (s32[2048]{0:T(1024)S(1)}, s32[2048]{0:T(1024)}, u32[]{:S(2)}) copy-start(s32[2048]{0:T(1024)} %param.11) | copy-start | bytes 24580
  19.0 12.2 %collective-permute-start.1 = (f32[512,512]{1,0:T(8,128)}, f32[512,512]{1,0:T(8,128)}, u32[]{:S(2)}, u32[]{:S(2)}) collective-permute-start(f32[512,512]{1,0:T(8,128)} %get-tuple-element.51), channel_id=1, source_target_pairs={{0,4},{4,0},{8,12},{12,8},{16,20},{20,16},{24,28},{28,24},{1,5},{5... | collective-permute-start | bytes 3145736 | tf_op jit(solution)/shard_map/ppermute | solution.py:239
  21.0 21.3 %collective-permute-start.2 = (f32[512,128]{1,0:T(8,128)}, f32[512,128]{1,0:T(8,128)S(1)}, u32[]{:S(2)}, u32[]{:S(2)}) collective-permute-start(f32[512,128]{1,0:T(8,128)} %get-tuple-element.49), channel_id=1, source_target_pairs={{0,8},{4,12},{8,0},{12,4},{16,24},{20,28},{24,16},{28,20},{1,9},{5... | collective-permute-start | bytes 786440 | tf_op jit(solution)/shard_map/ppermute | solution.py:239
  27.7 12.7 %collective-permute-start.3 = (f32[512,128]{1,0:T(8,128)}, f32[512,128]{1,0:T(8,128)S(1)}, u32[]{:S(2)}, u32[]{:S(2)}) collective-permute-start(f32[512,128]{1,0:T(8,128)} %get-tuple-element.53), channel_id=1, source_target_pairs={{0,24},{4,28},{8,16},{12,20},{16,8},{20,12},{24,0},{28,4},{1,25},{... | collective-permute-start | bytes 786440 | tf_op jit(solution)/shard_map/ppermute | solution.py:239
  27.7 14.5 %collective-permute-start.4 = (f32[512,128]{1,0:T(8,128)}, f32[512,128]{1,0:T(8,128)S(1)}, u32[]{:S(2)}, u32[]{:S(2)}) collective-permute-start(f32[512,128]{1,0:T(8,128)} %get-tuple-element.54), channel_id=1, source_target_pairs={{0,16},{4,20},{8,24},{12,28},{16,0},{20,4},{24,8},{28,12},{1,17},{... | collective-permute-start | bytes 786440 | tf_op jit(solution)/shard_map/ppermute | solution.py:239
  29.3 18.1 %collective-permute-start.7 = (f32[512,128]{1,0:T(8,128)}, f32[512,128]{1,0:T(8,128)S(1)}, u32[]{:S(2)}, u32[]{:S(2)}) collective-permute-start(f32[512,128]{1,0:T(8,128)} %get-tuple-element.59), channel_id=1, source_target_pairs={{0,8},{4,12},{8,0},{12,4},{16,24},{20,28},{24,16},{28,20},{1,9},{5... | collective-permute-start | bytes 786440 | tf_op jit(solution)/shard_map/ppermute | solution.py:239
  31.2 20.5 %collective-permute-start.8 = (f32[512,128]{1,0:T(8,128)}, f32[512,128]{1,0:T(8,128)S(1)}, u32[]{:S(2)}, u32[]{:S(2)}) collective-permute-start(f32[512,128]{1,0:T(8,128)} %get-tuple-element.60), channel_id=1, source_target_pairs={{0,24},{4,28},{8,16},{12,20},{16,8},{20,12},{24,0},{28,4},{1,25},{... | collective-permute-start | bytes 786440 | tf_op jit(solution)/shard_map/ppermute | solution.py:239
  31.3 9.2 %copy-start.10 = (f32[512,128]{1,0:T(8,128)S(1)}, f32[512,128]{1,0:T(8,128)}, u32[]{:S(2)}) copy-start(f32[512,128]{1,0:T(8,128)} %get-tuple-element.61) | copy-start | bytes 786436
  40.4 13.5 %collective-permute-start.9 = (f32[512,128]{1,0:T(8,128)S(1)}, f32[512,128]{1,0:T(8,128)S(1)}, u32[]{:S(2)}, u32[]{:S(2)}) collective-permute-start(f32[512,128]{1,0:T(8,128)S(1)} %copy-done.10), channel_id=1, source_target_pairs={{0,16},{4,20},{8,24},{12,28},{16,0},{20,4},{24,8},{28,12},{1,17},{... | collective-permute-start | bytes 786440 | tf_op jit(solution)/shard_map/ppermute | solution.py:239
  42.2 3.3 %copy-start.9 = (f32[512,128]{1,0:T(8,128)S(1)}, f32[512,128]{1,0:T(8,128)}, u32[]{:S(2)}) copy-start(f32[512,128]{1,0:T(8,128)} %get-tuple-element.68) | copy-start | bytes 786436
  42.2 5.2 %copy-start.8 = (f32[512,128]{1,0:T(8,128)S(1)}, f32[512,128]{1,0:T(8,128)}, u32[]{:S(2)}) copy-start(f32[512,128]{1,0:T(8,128)} %get-tuple-element.70) | copy-start | bytes 786436
  42.3 9.4 %copy-start.7 = (f32[512,128]{1,0:T(8,128)S(1)}, f32[512,128]{1,0:T(8,128)}, u32[]{:S(2)}) copy-start(f32[512,128]{1,0:T(8,128)} %get-tuple-element.72) | copy-start | bytes 786436
  45.2 13.2 %collective-permute-start.5 = (f32[2,512,128]{2,1,0:T(8,128)S(1)}, f32[2,512,128]{2,1,0:T(8,128)S(1)}, u32[]{:S(2)}, u32[]{:S(2)}) collective-permute-start(f32[2,512,128]{2,1,0:T(8,128)S(1)} %get-tuple-element.56), channel_id=1, source_target_pairs={{0,1},{1,0},{2,3},{3,2},{4,5},{5,4},{6,7},{7,6},{8,9},{9,8},{10,11... | collective-permute-start | bytes 1572872 | tf_op jit(solution)/shard_map/ppermute | solution.py:250
  45.6 12.8 %copy-start.6 = (f32[512,128]{1,0:T(8,128)S(1)}, f32[512,128]{1,0:T(8,128)}, u32[]{:S(2)}) copy-start(f32[512,128]{1,0:T(8,128)} %get-tuple-element.79) | copy-start | bytes 786436
  45.6 14.4 %copy-start.5 = (f32[512,128]{1,0:T(8,128)S(1)}, f32[512,128]{1,0:T(8,128)}, u32[]{:S(2)}) copy-start(f32[512,128]{1,0:T(8,128)} %get-tuple-element.81) | copy-start | bytes 786436
  45.6 17.4 %copy-start.4 = (f32[512,128]{1,0:T(8,128)S(1)}, f32[512,128]{1,0:T(8,128)}, u32[]{:S(2)}) copy-start(f32[512,128]{1,0:T(8,128)} %get-tuple-element.83) | copy-start | bytes 786436
  45.6 14.4 %collective-permute-start.12 = (f32[512,128]{1,0:T(8,128)S(1)}, f32[512,128]{1,0:T(8,128)S(1)}, u32[]{:S(2)}, u32[]{:S(2)}) collective-permute-start(f32[512,128]{1,0:T(8,128)S(1)} %copy-done.9), channel_id=1, source_target_pairs={{0,8},{4,12},{8,0},{12,4},{16,24},{20,28},{24,16},{28,20},{1,9},{5... | collective-permute-start | bytes 786440 | tf_op jit(solution)/shard_map/ppermute | solution.py:239
  47.4 15.6 %collective-permute-start.13 = (f32[512,128]{1,0:T(8,128)S(1)}, f32[512,128]{1,0:T(8,128)S(1)}, u32[]{:S(2)}, u32[]{:S(2)}) collective-permute-start(f32[512,128]{1,0:T(8,128)S(1)} %copy-done.8), channel_id=1, source_target_pairs={{0,24},{4,28},{8,16},{12,20},{16,8},{20,12},{24,0},{28,4},{1,25},{... | collective-permute-start | bytes 786440 | tf_op jit(solution)/shard_map/ppermute | solution.py:239
  51.7 13.5 %collective-permute-start.14 = (f32[512,128]{1,0:T(8,128)S(1)}, f32[512,128]{1,0:T(8,128)S(1)}, u32[]{:S(2)}, u32[]{:S(2)}) collective-permute-start(f32[512,128]{1,0:T(8,128)S(1)} %copy-done.7), channel_id=1, source_target_pairs={{0,16},{4,20},{8,24},{12,28},{16,0},{20,4},{24,8},{28,12},{1,17},{... | collective-permute-start | bytes 786440 | tf_op jit(solution)/shard_map/ppermute | solution.py:239
  56.7 17.4 %collective-permute-start.10 = (f32[2,512,128]{2,1,0:T(8,128)S(1)}, f32[2,512,128]{2,1,0:T(8,128)S(1)}, u32[]{:S(2)}, u32[]{:S(2)}) collective-permute-start(f32[2,512,128]{2,1,0:T(8,128)S(1)} %get-tuple-element.63), channel_id=1, source_target_pairs={{0,1},{1,0},{2,3},{3,2},{4,5},{5,4},{6,7},{7,6},{8,9},{9,8},{10,11... | collective-permute-start | bytes 1572872 | tf_op jit(solution)/shard_map/ppermute | solution.py:250
  58.4 19.4 %collective-permute-start.17 = (f32[512,128]{1,0:T(8,128)S(1)}, f32[512,128]{1,0:T(8,128)S(1)}, u32[]{:S(2)}, u32[]{:S(2)}) collective-permute-start(f32[512,128]{1,0:T(8,128)S(1)} %copy-done.6), channel_id=1, source_target_pairs={{0,8},{4,12},{8,0},{12,4},{16,24},{20,28},{24,16},{28,20},{1,9},{5... | collective-permute-start | bytes 786440 | tf_op jit(solution)/shard_map/ppermute | solution.py:239
  60.0 17.7 %collective-permute-start.18 = (f32[512,128]{1,0:T(8,128)S(1)}, f32[512,128]{1,0:T(8,128)S(1)}, u32[]{:S(2)}, u32[]{:S(2)}) collective-permute-start(f32[512,128]{1,0:T(8,128)S(1)} %copy-done.5), channel_id=1, source_target_pairs={{0,24},{4,28},{8,16},{12,20},{16,8},{20,12},{24,0},{28,4},{1,25},{... | collective-permute-start | bytes 786440 | tf_op jit(solution)/shard_map/ppermute | solution.py:239
  63.0 14.8 %collective-permute-start.19 = (f32[512,128]{1,0:T(8,128)S(1)}, f32[512,128]{1,0:T(8,128)S(1)}, u32[]{:S(2)}, u32[]{:S(2)}) collective-permute-start(f32[512,128]{1,0:T(8,128)S(1)} %copy-done.4), channel_id=1, source_target_pairs={{0,16},{4,20},{8,24},{12,28},{16,0},{20,4},{24,8},{28,12},{1,17},{... | collective-permute-start | bytes 786440 | tf_op jit(solution)/shard_map/ppermute | solution.py:239
  65.2 12.6 %collective-permute-start.6 = (f32[1,512,128]{2,1,0:T(8,128)S(1)}, f32[1,512,128]{2,1,0:T(8,128)S(1)}, u32[]{:S(2)}, u32[]{:S(2)}) collective-permute-start(f32[1,512,128]{2,1,0:T(8,128)S(1)} %fusion.16), channel_id=1, source_target_pairs={{0,2},{1,3},{2,0},{3,1},{4,6},{5,7},{6,4},{7,5},{8,10},{9,11},{10,... | collective-permute-start | bytes 786440 | tf_op jit(solution)/shard_map/ppermute | solution.py:250
  74.1 23.3 %collective-permute-start.15 = (f32[2,512,128]{2,1,0:T(8,128)S(1)}, f32[2,512,128]{2,1,0:T(8,128)S(1)}, u32[]{:S(2)}, u32[]{:S(2)}) collective-permute-start(f32[2,512,128]{2,1,0:T(8,128)S(1)} %get-tuple-element.74), channel_id=1, source_target_pairs={{0,1},{1,0},{2,3},{3,2},{4,5},{5,4},{6,7},{7,6},{8,9},{9,8},{10,11... | collective-permute-start | bytes 1572872 | tf_op jit(solution)/shard_map/ppermute | solution.py:250
  80.6 25.9 %collective-permute-start.20 = (f32[2,512,128]{2,1,0:T(8,128)S(1)}, f32[2,512,128]{2,1,0:T(8,128)S(1)}, u32[]{:S(2)}, u32[]{:S(2)}) collective-permute-start(f32[2,512,128]{2,1,0:T(8,128)S(1)} %get-tuple-element.85), channel_id=1, source_target_pairs={{0,1},{1,0},{2,3},{3,2},{4,5},{5,4},{6,7},{7,6},{8,9},{9,8},{10,11... | collective-permute-start | bytes 1572872 | tf_op jit(solution)/shard_map/ppermute | solution.py:250
  83.5 23.6 %collective-permute-start.11 = (f32[1,512,128]{2,1,0:T(8,128)S(1)}, f32[1,512,128]{2,1,0:T(8,128)S(1)}, u32[]{:S(2)}, u32[]{:S(2)}) collective-permute-start(f32[1,512,128]{2,1,0:T(8,128)S(1)} %fusion.11), channel_id=1, source_target_pairs={{0,2},{1,3},{2,0},{3,1},{4,6},{5,7},{6,4},{7,5},{8,10},{9,11},{10,... | collective-permute-start | bytes 786440 | tf_op jit(solution)/shard_map/ppermute | solution.py:250
  97.5 24.1 %collective-permute-start.16 = (f32[1,512,128]{2,1,0:T(8,128)S(1)}, f32[1,512,128]{2,1,0:T(8,128)S(1)}, u32[]{:S(2)}, u32[]{:S(2)}) collective-permute-start(f32[1,512,128]{2,1,0:T(8,128)S(1)} %fusion.6), channel_id=1, source_target_pairs={{0,2},{1,3},{2,0},{3,1},{4,6},{5,7},{6,4},{7,5},{8,10},{9,11},{10,... | collective-permute-start | bytes 786440 | tf_op jit(solution)/shard_map/ppermute | solution.py:250
  106.5 18.3 %collective-permute-start.21 = (f32[1,512,128]{2,1,0:T(8,128)S(1)}, f32[1,512,128]{2,1,0:T(8,128)S(1)}, u32[]{:S(2)}, u32[]{:S(2)}) collective-permute-start(f32[1,512,128]{2,1,0:T(8,128)S(1)} %fusion.1), channel_id=1, source_target_pairs={{0,2},{1,3},{2,0},{3,1},{4,6},{5,7},{6,4},{7,5},{8,10},{9,11},{10,... | collective-permute-start | bytes 786440 | tf_op jit(solution)/shard_map/ppermute | solution.py:250

commit v2 on v1

v2 whole, which is shorter than its diff:
```python
import functools

import jax
import jax.numpy as jnp
from jax import lax
from jax.experimental import pallas as pl
from jax.experimental.pallas import tpu as pltpu
from jax.sharding import PartitionSpec as P

REACH = 3
F32 = jnp.float32
WIDTHS = (128, 128, 128, 128)
ORDER = (0, 1, 2, 3)
HOLD = {0: (), 1: (), 2: ((0, 1),), 3: ((0, 1),)}
AFTER = ((), (), (('got', 0),), (('got', 1), ('squared', 0)))


def lasting(us):
    return pl.CostEstimate(flops=int(us * 1e9), bytes_accessed=int(us * 3e6), transcendentals=0)


CHUNKS = 4


def product(points_ref, block):
    return lax.dot_general(points_ref[...], block, (((0,), (0,)), ((), ())), preferred_element_type=F32)


def stream(block_of, live, points_ref, blocks_hbm, slots, done, base, count, emit):
    rows = slots.shape[1] // CHUNKS

    def copies(n):
        return [
            pltpu.make_async_copy(
                blocks_hbm.at[block_of[base + n], pl.ds(c * rows, rows)],
                slots.at[n % 2, pl.ds(c * rows, rows)],
                done.at[n % 2, c],
            )
            for c in range(CHUNKS)
        ]

    def start(n):
        @pl.when(live[base + n] != 0)
        def _():
            for copy in copies(n):
                copy.start()

    start(0)
    for n in range(count):

        @pl.when(live[base + n] != 0)
        def _(n=n):
            for copy in copies(n):
                copy.wait()

        if n + 1 < count:
            start(n + 1)

        @pl.when(live[base + n] != 0)
        def _(n=n):
            emit(n, product(points_ref, slots[n % 2]))

        @pl.when(live[base + n] == 0)
        def _(n=n):
            emit(n, None)


def fetched_kernel(count, block_of, live, points_ref, blocks_hbm, out_ref, slots, done):
    def emit(n, term):
        out_ref[n] = jnp.zeros(out_ref.shape[1:], F32) if term is None else term

    stream(block_of, live, points_ref, blocks_hbm, slots, done, 0, count, emit)


HBM = pl.BlockSpec(memory_space=pltpu.HBM)
SMEM = pl.BlockSpec(memory_space=pltpu.SMEM)
VMEM = pl.BlockSpec(memory_space=pltpu.VMEM)


def slots_for(blocks):
    return [pltpu.VMEM((2, *blocks.shape[1:]), blocks.dtype), pltpu.SemaphoreType.DMA((2, CHUNKS))]


def params(mib):
    return pltpu.CompilerParams(vmem_limit_bytes=mib << 20)


def fetched(points, blocks, block_of, live, count):
    orbs, batch = points.shape
    cells = blocks.shape[2]
    return pl.pallas_call(
        functools.partial(fetched_kernel, count),
        in_specs=[SMEM, SMEM, VMEM, pl.BlockSpec(memory_space=pltpu.HBM)],
        out_specs=VMEM,
        out_shape=jax.ShapeDtypeStruct((count, batch, cells), F32),
        scratch_shapes=slots_for(blocks),
        compiler_params=params(10),
        cost_estimate=lasting(2.5 * count),
        name="fetched",
    )(block_of, live, in_vmem(points), blocks)


def held_kernel(base, block_of, live, points_ref, blocks_hbm, *refs):
    *outs, slots, done = refs

    def emit(n, term):
        outs[n][...] = jnp.zeros(outs[n].shape, F32) if term is None else term

    stream(block_of, live, points_ref, blocks_hbm, slots, done, base, len(outs), emit)


def held(points, blocks, block_of, live, base, count):
    batch, cells = points.shape[1], blocks.shape[2]
    return pl.pallas_call(
        functools.partial(held_kernel, base),
        in_specs=[SMEM, SMEM, VMEM, HBM],
        out_specs=[VMEM] * count,
        out_shape=[jax.ShapeDtypeStruct((batch, cells), F32)] * count,
        scratch_shapes=slots_for(blocks),
        compiler_params=params(10),
        cost_estimate=lasting(2.0 * count),
        name="held",
    )(block_of, live, in_vmem(points), blocks)


def near_kernel(base, widths, block_of, live, points_ref, blocks_hbm, came_ref, *refs):
    *outs, slots, done = refs
    pieces = len(widths)

    def put(n, value):
        start = 0
        for out, width in zip(outs[n * pieces : (n + 1) * pieces], widths):
            out[...] = value[:, start : start + width]
            start += width

    put(2, came_ref[2])

    def emit(n, term):
        put(n, came_ref[n] if term is None else term + came_ref[n])

    stream(block_of, live, points_ref, blocks_hbm, slots, done, base, 2, emit)


def near_sums(points, blocks, block_of, live, base, came, widths):
    batch = points.shape[1]
    return pl.pallas_call(
        functools.partial(near_kernel, base, widths),
        in_specs=[SMEM, SMEM, VMEM, HBM, VMEM],
        scratch_shapes=slots_for(blocks),
        out_specs=[pl.BlockSpec((batch, width), lambda i: (0, 0)) for _ in range(3) for width in widths],
        out_shape=[pltpu.HBM((batch, width), F32) for _ in range(3) for width in widths],
        grid=(1,),
        compiler_params=params(16),
        cost_estimate=lasting(5.0),
        name="near_sums",
    )(block_of, live, in_vmem(points), blocks, in_vmem(came))


def in_vmem(array):
    return pltpu.with_memory_space_constraint(array, pltpu.VMEM)


def picked_kernel(where, order_ref, gram_ref, out_ref):
    del where
    rows = lax.broadcasted_iota(jnp.int32, (gram_ref.shape[1], order_ref.shape[1]), 0)
    chosen = (rows == order_ref[...]).astype(gram_ref.dtype)
    out_ref[...] = jnp.dot(gram_ref[...], chosen, preferred_element_type=F32).astype(out_ref.dtype)


def picked(where, gram, point_order, given):
    batch, points = gram.shape
    rows, span = batch // 2 if given else batch, 256
    per = batch // span

    def turn(i, where):
        return 0, (where[0] ^ (2 * lax.div(i, per) + given)) * per + lax.rem(i, per)

    return pl.pallas_call(
        picked_kernel,
        grid_spec=pltpu.PrefetchScalarGridSpec(
            num_scalar_prefetch=1,
            grid=(points // 2 // span,),
            in_specs=[
                pl.BlockSpec((1, span), turn),
                pl.BlockSpec(
                    (rows, points), lambda i, where: (where[1] if given else 0, 0), pipeline_mode=pl.Buffered(1)
                ),
            ],
            out_specs=pl.BlockSpec((rows, span), lambda i, where: (0, i)),
        ),
        out_shape=jax.ShapeDtypeStruct((rows, points // 2), F32 if given else gram.dtype),
        compiler_params=params(12),
        cost_estimate=lasting(3.0),
        name="picked",
    )(where, point_order[None, :], gram)


def joined_kernel(where, mine_ref, other_ref, out_ref):
    rows = mine_ref.shape[0]

    @pl.when(where[1] == 0)
    def _():
        out_ref[:rows] = mine_ref[...].astype(out_ref.dtype)
        out_ref[rows:] = other_ref[...].astype(out_ref.dtype)

    @pl.when(where[1] != 0)
    def _():
        out_ref[rows:] = mine_ref[...].astype(out_ref.dtype)
        out_ref[:rows] = other_ref[...].astype(out_ref.dtype)


def joined(where, mine, other):
    rows, columns = mine.shape
    return pl.pallas_call(
        joined_kernel,
        in_specs=[SMEM, VMEM, VMEM],
        out_specs=VMEM,
        out_shape=jax.ShapeDtypeStruct((2 * rows, columns), jnp.bfloat16),
        compiler_params=params(8),
        cost_estimate=lasting(1.5),
        name="joined",
    )(where, mine, other)


def squares_kernel(*refs):
    field = refs[0][...]
    for term in refs[1:-1]:
        field = field + term[...]
    refs[-1][...] = (field * field).astype(jnp.bfloat16).astype(F32)


def squares(width, terms):
    batch = terms[0][0].shape[-2]
    in_specs = []
    for array, at in terms:
        lead = (pl.Squeezed(),) * (array.ndim - 2)
        in_specs.append(pl.BlockSpec((*lead, batch, width), lambda i, at=at: at))
    return pl.pallas_call(
        squares_kernel,
        grid=(1,),
        in_specs=in_specs,
        out_specs=pl.BlockSpec((batch, width), lambda i: (0, 0)),
        out_shape=jax.ShapeDtypeStruct((batch, width), F32),
        compiler_params=params(8),
        cost_estimate=lasting(1.5),
        name="squares",
    )(*[array for array, _ in terms])


def shares_kernel(kept_ref, joined_ref, own_ref, came_ref, *outs):
    own, came = own_ref[...].astype(kept_ref.dtype), came_ref[...].astype(kept_ref.dtype)
    batch = own.shape[0]
    for n, out in enumerate(outs):
        cut = slice(n * batch, (n + 1) * batch)
        out[...] = lax.dot_general(
            kept_ref[:, cut], own, (((0,), (0,)), ((), ())), preferred_element_type=F32
        ) + lax.dot_general(joined_ref[:, cut], came, (((0,), (0,)), ((), ())), preferred_element_type=F32)


def shares(kept, joined, own, came):
    batch, width = own.shape
    count = kept.shape[1] // batch
    return pl.pallas_call(
        shares_kernel,
        in_specs=[VMEM] * 4,
        out_specs=[VMEM] * count,
        out_shape=[jax.ShapeDtypeStruct((batch, width), F32)] * count,
        compiler_params=params(8),
        cost_estimate=lasting(2.0),
        name="shares",
    )(kept, joined, own, came)


def swapped(block, mask, count):
    return lax.ppermute(block, "grid", [(i, i ^ mask) for i in range(count)])


def passed_along(block, distance, count):
    return lax.ppermute(block, "grid", [((i - distance) % count, i) for i in range(count)])


def turned(block, distance, count):
    return lax.ppermute(block, "pts", [(i, i ^ distance) for i in range(count)])


def combined(share, batches):
    kept, links = list(share), []
    distance = 2
    while distance < batches:
        sent, kept = kept[1::2], kept[0::2]
        came = turned(jnp.stack(sent) if len(sent) > 1 else sent[0][None], distance, batches)
        links.append(came)
        kept = [block + came[n] for n, block in enumerate(kept)]
        distance *= 2
    return kept[0].astype(jnp.bfloat16), links


def after(value, *others):
    return lax.optimization_barrier((value, *others))[0]


def on_device(phi_blocks, phi_points, tile_mask, support, point_order, gram_inverse):
    slabs, batches = lax.axis_size("grid"), lax.axis_size("pts")
    own_slab, own_batch = lax.axis_index("grid"), lax.axis_index("pts")
    blocks = pltpu.with_memory_space_constraint(phi_blocks[0], pltpu.HBM)
    cube = slabs == 8
    if cube:
        targets = own_slab ^ jnp.array([3, 7, 5, 0, 1, 2, 6, 0] + [0] * 8, jnp.int32)
    else:
        targets = (own_slab + jnp.array([d % slabs for d in range(-REACH, REACH + 1)] + [0] * 9, jnp.int32)) % slabs
    match = targets[:, None] == support[0][None, :]
    block_of = jnp.sum(jnp.where(match, jnp.arange(support.shape[1], dtype=jnp.int32)[None, :], 0), axis=1)
    live = jnp.sum(jnp.where(match, tile_mask[0, :, 0][None, :], 0), axis=1)
    where = jnp.stack([own_batch, own_slab & 1]).astype(jnp.int32)
    cells = phi_blocks.shape[-1]
    points = phi_points[0]
    if cube:
        away = fetched(points, blocks, block_of, live, 3)
        came = swapped(away, 1, slabs)
        own, other = held(after(points, away), blocks, block_of, live, 3, 2)
        theirs = turned(picked(where, after(gram_inverse, own), point_order, 1), 1, batches)
        near = near_sums(after(points, own), blocks, block_of, live, 5, came, WIDTHS)
        pieces, links, gots, squared = {}, {}, {}, {}
        columns = None
        for n in ORDER:
            width = WIDTHS[n]
            at = sum(WIDTHS[:n]) // width
            sums = [near[place * len(WIDTHS) + n] for place in range(3)]
            if n == ORDER[1]:
                sums = after(sums, late)
            if AFTER[n]:
                sums = after(sums, [{"got": gots, "squared": squared, "sum": links}[kind][p] for kind, p in AFTER[n]])
            got = gots[n] = [swapped(block, mask, slabs) for block, mask in zip(sums, (2, 6, 4))]
            if columns is None:
                late = swapped(after(other, near), 1, slabs)
                theirs = after(theirs, got)
                columns = joined(where, theirs, swapped(theirs, 1, slabs))
            terms = [(own, (0, at)), (late, (0, at))] + [(block, (0, 0)) for block in got]
            mine = squares(width, terms)
            squared[n] = turned(mine, 1, batches)
            if n == ORDER[0]:
                kept = picked(where, after(gram_inverse, near), point_order, 0)
            pending = [links[p][0] if step else squared[p] for p, step in HOLD[n]]
            if pending:
                kept = after(kept, pending)
            share = shares(kept, columns, mine, squared[n])
            kept = after(kept, share[0])
            pieces[n], links[n] = combined(share, batches)
        fitted = [pieces[n] for n in range(len(WIDTHS))]
    else:
        tiles = fetched(points, blocks, block_of, live, 2 * REACH + 1)
        kept = picked(where, gram_inverse, point_order, 0)
        theirs = turned(picked(where, gram_inverse, point_order, 1), 1, batches)
        columns = joined(where, theirs, swapped(theirs, 1, slabs))
        terms = [(tiles, (REACH, 0, 0))] + [
            (passed_along(tiles[REACH + d], d, slabs), (0, 0)) for d in range(-REACH, REACH + 1) if d != 0
        ]
        mine = squares(cells, terms)
        fitted = [combined(shares(kept, columns, mine, turned(mine, 1, batches)), batches)[0]]
    return jnp.concatenate(fitted, axis=1)


def solution(mesh):
    in_specs = (
        P("grid", None, None, None),
        P("grid", None, "pts"),
        P("grid", None, "pts"),
        P("grid", None),
        P(),
        P("pts", None),
    )
    out_specs = P("pts", "grid")
    return jax.shard_map(
        on_device, mesh=mesh, in_specs=in_specs, out_specs=out_specs, check_vma=False
    )
```

time: 126 us -> 121 us (0.960)
  starting transfers between devices: 36.6 us -> 26.3 us
  Pallas kernels: 30.1 us -> 34.8 us
    ppermute x14 -> x15, waiting for transfers between devices: 9.44 us -> 19.2 us  [swapped(): return lax.ppermute(block, 'grid', [(i, i ^ mask) for i in range(count)])]
    ppermute x14 -> x15, starting transfers between devices: 25.6 us -> 16.3 us  [swapped(): return lax.ppermute(block, 'grid', [(i, i ^ mask) for i in range(count)])]
    ppermute x8 -> x9, waiting for transfers between devices: 44.7 us -> 35.7 us  [turned(): return lax.ppermute(block, 'pts', [(i, i ^ distance) for i in range(count)])]
    pallas_call x5 -> x11, Pallas kernels: 17.3 us -> 10.4 us  [the longest x2 5.96 us: picked(): pl.pallas_call(picked_kernel, grid_spec=pltpu.PrefetchScalarGridSpec(num_...]
    pallas_call x1, Pallas kernels: 2.62 us -> 9.44 us  [near_sums(): pl.pallas_call(functools.partial(near_kernel, base, widths), in_specs=[SM...]
    pallas_call x1, Pallas kernels: 4.78 us -> 8.45 us  [fetched(): pl.pallas_call(functools.partial(fetched_kernel, count), in_specs=[SMEM,...]
    ppermute x8 -> x9, starting transfers between devices: 11 us -> 10 us  [turned(): return lax.ppermute(block, 'pts', [(i, i ^ distance) for i in range(count)])]
  transfers between devices with their start and end apart: 22 -> 24, of which waited for: 12 -> 11; matrix products, arithmetic and copies ran while one was open for 0% -> 0% of each run, Pallas kernels for 18% -> 22%
where the time goes in v2:
time: 121 us
  waiting for transfers between devices  54.9 us (45%)
  Pallas kernels  34.8 us (29%)
  starting transfers between devices  26.3 us (22%)
  other arithmetic  2.49 us (2%)
  local copies, waits for them, and re-layouts  1.96 us (2%)
    ppermute x9, waiting for transfers between devices, turned(): return lax.ppermute(block, 'pts', [(i, i ^ distance) for i in range(count)])  35.7 us
    ppermute x15, waiting for transfers between devices, swapped(): return lax.ppermute(block, 'grid', [(i, i ^ mask) for i in range(count)])  19.2 us
    ppermute x15, starting transfers between devices, swapped(): return lax.ppermute(block, 'grid', [(i, i ^ mask) for i in range(count)])  16.3 us
    ppermute x9, starting transfers between devices, turned(): return lax.ppermute(block, 'pts', [(i, i ^ distance) for i in range(count)])  10 us
    pallas_call x1, Pallas kernels, near_sums(): pl.pallas_call(functools.partial(near_kernel, base, widths), in_specs=[SM...  9.44 us
    pallas_call x1, Pallas kernels, fetched(): pl.pallas_call(functools.partial(fetched_kernel, count), in_specs=[SMEM,...  8.45 us
    pallas_call x1, Pallas kernels, held(): pl.pallas_call(functools.partial(held_kernel, base), in_specs=[SMEM, SMEM...  6.51 us
    pallas_call x2, Pallas kernels, picked(): pl.pallas_call(picked_kernel, grid_spec=pltpu.PrefetchScalarGridSpec(num_...  5.96 us
  transfers between devices with their start and end apart: 24, of which 11 were waited for; matrix products, arithmetic and copies ran while one was open for 0% of the time, Pallas kernels for 22%

profile of v2, /device:TPU:0, one launch (start us, length us, event | category | flops | bytes accessed | tf_op | source)
XLA Modules:
  0.0 120.7 jit_solution(12736135864992607545)
XLA Ops:
  0.0 0.7 broadcast_xor_fusion
  0.7 0.8 fusion.5
  1.4 0.0 copy-start
  1.4 1.9 %copy-done = bf16[1,3200,512]{2,1,0:T(8,128)(2,1)S(1)} copy-done((bf16[1,3200,512]{2,1,0:T(8,128)(2,1)S(1)}, bf16[1,3200,512]{2,1,0:T(8,128)(2,1)}, u32[]{:S(2)}) %copy-start) | copy-done | bytes 3276824
  3.3 8.4 %fetched.1 = f32[3,512,512]{2,1,0:T(8,128)} custom-call(s32[16]{0:T(128)S(1)} %get-tuple-element.90.block_of, s32[16]{0:T(128)S(1)} %get-tuple-element.89.live, bf16[3200,512]{1,0:T(8,128)(2,1)S(1)} %bitcast.27, bf16[6,3200,512]{2,1,0:T(8,128)(2,1)} %bitcast.36), custom_call_target="tpu_custom_call" | custom-call | flops 7500000256 | bytes 22500000 | tf_op jit(solution)/shard_map/fetched/pallas_call | solution.py:91
  11.8 2.4 %collective-permute-start = (f32[3,512,512]{2,1,0:T(8,128)}, f32[3,512,512]{2,1,0:T(8,128)}, u32[]{:S(2)}, u32[]{:S(2)}) collective-permute-start(f32[3,512,512]{2,1,0:T(8,128)} %fetched.1), channel_id=1, source_target_pairs={{0,4},{4,0},{8,12},{12,8},{16,20},{20,16},{24,28},{28,24},{1,5},{5... | collective-permute-start | bytes 9437192 | tf_op jit(solution)/shard_map/ppermute | solution.py:275
  14.2 6.5 %held.1 = (f32[512,512]{1,0:T(8,128)S(1)}, f32[512,512]{1,0:T(8,128)S(1)}) custom-call(s32[16]{0:T(128)S(1)} %get-tuple-element.90.block_of, s32[16]{0:T(128)S(1)} %get-tuple-element.89.live, bf16[3200,512]{1,0:T(8,128)(2,1)S(1)} %bitcast.28, bf16[6,3200,512]{2,1,0:T(8,128)(2,1)} %bitcast.37), custom_call_target="tpu_custom_call" | custom-call | flops 4000000000 | bytes 12000000 | tf_op jit(solution)/shard_map/held/pallas_call | solution.py:114
  20.7 0.1 pad_add_fusion.where
  20.8 2.4 %picked.3 = f32[256,1024]{1,0:T(8,128)S(1)} custom-call(s32[2]{0:T(128)S(1)} %pad_add_fusion.where, s32[1,2048]{1,0:T(1,128)S(1)} %bitcast.34, bf16[512,2048]{1,0:T(8,128)(2,1)S(1)} %copy-done.2), custom_call_target="tpu_custom_call" | custom-call | flops 3000000000 | bytes 9000000 | tf_op jit(solution)/shard_map/picked/pallas_call | solution.py:178
  23.2 0.1 collective-permute-start.1
  23.3 0.0 collective-permute-done.came_ref
  23.3 9.4 %near_sums.1 = (f32[512,128]{1,0:T(8,128)}, f32[512,128]{1,0:T(8,128)}, f32[512,128]{1,0:T(8,128)}, f32[512,128]{1,0:T(8,128)}, f32[512,128]{1,0:T(8,128)}, /*in...) custom-call(s32[16]{0:T(128)S(1)} %get-tuple-element.90.block_of, ...), custom_call_target="tpu_custom_call" | custom-call | flops 5000000000 | bytes 15000000 | tf_op jit(solution)/shard_map/near_sums/pallas_call | solution.py:146
  32.8 0.1 collective-permute-start.6
  32.8 0.5 collective-permute-start.2
  33.3 3.0 %collective-permute-start.3 = (f32[512,128]{1,0:T(8,128)}, f32[512,128]{1,0:T(8,128)S(1)}, u32[]{:S(2)}, u32[]{:S(2)}) collective-permute-start(f32[512,128]{1,0:T(8,128)} %get-tuple-element.54), channel_id=1, source_target_pairs={{0,24},{4,28},{8,16},{12,20},{16,8},{20,12},{24,0},{28,4},{1,25},{... | collective-permute-start | bytes 786440 | tf_op jit(solution)/shard_map/ppermute | solution.py:275
  36.3 0.1 collective-permute-start.4
  36.4 12.7 %collective-permute-done.1.mine_ref = f32[256,1024]{1,0:T(8,128)S(1)} collective-permute-done((f32[256,1024]{1,0:T(8,128)S(1)}, f32[256,1024]{1,0:T(8,128)S(1)}, u32[]{:S(2)}, u32[]{:S(2)}) %collective-permute-start.1) | collective-permute-done | bytes 1048608 | tf_op jit(solution)/shard_map/ppermute | solution.py:283
  49.0 0.0 collective-permute-done.2.refs_2_
  49.0 0.0 collective-permute-done.3.refs_3_
  49.0 1.2 collective-permute-done.4.refs_4_
  50.2 0.0 collective-permute-start.5
  50.2 0.3 collective-permute-start.9
  50.5 1.5 %collective-permute-start.10 = (f32[512,128]{1,0:T(8,128)}, f32[512,128]{1,0:T(8,128)S(1)}, u32[]{:S(2)}, u32[]{:S(2)}) collective-permute-start(f32[512,128]{1,0:T(8,128)} %get-tuple-element.71), channel_id=1, source_target_pairs={{0,24},{4,28},{8,16},{12,20},{16,8},{20,12},{24,0},{28,4},{1,25},{... | collective-permute-start | bytes 786440 | tf_op jit(solution)/shard_map/ppermute | solution.py:275
  52.0 1.7 %collective-permute-start.11 = (f32[512,128]{1,0:T(8,128)}, f32[512,128]{1,0:T(8,128)S(1)}, u32[]{:S(2)}, u32[]{:S(2)}) collective-permute-start(f32[512,128]{1,0:T(8,128)} %get-tuple-element.72), channel_id=1, source_target_pairs={{0,16},{4,20},{8,24},{12,28},{16,0},{20,4},{24,8},{28,12},{1,17},{... | collective-permute-start | bytes 786440 | tf_op jit(solution)/shard_map/ppermute | solution.py:275
  53.7 0.1 squares.4.own_ref
  53.9 0.1 collective-permute-start.7
  54.0 3.5 %picked.2.kept_ref = bf16[512,1024]{1,0:T(8,128)(2,1)S(1)} custom-call(s32[2]{0:T(128)S(1)} %pad_add_fusion.where, s32[1,2048]{1,0:T(1,128)S(1)} %bitcast.35, bf16[512,2048]{1,0:T(8,128)(2,1)S(1)} %copy-done.2), custom_call_target="tpu_custom_call" | custom-call | flops 3000000000 | bytes 9000000 | tf_op jit(solution)/shard_map/picked/pallas_call | solution.py:178
  57.5 2.0 %collective-permute-done.9.refs_2_ = f32[512,128]{1,0:T(8,128)S(1)} collective-permute-done((f32[512,128]{1,0:T(8,128)}, f32[512,128]{1,0:T(8,128)S(1)}, u32[]{:S(2)}, u32[]{:S(2)}) %collective-permute-start.9) | collective-permute-done | bytes 262176 | tf_op jit(solution)/shard_map/ppermute | solution.py:275
  59.6 0.3 collective-permute-start.14
  59.8 5.1 %collective-permute-done.10.refs_3_ = f32[512,128]{1,0:T(8,128)S(1)} collective-permute-done((f32[512,128]{1,0:T(8,128)}, f32[512,128]{1,0:T(8,128)S(1)}, u32[]{:S(2)}, u32[]{:S(2)}) %collective-permute-start.10) | collective-permute-done | bytes 262176 | tf_op jit(solution)/shard_map/ppermute | solution.py:275
  64.9 1.4 %collective-permute-start.15 = (f32[512,128]{1,0:T(8,128)S(1)}, f32[512,128]{1,0:T(8,128)S(1)}, u32[]{:S(2)}, u32[]{:S(2)}) collective-permute-start(f32[512,128]{1,0:T(8,128)S(1)} %copy-done.8), channel_id=1, source_target_pairs={{0,24},{4,28},{8,16},{12,20},{16,8},{20,12},{24,0},{28,4},{1,25},{... | collective-permute-start | bytes 786440 | tf_op jit(solution)/shard_map/ppermute | solution.py:275
  66.4 1.3 %collective-permute-start.16 = (f32[512,128]{1,0:T(8,128)S(1)}, f32[512,128]{1,0:T(8,128)S(1)}, u32[]{:S(2)}, u32[]{:S(2)}) collective-permute-start(f32[512,128]{1,0:T(8,128)S(1)} %copy-done.7), channel_id=1, source_target_pairs={{0,16},{4,20},{8,24},{12,28},{16,0},{20,4},{24,8},{28,12},{1,17},{... | collective-permute-start | bytes 786440 | tf_op jit(solution)/shard_map/ppermute | solution.py:275
  67.7 0.1 squares.5.own_ref
  67.8 0.8 collective-permute-start.12
  68.6 0.8 joined.1.joined_ref
  69.5 0.8 shares.4
  70.3 2.4 %collective-permute-start.8 = (f32[1,512,128]{2,1,0:T(8,128)S(1)}, f32[1,512,128]{2,1,0:T(8,128)S(1)}, u32[]{:S(2)}, u32[]{:S(2)}) collective-permute-start(f32[1,512,128]{2,1,0:T(8,128)S(1)} %bitcast.31), channel_id=1, source_target_pairs={{0,2},{1,3},{2,0},{3,1},{4,6},{5,7},{6,4},{7,5},{8,10},{9,11},{10,... | collective-permute-start | bytes 786440 | tf_op jit(solution)/shard_map/ppermute | solution.py:283
  72.7 0.0 collective-permute-done.14.refs_2_
  72.7 1.0 collective-permute-start.19
  73.7 2.5 %collective-permute-done.15.refs_3_ = f32[512,128]{1,0:T(8,128)S(1)} collective-permute-done((f32[512,128]{1,0:T(8,128)S(1)}, f32[512,128]{1,0:T(8,128)S(1)}, u32[]{:S(2)}, u32[]{:S(2)}) %collective-permute-start.15) | collective-permute-done | bytes 262176 | tf_op jit(solution)/shard_map/ppermute | solution.py:275
  76.2 1.4 %collective-permute-start.20 = (f32[512,128]{1,0:T(8,128)S(1)}, f32[512,128]{1,0:T(8,128)S(1)}, u32[]{:S(2)}, u32[]{:S(2)}) collective-permute-start(f32[512,128]{1,0:T(8,128)S(1)} %copy-done.5), channel_id=1, source_target_pairs={{0,24},{4,28},{8,16},{12,20},{16,8},{20,12},{24,0},{28,4},{1,25},{... | collective-permute-start | bytes 786440 | tf_op jit(solution)/shard_map/ppermute | solution.py:275
  77.7 1.6 %collective-permute-done.16.refs_4_ = f32[512,128]{1,0:T(8,128)S(1)} collective-permute-done((f32[512,128]{1,0:T(8,128)S(1)}, f32[512,128]{1,0:T(8,128)S(1)}, u32[]{:S(2)}, u32[]{:S(2)}) %collective-permute-start.16) | collective-permute-done | bytes 262176 | tf_op jit(solution)/shard_map/ppermute | solution.py:275
  79.3 1.3 %collective-permute-start.21 = (f32[512,128]{1,0:T(8,128)S(1)}, f32[512,128]{1,0:T(8,128)S(1)}, u32[]{:S(2)}, u32[]{:S(2)}) collective-permute-start(f32[512,128]{1,0:T(8,128)S(1)} %copy-done.4), channel_id=1, source_target_pairs={{0,16},{4,20},{8,24},{12,28},{16,0},{20,4},{24,8},{28,12},{1,17},{... | collective-permute-start | bytes 786440 | tf_op jit(solution)/shard_map/ppermute | solution.py:275
  80.6 0.1 squares.6.own_ref
  80.8 0.0 collective-permute-done.12.came_ref
  80.8 2.2 %collective-permute-start.17 = (f32[512,128]{1,0:T(8,128)S(1)}, f32[512,128]{1,0:T(8,128)S(1)}, u32[]{:S(2)}, u32[]{:S(2)}) collective-permute-start(f32[512,128]{1,0:T(8,128)S(1)} %squares.6.own_ref), channel_id=1, source_target_pairs={{0,1},{1,0},{2,3},{3,2},{4,5},{5,4},{6,7},{7,6},{8,9},{9,8},{10,11... | collective-permute-start | bytes 786440 | tf_op jit(solution)/shard_map/ppermute | solution.py:283
  82.9 0.8 shares.5
  83.7 0.0 collective-permute-done.8
  83.7 1.0 collective-permute-start.13
  84.7 0.0 collective-permute-done.19.refs_2_
  84.7 2.4 %collective-permute-done.20.refs_3_ = f32[512,128]{1,0:T(8,128)S(1)} collective-permute-done((f32[512,128]{1,0:T(8,128)S(1)}, f32[512,128]{1,0:T(8,128)S(1)}, u32[]{:S(2)}, u32[]{:S(2)}) %collective-permute-start.20) | collective-permute-done | bytes 262176 | tf_op jit(solution)/shard_map/ppermute | solution.py:275
  87.2 4.2 %collective-permute-done.21.refs_4_ = f32[512,128]{1,0:T(8,128)S(1)} collective-permute-done((f32[512,128]{1,0:T(8,128)S(1)}, f32[512,128]{1,0:T(8,128)S(1)}, u32[]{:S(2)}, u32[]{:S(2)}) %collective-permute-start.21) | collective-permute-done | bytes 262176 | tf_op jit(solution)/shard_map/ppermute | solution.py:275
  91.4 0.1 squares.7.own_ref
  91.5 0.3 collective-permute-start.22
  91.8 0.6 collective-permute-done.17.came_ref
  92.4 0.8 shares.6
  93.2 3.2 %collective-permute-start.18 = (f32[1,512,128]{2,1,0:T(8,128)S(1)}, f32[1,512,128]{2,1,0:T(8,128)S(1)}, u32[]{:S(2)}, u32[]{:S(2)}) collective-permute-start(f32[1,512,128]{2,1,0:T(8,128)S(1)} %bitcast.32), channel_id=1, source_target_pairs={{0,2},{1,3},{2,0},{3,1},{4,6},{5,7},{6,4},{7,5},{8,10},{9,11},{10,... | collective-permute-start | bytes 786440 | tf_op jit(solution)/shard_map/ppermute | solution.py:283
  96.5 8.3 %collective-permute-done.22.came_ref = f32[512,128]{1,0:T(8,128)S(1)} collective-permute-done((f32[512,128]{1,0:T(8,128)S(1)}, f32[512,128]{1,0:T(8,128)S(1)}, u32[]{:S(2)}, u32[]{:S(2)}) %collective-permute-start.22) | collective-permute-done | bytes 262176 | tf_op jit(solution)/shard_map/ppermute | solution.py:283
  104.8 0.8 shares.7
  105.6 0.1 collective-permute-start.23
  105.7 0.0 collective-permute-done.13
  105.7 0.0 collective-permute-done.18
  105.8 14.0 %collective-permute-done.23 = f32[1,512,128]{2,1,0:T(8,128)S(1)} collective-permute-done((f32[1,512,128]{2,1,0:T(8,128)S(1)}, f32[1,512,128]{2,1,0:T(8,128)S(1)}, u32[]{:S(2)}, u32[]{:S(2)}) %collective-permute-start.23) | collective-permute-done | bytes 262176 | tf_op jit(solution)/shard_map/ppermute | solution.py:283
  119.8 0.9 pad_maximum_fusion
  (26 shorter events, 0.2 us)
Async XLA Ops:
  1.4 1.9 %copy-start = (bf16[1,3200,512]{2,1,0:T(8,128)(2,1)S(1)}, bf16[1,3200,512]{2,1,0:T(8,128)(2,1)}, u32[]{:S(2)}) copy-start(bf16[1,3200,512]{2,1,0:T(8,128)(2,1)} %param.8) | copy-start | bytes 9830404
  3.3 10.8 %copy-start.1 = (bf16[1,3200,512]{2,1,0:T(8,128)(2,1)S(1)}, bf16[1,3200,512]{2,1,0:T(8,128)(2,1)}, u32[]{:S(2)}) copy-start(bf16[1,3200,512]{2,1,0:T(8,128)(2,1)} %param.8) | copy-start | bytes 9830404
  11.8 11.5 %collective-permute-start = (f32[3,512,512]{2,1,0:T(8,128)}, f32[3,512,512]{2,1,0:T(8,128)}, u32[]{:S(2)}, u32[]{:S(2)}) collective-permute-start(f32[3,512,512]{2,1,0:T(8,128)} %fetched.1), channel_id=1, source_target_pairs={{0,4},{4,0},{8,12},{12,8},{16,20},{20,16},{24,28},{28,24},{1,5},{5... | collective-permute-start | bytes 9437192 | tf_op jit(solution)/shard_map/ppermute | solution.py:275
  14.2 6.6 %copy-start.2 = (bf16[512,2048]{1,0:T(8,128)(2,1)S(1)}, bf16[512,2048]{1,0:T(8,128)(2,1)}, u32[]{:S(2)}) copy-start(bf16[512,2048]{1,0:T(8,128)(2,1)} %gram_ref.1) | copy-start | bytes 6291460
  14.2 6.6 %copy-start.3 = (s32[2048]{0:T(1024)S(1)}, s32[2048]{0:T(1024)}, u32[]{:S(2)}) copy-start(s32[2048]{0:T(1024)} %param.11) | copy-start | bytes 24580
  23.2 25.8 %collective-permute-start.1 = (f32[256,1024]{1,0:T(8,128)S(1)}, f32[256,1024]{1,0:T(8,128)S(1)}, u32[]{:S(2)}, u32[]{:S(2)}) collective-permute-start(f32[256,1024]{1,0:T(8,128)S(1)} %picked.3), channel_id=1, source_target_pairs={{0,1},{1,0},{2,3},{3,2},{4,5},{5,4},{6,7},{7,6},{8,9},{9,8},{10,11... | collective-permute-start | bytes 3145736 | tf_op jit(solution)/shard_map/ppermute | solution.py:283
  32.8 17.5 %collective-permute-start.6 = (f32[512,512]{1,0:T(8,128)S(1)}, f32[512,512]{1,0:T(8,128)S(1)}, u32[]{:S(2)}, u32[]{:S(2)}) collective-permute-start(f32[512,512]{1,0:T(8,128)S(1)} %get-tuple-element.66), channel_id=1, source_target_pairs={{0,4},{4,0},{8,12},{12,8},{16,20},{20,16},{24,28},{28,24},{1,5},{5... | collective-permute-start | bytes 3145736 | tf_op jit(solution)/shard_map/ppermute | solution.py:275
  32.8 16.2 %collective-permute-start.2 = (f32[512,128]{1,0:T(8,128)}, f32[512,128]{1,0:T(8,128)S(1)}, u32[]{:S(2)}, u32[]{:S(2)}) collective-permute-start(f32[512,128]{1,0:T(8,128)} %get-tuple-element.50), channel_id=1, source_target_pairs={{0,8},{4,12},{8,0},{12,4},{16,24},{20,28},{24,16},{28,20},{1,9},{5... | collective-permute-start | bytes 786440 | tf_op jit(solution)/shard_map/ppermute | solution.py:275
  33.3 15.7 %collective-permute-start.3 = (f32[512,128]{1,0:T(8,128)}, f32[512,128]{1,0:T(8,128)S(1)}, u32[]{:S(2)}, u32[]{:S(2)}) collective-permute-start(f32[512,128]{1,0:T(8,128)} %get-tuple-element.54), channel_id=1, source_target_pairs={{0,24},{4,28},{8,16},{12,20},{16,8},{20,12},{24,0},{28,4},{1,25},{... | collective-permute-start | bytes 786440 | tf_op jit(solution)/shard_map/ppermute | solution.py:275
  36.3 13.9 %collective-permute-start.4 = (f32[512,128]{1,0:T(8,128)}, f32[512,128]{1,0:T(8,128)S(1)}, u32[]{:S(2)}, u32[]{:S(2)}) collective-permute-start(f32[512,128]{1,0:T(8,128)} %get-tuple-element.58), channel_id=1, source_target_pairs={{0,16},{4,20},{8,24},{12,28},{16,0},{20,4},{24,8},{28,12},{1,17},{... | collective-permute-start | bytes 786440 | tf_op jit(solution)/shard_map/ppermute | solution.py:275
  50.2 18.4 %collective-permute-start.5 = (f32[256,1024]{1,0:T(8,128)S(1)}, f32[256,1024]{1,0:T(8,128)S(1)}, u32[]{:S(2)}, u32[]{:S(2)}) collective-permute-start(f32[256,1024]{1,0:T(8,128)S(1)} %collective-permute-done.1.mine_ref), channel_id=1, source_target_pairs={{0,4},{4,0},{8,12},{12,8},{16,20},{20,16},{24,28},{28,24},{1,5},{5... | collective-permute-start | bytes 3145736 | tf_op jit(solution)/shard_map/ppermute | solution.py:275
  50.2 9.3 %collective-permute-start.9 = (f32[512,128]{1,0:T(8,128)}, f32[512,128]{1,0:T(8,128)S(1)}, u32[]{:S(2)}, u32[]{:S(2)}) collective-permute-start(f32[512,128]{1,0:T(8,128)} %get-tuple-element.70), channel_id=1, source_target_pairs={{0,8},{4,12},{8,0},{12,4},{16,24},{20,28},{24,16},{28,20},{1,9},{5... | collective-permute-start | bytes 786440 | tf_op jit(solution)/shard_map/ppermute | solution.py:275
  50.5 14.4 %collective-permute-start.10 = (f32[512,128]{1,0:T(8,128)}, f32[512,128]{1,0:T(8,128)S(1)}, u32[]{:S(2)}, u32[]{:S(2)}) collective-permute-start(f32[512,128]{1,0:T(8,128)} %get-tuple-element.71), channel_id=1, source_target_pairs={{0,24},{4,28},{8,16},{12,20},{16,8},{20,12},{24,0},{28,4},{1,25},{... | collective-permute-start | bytes 786440 | tf_op jit(solution)/shard_map/ppermute | solution.py:275
  52.0 14.4 %collective-permute-start.11 = (f32[512,128]{1,0:T(8,128)}, f32[512,128]{1,0:T(8,128)S(1)}, u32[]{:S(2)}, u32[]{:S(2)}) collective-permute-start(f32[512,128]{1,0:T(8,128)} %get-tuple-element.72), channel_id=1, source_target_pairs={{0,16},{4,20},{8,24},{12,28},{16,0},{20,4},{24,8},{28,12},{1,17},{... | collective-permute-start | bytes 786440 | tf_op jit(solution)/shard_map/ppermute | solution.py:275
  53.8 5.7 %copy-start.9 = (f32[512,128]{1,0:T(8,128)S(1)}, f32[512,128]{1,0:T(8,128)}, u32[]{:S(2)}) copy-start(f32[512,128]{1,0:T(8,128)} %get-tuple-element.77) | copy-start | bytes 786436
  53.9 11.1 %copy-start.8 = (f32[512,128]{1,0:T(8,128)S(1)}, f32[512,128]{1,0:T(8,128)}, u32[]{:S(2)}) copy-start(f32[512,128]{1,0:T(8,128)} %get-tuple-element.78) | copy-start | bytes 786436
  53.9 12.5 %copy-start.7 = (f32[512,128]{1,0:T(8,128)S(1)}, f32[512,128]{1,0:T(8,128)}, u32[]{:S(2)}) copy-start(f32[512,128]{1,0:T(8,128)} %get-tuple-element.79) | copy-start | bytes 786436
  53.9 14.0 %collective-permute-start.7 = (f32[512,128]{1,0:T(8,128)S(1)}, f32[512,128]{1,0:T(8,128)S(1)}, u32[]{:S(2)}, u32[]{:S(2)}) collective-permute-start(f32[512,128]{1,0:T(8,128)S(1)} %squares.4.own_ref), channel_id=1, source_target_pairs={{0,1},{1,0},{2,3},{3,2},{4,5},{5,4},{6,7},{7,6},{8,9},{9,8},{10,11... | collective-permute-start | bytes 786440 | tf_op jit(solution)/shard_map/ppermute | solution.py:283
  59.6 13.1 %collective-permute-start.14 = (f32[512,128]{1,0:T(8,128)S(1)}, f32[512,128]{1,0:T(8,128)S(1)}, u32[]{:S(2)}, u32[]{:S(2)}) collective-permute-start(f32[512,128]{1,0:T(8,128)S(1)} %copy-done.9), channel_id=1, source_target_pairs={{0,8},{4,12},{8,0},{12,4},{16,24},{20,28},{24,16},{28,20},{1,9},{5... | collective-permute-start | bytes 786440 | tf_op jit(solution)/shard_map/ppermute | solution.py:275
  64.9 11.3 %collective-permute-start.15 = (f32[512,128]{1,0:T(8,128)S(1)}, f32[512,128]{1,0:T(8,128)S(1)}, u32[]{:S(2)}, u32[]{:S(2)}) collective-permute-start(f32[512,128]{1,0:T(8,128)S(1)} %copy-done.8), channel_id=1, source_target_pairs={{0,24},{4,28},{8,16},{12,20},{16,8},{20,12},{24,0},{28,4},{1,25},{... | collective-permute-start | bytes 786440 | tf_op jit(solution)/shard_map/ppermute | solution.py:275
  66.4 12.9 %collective-permute-start.16 = (f32[512,128]{1,0:T(8,128)S(1)}, f32[512,128]{1,0:T(8,128)S(1)}, u32[]{:S(2)}, u32[]{:S(2)}) collective-permute-start(f32[512,128]{1,0:T(8,128)S(1)} %copy-done.7), channel_id=1, source_target_pairs={{0,16},{4,20},{8,24},{12,28},{16,0},{20,4},{24,8},{28,12},{1,17},{... | collective-permute-start | bytes 786440 | tf_op jit(solution)/shard_map/ppermute | solution.py:275
  67.8 12.9 %collective-permute-start.12 = (f32[512,128]{1,0:T(8,128)S(1)}, f32[512,128]{1,0:T(8,128)S(1)}, u32[]{:S(2)}, u32[]{:S(2)}) collective-permute-start(f32[512,128]{1,0:T(8,128)S(1)} %squares.5.own_ref), channel_id=1, source_target_pairs={{0,1},{1,0},{2,3},{3,2},{4,5},{5,4},{6,7},{7,6},{8,9},{9,8},{10,11... | collective-permute-start | bytes 786440 | tf_op jit(solution)/shard_map/ppermute | solution.py:283
  69.5 3.2 %copy-start.6 = (f32[512,128]{1,0:T(8,128)S(1)}, f32[512,128]{1,0:T(8,128)}, u32[]{:S(2)}) copy-start(f32[512,128]{1,0:T(8,128)} %get-tuple-element.84) | copy-start | bytes 786436
  69.5 6.8 %copy-start.5 = (f32[512,128]{1,0:T(8,128)S(1)}, f32[512,128]{1,0:T(8,128)}, u32[]{:S(2)}) copy-start(f32[512,128]{1,0:T(8,128)} %get-tuple-element.85) | copy-start | bytes 786436
  69.5 9.8 %copy-start.4 = (f32[512,128]{1,0:T(8,128)S(1)}, f32[512,128]{1,0:T(8,128)}, u32[]{:S(2)}) copy-start(f32[512,128]{1,0:T(8,128)} %get-tuple-element.86) | copy-start | bytes 786436
  70.3 13.4 %collective-permute-start.8 = (f32[1,512,128]{2,1,0:T(8,128)S(1)}, f32[1,512,128]{2,1,0:T(8,128)S(1)}, u32[]{:S(2)}, u32[]{:S(2)}) collective-permute-start(f32[1,512,128]{2,1,0:T(8,128)S(1)} %bitcast.31), channel_id=1, source_target_pairs={{0,2},{1,3},{2,0},{3,1},{4,6},{5,7},{6,4},{7,5},{8,10},{9,11},{10,... | collective-permute-start | bytes 786440 | tf_op jit(solution)/shard_map/ppermute | solution.py:283
  72.7 12.1 %collective-permute-start.19 = (f32[512,128]{1,0:T(8,128)S(1)}, f32[512,128]{1,0:T(8,128)S(1)}, u32[]{:S(2)}, u32[]{:S(2)}) collective-permute-start(f32[512,128]{1,0:T(8,128)S(1)} %copy-done.6), channel_id=1, source_target_pairs={{0,8},{4,12},{8,0},{12,4},{16,24},{20,28},{24,16},{28,20},{1,9},{5... | collective-permute-start | bytes 786440 | tf_op jit(solution)/shard_map/ppermute | solution.py:275
  76.2 11.0 %collective-permute-start.20 = (f32[512,128]{1,0:T(8,128)S(1)}, f32[512,128]{1,0:T(8,128)S(1)}, u32[]{:S(2)}, u32[]{:S(2)}) collective-permute-start(f32[512,128]{1,0:T(8,128)S(1)} %copy-done.5), channel_id=1, source_target_pairs={{0,24},{4,28},{8,16},{12,20},{16,8},{20,12},{24,0},{28,4},{1,25},{... | collective-permute-start | bytes 786440 | tf_op jit(solution)/shard_map/ppermute | solution.py:275
  79.3 12.1 %collective-permute-start.21 = (f32[512,128]{1,0:T(8,128)S(1)}, f32[512,128]{1,0:T(8,128)S(1)}, u32[]{:S(2)}, u32[]{:S(2)}) collective-permute-start(f32[512,128]{1,0:T(8,128)S(1)} %copy-done.4), channel_id=1, source_target_pairs={{0,16},{4,20},{8,24},{12,28},{16,0},{20,4},{24,8},{28,12},{1,17},{... | collective-permute-start | bytes 786440 | tf_op jit(solution)/shard_map/ppermute | solution.py:275
  80.8 11.7 %collective-permute-start.17 = (f32[512,128]{1,0:T(8,128)S(1)}, f32[512,128]{1,0:T(8,128)S(1)}, u32[]{:S(2)}, u32[]{:S(2)}) collective-permute-start(f32[512,128]{1,0:T(8,128)S(1)} %squares.6.own_ref), channel_id=1, source_target_pairs={{0,1},{1,0},{2,3},{3,2},{4,5},{5,4},{6,7},{7,6},{8,9},{9,8},{10,11... | collective-permute-start | bytes 786440 | tf_op jit(solution)/shard_map/ppermute | solution.py:283
  83.7 21.9 %collective-permute-start.13 = (f32[1,512,128]{2,1,0:T(8,128)S(1)}, f32[1,512,128]{2,1,0:T(8,128)S(1)}, u32[]{:S(2)}, u32[]{:S(2)}) collective-permute-start(f32[1,512,128]{2,1,0:T(8,128)S(1)} %bitcast.30), channel_id=1, source_target_pairs={{0,2},{1,3},{2,0},{3,1},{4,6},{5,7},{6,4},{7,5},{8,10},{9,11},{10,... | collective-permute-start | bytes 786440 | tf_op jit(solution)/shard_map/ppermute | solution.py:283
  91.5 13.3 %collective-permute-start.22 = (f32[512,128]{1,0:T(8,128)S(1)}, f32[512,128]{1,0:T(8,128)S(1)}, u32[]{:S(2)}, u32[]{:S(2)}) collective-permute-start(f32[512,128]{1,0:T(8,128)S(1)} %squares.7.own_ref), channel_id=1, source_target_pairs={{0,1},{1,0},{2,3},{3,2},{4,5},{5,4},{6,7},{7,6},{8,9},{9,8},{10,11... | collective-permute-start | bytes 786440 | tf_op jit(solution)/shard_map/ppermute | solution.py:283
  93.2 12.5 %collective-permute-start.18 = (f32[1,512,128]{2,1,0:T(8,128)S(1)}, f32[1,512,128]{2,1,0:T(8,128)S(1)}, u32[]{:S(2)}, u32[]{:S(2)}) collective-permute-start(f32[1,512,128]{2,1,0:T(8,128)S(1)} %bitcast.32), channel_id=1, source_target_pairs={{0,2},{1,3},{2,0},{3,1},{4,6},{5,7},{6,4},{7,5},{8,10},{9,11},{10,... | collective-permute-start | bytes 786440 | tf_op jit(solution)/shard_map/ppermute | solution.py:283
  105.6 14.2 %collective-permute-start.23 = (f32[1,512,128]{2,1,0:T(8,128)S(1)}, f32[1,512,128]{2,1,0:T(8,128)S(1)}, u32[]{:S(2)}, u32[]{:S(2)}) collective-permute-start(f32[1,512,128]{2,1,0:T(8,128)S(1)} %bitcast.33), channel_id=1, source_target_pairs={{0,2},{1,3},{2,0},{3,1},{4,6},{5,7},{6,4},{7,5},{8,10},{9,11},{10,... | collective-permute-start | bytes 786440 | tf_op jit(solution)/shard_map/ppermute | solution.py:283

commit v3 on v2

--- a/solution.py
+++ b/solution.py
@@ -26,7 +26,7 @@
     return lax.dot_general(points_ref[...], block, (((0,), (0,)), ((), ())), preferred_element_type=F32)
 
 
-def stream(block_of, live, points_ref, blocks_hbm, slots, done, base, count, emit):
+def stream(block_of, live, points_ref, blocks_hbm, slots, done, base, count, emit, before=None, behind=None):
     rows = slots.shape[1] // CHUNKS
 
     def copies(n):
@@ -56,6 +56,9 @@
         if n + 1 < count:
             start(n + 1)
 
+        if before:
+            before(n)
+
         @pl.when(live[base + n] != 0)
         def _(n=n):
             emit(n, product(points_ref, slots[n % 2]))
@@ -64,12 +67,27 @@
         def _(n=n):
             emit(n, None)
 
-
-def fetched_kernel(count, block_of, live, points_ref, blocks_hbm, out_ref, slots, done):
+        if behind:
+            behind(n)
+
+
+def fetched_kernel(count, block_of, live, points_ref, blocks_hbm, out_hbm, slots, done, stage, sent):
+    def copy(n):
+        return pltpu.make_async_copy(stage.at[n % 2], out_hbm.at[n], sent.at[n % 2])
+
+    def before(n):
+        if n >= 2:
+            copy(n - 2).wait()
+
     def emit(n, term):
-        out_ref[n] = jnp.zeros(out_ref.shape[1:], F32) if term is None else term
-
-    stream(block_of, live, points_ref, blocks_hbm, slots, done, 0, count, emit)
+        stage[n % 2] = jnp.zeros(stage.shape[1:], F32) if term is None else term
+
+    def behind(n):
+        copy(n).start()
+
+    stream(block_of, live, points_ref, blocks_hbm, slots, done, 0, count, emit, before, behind)
+    for n in range(max(count - 2, 0), count):
+        copy(n).wait()
 
 
 HBM = pl.BlockSpec(memory_space=pltpu.HBM)
@@ -91,9 +109,10 @@
     return pl.pallas_call(
         functools.partial(fetched_kernel, count),
         in_specs=[SMEM, SMEM, VMEM, pl.BlockSpec(memory_space=pltpu.HBM)],
-        out_specs=VMEM,
+        out_specs=HBM,
         out_shape=jax.ShapeDtypeStruct((count, batch, cells), F32),
-        scratch_shapes=slots_for(blocks),
+        scratch_shapes=slots_for(blocks)
+        + [pltpu.VMEM((2, batch, cells), F32), pltpu.SemaphoreType.DMA((2,))],
         compiler_params=params(10),
         cost_estimate=lasting(2.5 * count),
         name="fetched",

time: 121 us -> 121 us (level)
  starting transfers between devices: 26.3 us -> 35.5 us
  waiting for transfers between devices: 54.9 us -> 46.1 us
    ppermute x9, starting transfers between devices: 10 us -> 20.3 us  [turned(): return lax.ppermute(block, 'pts', [(i, i ^ distance) for i in range(count)])]
    ppermute x15, waiting for transfers between devices: 19.2 us -> 13.9 us  [swapped(): return lax.ppermute(block, 'grid', [(i, i ^ mask) for i in range(count)])]
    ppermute x9, waiting for transfers between devices: 35.7 us -> 32.2 us  [turned(): return lax.ppermute(block, 'pts', [(i, i ^ distance) for i in range(count)])]
    pallas_call x1, Pallas kernels: 6.51 us -> 4.61 us  [held(): pl.pallas_call(functools.partial(held_kernel, base), in_specs=[SMEM, SMEM...]
    pallas_call x1, Pallas kernels: 8.45 us -> 9.95 us  [fetched(): pl.pallas_call(functools.partial(fetched_kernel, count), in_specs=[SMEM,...]
  transfers between devices with their start and end apart: 24 -> 24, of which waited for: 11 -> 13; matrix products, arithmetic and copies ran while one was open for 0% -> 0% of each run, Pallas kernels for 22% -> 20%
where the time goes in v3:
time: 121 us
  waiting for transfers between devices  46.1 us (38%)
  starting transfers between devices  35.5 us (29%)
  Pallas kernels  34.4 us (28%)
  other arithmetic  2.48 us (2%)
  local copies, waits for them, and re-layouts  1.96 us (2%)
    ppermute x9, waiting for transfers between devices, turned(): return lax.ppermute(block, 'pts', [(i, i ^ distance) for i in range(count)])  32.2 us
    ppermute x9, starting transfers between devices, turned(): return lax.ppermute(block, 'pts', [(i, i ^ distance) for i in range(count)])  20.3 us
    ppermute x15, starting transfers between devices, swapped(): return lax.ppermute(block, 'grid', [(i, i ^ mask) for i in range(count)])  15.2 us
    ppermute x15, waiting for transfers between devices, swapped(): return lax.ppermute(block, 'grid', [(i, i ^ mask) for i in range(count)])  13.9 us
    pallas_call x1, Pallas kernels, fetched(): pl.pallas_call(functools.partial(fetched_kernel, count), in_specs=[SMEM,...  9.95 us
    pallas_call x1, Pallas kernels, near_sums(): pl.pallas_call(functools.partial(near_kernel, base, widths), in_specs=[SM...  9.43 us
    pallas_call x2, Pallas kernels, picked(): pl.pallas_call(picked_kernel, grid_spec=pltpu.PrefetchScalarGridSpec(num_...  5.96 us
    pallas_call x1, Pallas kernels, held(): pl.pallas_call(functools.partial(held_kernel, base), in_specs=[SMEM, SMEM...  4.61 us
  transfers between devices with their start and end apart: 24, of which 13 were waited for; matrix products, arithmetic and copies ran while one was open for 0% of the time, Pallas kernels for 20%

profile of v3, /device:TPU:0, one launch (start us, length us, event | category | flops | bytes accessed | tf_op | source)
XLA Modules:
  0.0 120.7 jit_solution(10213740471326810062)
XLA Ops:
  0.0 0.7 broadcast_xor_fusion
  0.7 0.8 fusion.5
  1.4 0.0 copy-start
  1.4 1.9 %copy-done = bf16[1,3200,512]{2,1,0:T(8,128)(2,1)S(1)} copy-done((bf16[1,3200,512]{2,1,0:T(8,128)(2,1)S(1)}, bf16[1,3200,512]{2,1,0:T(8,128)(2,1)}, u32[]{:S(2)}) %copy-start) | copy-done | bytes 3276824
  3.3 9.9 %fetched.1 = f32[3,512,512]{2,1,0:T(8,128)} custom-call(s32[16]{0:T(128)S(1)} %get-tuple-element.90.block_of, s32[16]{0:T(128)S(1)} %get-tuple-element.89.live, bf16[3200,512]{1,0:T(8,128)(2,1)S(1)} %bitcast.27, bf16[6,3200,512]{2,1,0:T(8,128)(2,1)} %bitcast.36), custom_call_target="tpu_custom_call" | custom-call | flops 7500000256 | bytes 22500000 | tf_op jit(solution)/shard_map/fetched/pallas_call | solution.py:109
  13.3 0.1 collective-permute-start
  13.4 0.0 copy-start.2
  13.4 0.0 copy-start.3
  13.4 4.6 %held.1 = (f32[512,512]{1,0:T(8,128)S(1)}, f32[512,512]{1,0:T(8,128)S(1)}) custom-call(s32[16]{0:T(128)S(1)} %get-tuple-element.90.block_of, s32[16]{0:T(128)S(1)} %get-tuple-element.89.live, bf16[3200,512]{1,0:T(8,128)(2,1)S(1)} %bitcast.28, bf16[6,3200,512]{2,1,0:T(8,128)(2,1)} %bitcast.37), custom_call_target="tpu_custom_call" | custom-call | flops 4000000000 | bytes 12000000 | tf_op jit(solution)/shard_map/held/pallas_call | solution.py:133
  18.0 0.1 pad_add_fusion.where
  18.1 2.4 %picked.3 = f32[256,1024]{1,0:T(8,128)S(1)} custom-call(s32[2]{0:T(128)S(1)} %pad_add_fusion.where, s32[1,2048]{1,0:T(1,128)S(1)} %bitcast.34, bf16[512,2048]{1,0:T(8,128)(2,1)S(1)} %copy-done.2), custom_call_target="tpu_custom_call" | custom-call | flops 3000000000 | bytes 9000000 | tf_op jit(solution)/shard_map/picked/pallas_call | solution.py:197
  20.5 1.2 collective-permute-start.1
  21.7 0.0 collective-permute-done.came_ref
  21.8 9.4 %near_sums.1 = (f32[512,128]{1,0:T(8,128)}, f32[512,128]{1,0:T(8,128)}, f32[512,128]{1,0:T(8,128)}, f32[512,128]{1,0:T(8,128)}, f32[512,128]{1,0:T(8,128)}, /*in...) custom-call(s32[16]{0:T(128)S(1)} %get-tuple-element.90.block_of, ...), custom_call_target="tpu_custom_call" | custom-call | flops 5000000000 | bytes 15000000 | tf_op jit(solution)/shard_map/near_sums/pallas_call | solution.py:165
  31.2 0.1 collective-permute-start.6
  31.3 0.7 collective-permute-start.2
  32.0 2.5 %collective-permute-start.3 = (f32[512,128]{1,0:T(8,128)}, f32[512,128]{1,0:T(8,128)S(1)}, u32[]{:S(2)}, u32[]{:S(2)}) collective-permute-start(f32[512,128]{1,0:T(8,128)} %get-tuple-element.54), channel_id=1, source_target_pairs={{0,24},{4,28},{8,16},{12,20},{16,8},{20,12},{24,0},{28,4},{1,25},{... | collective-permute-start | bytes 786440 | tf_op jit(solution)/shard_map/ppermute | solution.py:294
  34.4 0.4 collective-permute-start.4
  34.8 11.3 %collective-permute-done.1.mine_ref = f32[256,1024]{1,0:T(8,128)S(1)} collective-permute-done((f32[256,1024]{1,0:T(8,128)S(1)}, f32[256,1024]{1,0:T(8,128)S(1)}, u32[]{:S(2)}, u32[]{:S(2)}) %collective-permute-start.1) | collective-permute-done | bytes 1048608 | tf_op jit(solution)/shard_map/ppermute | solution.py:302
  46.1 0.0 collective-permute-done.2.refs_2_
  46.1 0.9 collective-permute-done.3.refs_3_
  47.0 1.4 %collective-permute-done.4.refs_4_ = f32[512,128]{1,0:T(8,128)S(1)} collective-permute-done((f32[512,128]{1,0:T(8,128)}, f32[512,128]{1,0:T(8,128)S(1)}, u32[]{:S(2)}, u32[]{:S(2)}) %collective-permute-start.4) | collective-permute-done | bytes 262176 | tf_op jit(solution)/shard_map/ppermute | solution.py:294
  48.4 0.0 collective-permute-start.5
  48.4 0.0 collective-permute-done.6.refs_1_
  48.4 1.2 %collective-permute-start.9 = (f32[512,128]{1,0:T(8,128)}, f32[512,128]{1,0:T(8,128)S(1)}, u32[]{:S(2)}, u32[]{:S(2)}) collective-permute-start(f32[512,128]{1,0:T(8,128)} %get-tuple-element.70), channel_id=1, source_target_pairs={{0,8},{4,12},{8,0},{12,4},{16,24},{20,28},{24,16},{28,20},{1,9},{5... | collective-permute-start | bytes 786440 | tf_op jit(solution)/shard_map/ppermute | solution.py:294
  49.6 0.6 collective-permute-start.10
  50.2 1.7 %collective-permute-start.11 = (f32[512,128]{1,0:T(8,128)}, f32[512,128]{1,0:T(8,128)S(1)}, u32[]{:S(2)}, u32[]{:S(2)}) collective-permute-start(f32[512,128]{1,0:T(8,128)} %get-tuple-element.72), channel_id=1, source_target_pairs={{0,16},{4,20},{8,24},{12,28},{16,0},{20,4},{24,8},{28,12},{1,17},{... | collective-permute-start | bytes 786440 | tf_op jit(solution)/shard_map/ppermute | solution.py:294
  51.9 0.1 squares.4.own_ref
  52.0 1.7 %collective-permute-start.7 = (f32[512,128]{1,0:T(8,128)S(1)}, f32[512,128]{1,0:T(8,128)S(1)}, u32[]{:S(2)}, u32[]{:S(2)}) collective-permute-start(f32[512,128]{1,0:T(8,128)S(1)} %squares.4.own_ref), channel_id=1, source_target_pairs={{0,1},{1,0},{2,3},{3,2},{4,5},{5,4},{6,7},{7,6},{8,9},{9,8},{10,11... | collective-permute-start | bytes 786440 | tf_op jit(solution)/shard_map/ppermute | solution.py:302
  53.7 3.5 %picked.2.kept_ref = bf16[512,1024]{1,0:T(8,128)(2,1)S(1)} custom-call(s32[2]{0:T(128)S(1)} %pad_add_fusion.where, s32[1,2048]{1,0:T(1,128)S(1)} %bitcast.35, bf16[512,2048]{1,0:T(8,128)(2,1)S(1)} %copy-done.2), custom_call_target="tpu_custom_call" | custom-call | flops 3000000000 | bytes 9000000 | tf_op jit(solution)/shard_map/picked/pallas_call | solution.py:197
  57.3 0.4 collective-permute-done.9.refs_2_
  57.7 1.3 %collective-permute-start.14 = (f32[512,128]{1,0:T(8,128)S(1)}, f32[512,128]{1,0:T(8,128)S(1)}, u32[]{:S(2)}, u32[]{:S(2)}) collective-permute-start(f32[512,128]{1,0:T(8,128)S(1)} %copy-done.9), channel_id=1, source_target_pairs={{0,8},{4,12},{8,0},{12,4},{16,24},{20,28},{24,16},{28,20},{1,9},{5... | collective-permute-start | bytes 786440 | tf_op jit(solution)/shard_map/ppermute | solution.py:294
  59.0 4.1 %collective-permute-done.10.refs_3_ = f32[512,128]{1,0:T(8,128)S(1)} collective-permute-done((f32[512,128]{1,0:T(8,128)}, f32[512,128]{1,0:T(8,128)S(1)}, u32[]{:S(2)}, u32[]{:S(2)}) %collective-permute-start.10) | collective-permute-done | bytes 262176 | tf_op jit(solution)/shard_map/ppermute | solution.py:294
  63.2 2.3 %collective-permute-start.15 = (f32[512,128]{1,0:T(8,128)S(1)}, f32[512,128]{1,0:T(8,128)S(1)}, u32[]{:S(2)}, u32[]{:S(2)}) collective-permute-start(f32[512,128]{1,0:T(8,128)S(1)} %copy-done.8), channel_id=1, source_target_pairs={{0,24},{4,28},{8,16},{12,20},{16,8},{20,12},{24,0},{28,4},{1,25},{... | collective-permute-start | bytes 786440 | tf_op jit(solution)/shard_map/ppermute | solution.py:294
  65.5 0.0 collective-permute-done.11.refs_4_
  65.5 0.4 collective-permute-start.16
  65.9 0.1 squares.5.own_ref
  66.0 0.0 collective-permute-done.7.came_ref
  66.0 2.1 %collective-permute-start.12 = (f32[512,128]{1,0:T(8,128)S(1)}, f32[512,128]{1,0:T(8,128)S(1)}, u32[]{:S(2)}, u32[]{:S(2)}) collective-permute-start(f32[512,128]{1,0:T(8,128)S(1)} %squares.5.own_ref), channel_id=1, source_target_pairs={{0,1},{1,0},{2,3},{3,2},{4,5},{5,4},{6,7},{7,6},{8,9},{9,8},{10,11... | collective-permute-start | bytes 786440 | tf_op jit(solution)/shard_map/ppermute | solution.py:302
  68.1 0.0 collective-permute-done.5.other_ref
  68.1 0.8 joined.1.joined_ref
  68.9 0.8 shares.4
  69.8 3.0 %collective-permute-start.8 = (f32[1,512,128]{2,1,0:T(8,128)S(1)}, f32[1,512,128]{2,1,0:T(8,128)S(1)}, u32[]{:S(2)}, u32[]{:S(2)}) collective-permute-start(f32[1,512,128]{2,1,0:T(8,128)S(1)} %bitcast.31), channel_id=1, source_target_pairs={{0,2},{1,3},{2,0},{3,1},{4,6},{5,7},{6,4},{7,5},{8,10},{9,11},{10,... | collective-permute-start | bytes 786440 | tf_op jit(solution)/shard_map/ppermute | solution.py:302
  72.8 1.3 %collective-permute-start.19 = (f32[512,128]{1,0:T(8,128)S(1)}, f32[512,128]{1,0:T(8,128)S(1)}, u32[]{:S(2)}, u32[]{:S(2)}) collective-permute-start(f32[512,128]{1,0:T(8,128)S(1)} %copy-done.6), channel_id=1, source_target_pairs={{0,8},{4,12},{8,0},{12,4},{16,24},{20,28},{24,16},{28,20},{1,9},{5... | collective-permute-start | bytes 786440 | tf_op jit(solution)/shard_map/ppermute | solution.py:294
  74.1 0.1 collective-permute-done.15.refs_3_
  74.1 2.6 %collective-permute-start.20 = (f32[512,128]{1,0:T(8,128)S(1)}, f32[512,128]{1,0:T(8,128)S(1)}, u32[]{:S(2)}, u32[]{:S(2)}) collective-permute-start(f32[512,128]{1,0:T(8,128)S(1)} %copy-done.5), channel_id=1, source_target_pairs={{0,24},{4,28},{8,16},{12,20},{16,8},{20,12},{24,0},{28,4},{1,25},{... | collective-permute-start | bytes 786440 | tf_op jit(solution)/shard_map/ppermute | solution.py:294
  76.8 2.1 %collective-permute-done.16.refs_4_ = f32[512,128]{1,0:T(8,128)S(1)} collective-permute-done((f32[512,128]{1,0:T(8,128)S(1)}, f32[512,128]{1,0:T(8,128)S(1)}, u32[]{:S(2)}, u32[]{:S(2)}) %collective-permute-start.16) | collective-permute-done | bytes 262176 | tf_op jit(solution)/shard_map/ppermute | solution.py:294
  78.9 0.1 squares.6.own_ref
  79.0 2.5 %collective-permute-start.17 = (f32[512,128]{1,0:T(8,128)S(1)}, f32[512,128]{1,0:T(8,128)S(1)}, u32[]{:S(2)}, u32[]{:S(2)}) collective-permute-start(f32[512,128]{1,0:T(8,128)S(1)} %squares.6.own_ref), channel_id=1, source_target_pairs={{0,1},{1,0},{2,3},{3,2},{4,5},{5,4},{6,7},{7,6},{8,9},{9,8},{10,11... | collective-permute-start | bytes 786440 | tf_op jit(solution)/shard_map/ppermute | solution.py:302
  81.6 0.8 shares.5
  82.4 1.1 collective-permute-done.8
  83.5 1.3 %collective-permute-start.13 = (f32[1,512,128]{2,1,0:T(8,128)S(1)}, f32[1,512,128]{2,1,0:T(8,128)S(1)}, u32[]{:S(2)}, u32[]{:S(2)}) collective-permute-start(f32[1,512,128]{2,1,0:T(8,128)S(1)} %bitcast.30), channel_id=1, source_target_pairs={{0,2},{1,3},{2,0},{3,1},{4,6},{5,7},{6,4},{7,5},{8,10},{9,11},{10,... | collective-permute-start | bytes 786440 | tf_op jit(solution)/shard_map/ppermute | solution.py:302
  84.8 1.3 %collective-permute-done.20.refs_3_ = f32[512,128]{1,0:T(8,128)S(1)} collective-permute-done((f32[512,128]{1,0:T(8,128)S(1)}, f32[512,128]{1,0:T(8,128)S(1)}, u32[]{:S(2)}, u32[]{:S(2)}) %collective-permute-start.20) | collective-permute-done | bytes 262176 | tf_op jit(solution)/shard_map/ppermute | solution.py:294
  86.1 3.6 %collective-permute-done.21.refs_4_ = f32[512,128]{1,0:T(8,128)S(1)} collective-permute-done((f32[512,128]{1,0:T(8,128)S(1)}, f32[512,128]{1,0:T(8,128)S(1)}, u32[]{:S(2)}, u32[]{:S(2)}) %collective-permute-start.21) | collective-permute-done | bytes 262176 | tf_op jit(solution)/shard_map/ppermute | solution.py:294
  89.7 0.1 squares.7.own_ref
  89.8 2.5 %collective-permute-start.22 = (f32[512,128]{1,0:T(8,128)S(1)}, f32[512,128]{1,0:T(8,128)S(1)}, u32[]{:S(2)}, u32[]{:S(2)}) collective-permute-start(f32[512,128]{1,0:T(8,128)S(1)} %squares.7.own_ref), channel_id=1, source_target_pairs={{0,1},{1,0},{2,3},{3,2},{4,5},{5,4},{6,7},{7,6},{8,9},{9,8},{10,11... | collective-permute-start | bytes 786440 | tf_op jit(solution)/shard_map/ppermute | solution.py:302
  92.3 0.8 shares.6
  93.1 3.6 %collective-permute-start.18 = (f32[1,512,128]{2,1,0:T(8,128)S(1)}, f32[1,512,128]{2,1,0:T(8,128)S(1)}, u32[]{:S(2)}, u32[]{:S(2)}) collective-permute-start(f32[1,512,128]{2,1,0:T(8,128)S(1)} %bitcast.32), channel_id=1, source_target_pairs={{0,2},{1,3},{2,0},{3,1},{4,6},{5,7},{6,4},{7,5},{8,10},{9,11},{10,... | collective-permute-start | bytes 786440 | tf_op jit(solution)/shard_map/ppermute | solution.py:302
  96.7 6.3 %collective-permute-done.22.came_ref = f32[512,128]{1,0:T(8,128)S(1)} collective-permute-done((f32[512,128]{1,0:T(8,128)S(1)}, f32[512,128]{1,0:T(8,128)S(1)}, u32[]{:S(2)}, u32[]{:S(2)}) %collective-permute-start.22) | collective-permute-done | bytes 262176 | tf_op jit(solution)/shard_map/ppermute | solution.py:302
  103.0 0.8 shares.7
  103.8 2.4 %collective-permute-start.23 = (f32[1,512,128]{2,1,0:T(8,128)S(1)}, f32[1,512,128]{2,1,0:T(8,128)S(1)}, u32[]{:S(2)}, u32[]{:S(2)}) collective-permute-start(f32[1,512,128]{2,1,0:T(8,128)S(1)} %bitcast.33), channel_id=1, source_target_pairs={{0,2},{1,3},{2,0},{3,1},{4,6},{5,7},{6,4},{7,5},{8,10},{9,11},{10,... | collective-permute-start | bytes 786440 | tf_op jit(solution)/shard_map/ppermute | solution.py:302
  106.3 8.8 %collective-permute-done.18 = f32[1,512,128]{2,1,0:T(8,128)S(1)} collective-permute-done((f32[1,512,128]{2,1,0:T(8,128)S(1)}, f32[1,512,128]{2,1,0:T(8,128)S(1)}, u32[]{:S(2)}, u32[]{:S(2)}) %collective-permute-start.18) | collective-permute-done | bytes 262176 | tf_op jit(solution)/shard_map/ppermute | solution.py:302
  115.2 4.6 %collective-permute-done.23 = f32[1,512,128]{2,1,0:T(8,128)S(1)} collective-permute-done((f32[1,512,128]{2,1,0:T(8,128)S(1)}, f32[1,512,128]{2,1,0:T(8,128)S(1)}, u32[]{:S(2)}, u32[]{:S(2)}) %collective-permute-start.23) | collective-permute-done | bytes 262176 | tf_op jit(solution)/shard_map/ppermute | solution.py:302
  119.8 0.9 pad_maximum_fusion
  (26 shorter events, 0.2 us)
Async XLA Ops:
  1.4 1.9 %copy-start = (bf16[1,3200,512]{2,1,0:T(8,128)(2,1)S(1)}, bf16[1,3200,512]{2,1,0:T(8,128)(2,1)}, u32[]{:S(2)}) copy-start(bf16[1,3200,512]{2,1,0:T(8,128)(2,1)} %param.8) | copy-start | bytes 9830404
  3.3 10.0 %copy-start.1 = (bf16[1,3200,512]{2,1,0:T(8,128)(2,1)S(1)}, bf16[1,3200,512]{2,1,0:T(8,128)(2,1)}, u32[]{:S(2)}) copy-start(bf16[1,3200,512]{2,1,0:T(8,128)(2,1)} %param.8) | copy-start | bytes 9830404
  13.3 8.4 %collective-permute-start = (f32[3,512,512]{2,1,0:T(8,128)}, f32[3,512,512]{2,1,0:T(8,128)}, u32[]{:S(2)}, u32[]{:S(2)}) collective-permute-start(f32[3,512,512]{2,1,0:T(8,128)} %fetched.1), channel_id=1, source_target_pairs={{0,4},{4,0},{8,12},{12,8},{16,20},{20,16},{24,28},{28,24},{1,5},{5... | collective-permute-start | bytes 9437192 | tf_op jit(solution)/shard_map/ppermute | solution.py:294
  13.4 4.7 %copy-start.2 = (bf16[512,2048]{1,0:T(8,128)(2,1)S(1)}, bf16[512,2048]{1,0:T(8,128)(2,1)}, u32[]{:S(2)}) copy-start(bf16[512,2048]{1,0:T(8,128)(2,1)} %gram_ref.1) | copy-start | bytes 6291460
  13.4 4.7 %copy-start.3 = (s32[2048]{0:T(1024)S(1)}, s32[2048]{0:T(1024)}, u32[]{:S(2)}) copy-start(s32[2048]{0:T(1024)} %param.11) | copy-start | bytes 24580
  20.5 25.6 %collective-permute-start.1 = (f32[256,1024]{1,0:T(8,128)S(1)}, f32[256,1024]{1,0:T(8,128)S(1)}, u32[]{:S(2)}, u32[]{:S(2)}) collective-permute-start(f32[256,1024]{1,0:T(8,128)S(1)} %picked.3), channel_id=1, source_target_pairs={{0,1},{1,0},{2,3},{3,2},{4,5},{5,4},{6,7},{7,6},{8,9},{9,8},{10,11... | collective-permute-start | bytes 3145736 | tf_op jit(solution)/shard_map/ppermute | solution.py:302
  31.2 17.2 %collective-permute-start.6 = (f32[512,512]{1,0:T(8,128)S(1)}, f32[512,512]{1,0:T(8,128)S(1)}, u32[]{:S(2)}, u32[]{:S(2)}) collective-permute-start(f32[512,512]{1,0:T(8,128)S(1)} %get-tuple-element.66), channel_id=1, source_target_pairs={{0,4},{4,0},{8,12},{12,8},{16,20},{20,16},{24,28},{28,24},{1,5},{5... | collective-permute-start | bytes 3145736 | tf_op jit(solution)/shard_map/ppermute | solution.py:294
  31.3 14.8 %collective-permute-start.2 = (f32[512,128]{1,0:T(8,128)}, f32[512,128]{1,0:T(8,128)S(1)}, u32[]{:S(2)}, u32[]{:S(2)}) collective-permute-start(f32[512,128]{1,0:T(8,128)} %get-tuple-element.50), channel_id=1, source_target_pairs={{0,8},{4,12},{8,0},{12,4},{16,24},{20,28},{24,16},{28,20},{1,9},{5... | collective-permute-start | bytes 786440 | tf_op jit(solution)/shard_map/ppermute | solution.py:294
  32.0 15.0 %collective-permute-start.3 = (f32[512,128]{1,0:T(8,128)}, f32[512,128]{1,0:T(8,128)S(1)}, u32[]{:S(2)}, u32[]{:S(2)}) collective-permute-start(f32[512,128]{1,0:T(8,128)} %get-tuple-element.54), channel_id=1, source_target_pairs={{0,24},{4,28},{8,16},{12,20},{16,8},{20,12},{24,0},{28,4},{1,25},{... | collective-permute-start | bytes 786440 | tf_op jit(solution)/shard_map/ppermute | solution.py:294
  34.4 13.9 %collective-permute-start.4 = (f32[512,128]{1,0:T(8,128)}, f32[512,128]{1,0:T(8,128)S(1)}, u32[]{:S(2)}, u32[]{:S(2)}) collective-permute-start(f32[512,128]{1,0:T(8,128)} %get-tuple-element.58), channel_id=1, source_target_pairs={{0,16},{4,20},{8,24},{12,28},{16,0},{20,4},{24,8},{28,12},{1,17},{... | collective-permute-start | bytes 786440 | tf_op jit(solution)/shard_map/ppermute | solution.py:294
  48.4 19.7 %collective-permute-start.5 = (f32[256,1024]{1,0:T(8,128)S(1)}, f32[256,1024]{1,0:T(8,128)S(1)}, u32[]{:S(2)}, u32[]{:S(2)}) collective-permute-start(f32[256,1024]{1,0:T(8,128)S(1)} %collective-permute-done.1.mine_ref), channel_id=1, source_target_pairs={{0,4},{4,0},{8,12},{12,8},{16,20},{20,16},{24,28},{28,24},{1,5},{5... | collective-permute-start | bytes 3145736 | tf_op jit(solution)/shard_map/ppermute | solution.py:294
  48.4 9.3 %collective-permute-start.9 = (f32[512,128]{1,0:T(8,128)}, f32[512,128]{1,0:T(8,128)S(1)}, u32[]{:S(2)}, u32[]{:S(2)}) collective-permute-start(f32[512,128]{1,0:T(8,128)} %get-tuple-element.70), channel_id=1, source_target_pairs={{0,8},{4,12},{8,0},{12,4},{16,24},{20,28},{24,16},{28,20},{1,9},{5... | collective-permute-start | bytes 786440 | tf_op jit(solution)/shard_map/ppermute | solution.py:294
  49.6 13.6 %collective-permute-start.10 = (f32[512,128]{1,0:T(8,128)}, f32[512,128]{1,0:T(8,128)S(1)}, u32[]{:S(2)}, u32[]{:S(2)}) collective-permute-start(f32[512,128]{1,0:T(8,128)} %get-tuple-element.71), channel_id=1, source_target_pairs={{0,24},{4,28},{8,16},{12,20},{16,8},{20,12},{24,0},{28,4},{1,25},{... | collective-permute-start | bytes 786440 | tf_op jit(solution)/shard_map/ppermute | solution.py:294
  50.2 15.3 %collective-permute-start.11 = (f32[512,128]{1,0:T(8,128)}, f32[512,128]{1,0:T(8,128)S(1)}, u32[]{:S(2)}, u32[]{:S(2)}) collective-permute-start(f32[512,128]{1,0:T(8,128)} %get-tuple-element.72), channel_id=1, source_target_pairs={{0,16},{4,20},{8,24},{12,28},{16,0},{20,4},{24,8},{28,12},{1,17},{... | collective-permute-start | bytes 786440 | tf_op jit(solution)/shard_map/ppermute | solution.py:294
  52.0 5.7 %copy-start.9 = (f32[512,128]{1,0:T(8,128)S(1)}, f32[512,128]{1,0:T(8,128)}, u32[]{:S(2)}) copy-start(f32[512,128]{1,0:T(8,128)} %get-tuple-element.77) | copy-start | bytes 786436
  52.0 11.2 %copy-start.8 = (f32[512,128]{1,0:T(8,128)S(1)}, f32[512,128]{1,0:T(8,128)}, u32[]{:S(2)}) copy-start(f32[512,128]{1,0:T(8,128)} %get-tuple-element.78) | copy-start | bytes 786436
  52.0 13.5 %copy-start.7 = (f32[512,128]{1,0:T(8,128)S(1)}, f32[512,128]{1,0:T(8,128)}, u32[]{:S(2)}) copy-start(f32[512,128]{1,0:T(8,128)} %get-tuple-element.79) | copy-start | bytes 786436
  52.0 14.0 %collective-permute-start.7 = (f32[512,128]{1,0:T(8,128)S(1)}, f32[512,128]{1,0:T(8,128)S(1)}, u32[]{:S(2)}, u32[]{:S(2)}) collective-permute-start(f32[512,128]{1,0:T(8,128)S(1)} %squares.4.own_ref), channel_id=1, source_target_pairs={{0,1},{1,0},{2,3},{3,2},{4,5},{5,4},{6,7},{7,6},{8,9},{9,8},{10,11... | collective-permute-start | bytes 786440 | tf_op jit(solution)/shard_map/ppermute | solution.py:302
  57.7 15.1 %collective-permute-start.14 = (f32[512,128]{1,0:T(8,128)S(1)}, f32[512,128]{1,0:T(8,128)S(1)}, u32[]{:S(2)}, u32[]{:S(2)}) collective-permute-start(f32[512,128]{1,0:T(8,128)S(1)} %copy-done.9), channel_id=1, source_target_pairs={{0,8},{4,12},{8,0},{12,4},{16,24},{20,28},{24,16},{28,20},{1,9},{5... | collective-permute-start | bytes 786440 | tf_op jit(solution)/shard_map/ppermute | solution.py:294
  63.2 11.0 %collective-permute-start.15 = (f32[512,128]{1,0:T(8,128)S(1)}, f32[512,128]{1,0:T(8,128)S(1)}, u32[]{:S(2)}, u32[]{:S(2)}) collective-permute-start(f32[512,128]{1,0:T(8,128)S(1)} %copy-done.8), channel_id=1, source_target_pairs={{0,24},{4,28},{8,16},{12,20},{16,8},{20,12},{24,0},{28,4},{1,25},{... | collective-permute-start | bytes 786440 | tf_op jit(solution)/shard_map/ppermute | solution.py:294
  65.5 13.4 %collective-permute-start.16 = (f32[512,128]{1,0:T(8,128)S(1)}, f32[512,128]{1,0:T(8,128)S(1)}, u32[]{:S(2)}, u32[]{:S(2)}) collective-permute-start(f32[512,128]{1,0:T(8,128)S(1)} %copy-done.7), channel_id=1, source_target_pairs={{0,16},{4,20},{8,24},{12,28},{16,0},{20,4},{24,8},{28,12},{1,17},{... | collective-permute-start | bytes 786440 | tf_op jit(solution)/shard_map/ppermute | solution.py:294
  66.0 13.0 %collective-permute-start.12 = (f32[512,128]{1,0:T(8,128)S(1)}, f32[512,128]{1,0:T(8,128)S(1)}, u32[]{:S(2)}, u32[]{:S(2)}) collective-permute-start(f32[512,128]{1,0:T(8,128)S(1)} %squares.5.own_ref), channel_id=1, source_target_pairs={{0,1},{1,0},{2,3},{3,2},{4,5},{5,4},{6,7},{7,6},{8,9},{9,8},{10,11... | collective-permute-start | bytes 786440 | tf_op jit(solution)/shard_map/ppermute | solution.py:302
  68.9 3.9 %copy-start.6 = (f32[512,128]{1,0:T(8,128)S(1)}, f32[512,128]{1,0:T(8,128)}, u32[]{:S(2)}) copy-start(f32[512,128]{1,0:T(8,128)} %get-tuple-element.84) | copy-start | bytes 786436
  68.9 5.2 %copy-start.5 = (f32[512,128]{1,0:T(8,128)S(1)}, f32[512,128]{1,0:T(8,128)}, u32[]{:S(2)}) copy-start(f32[512,128]{1,0:T(8,128)} %get-tuple-element.85) | copy-start | bytes 786436
  68.9 10.0 %copy-start.4 = (f32[512,128]{1,0:T(8,128)S(1)}, f32[512,128]{1,0:T(8,128)}, u32[]{:S(2)}) copy-start(f32[512,128]{1,0:T(8,128)} %get-tuple-element.86) | copy-start | bytes 786436
  69.8 13.7 %collective-permute-start.8 = (f32[1,512,128]{2,1,0:T(8,128)S(1)}, f32[1,512,128]{2,1,0:T(8,128)S(1)}, u32[]{:S(2)}, u32[]{:S(2)}) collective-permute-start(f32[1,512,128]{2,1,0:T(8,128)S(1)} %bitcast.31), channel_id=1, source_target_pairs={{0,2},{1,3},{2,0},{3,1},{4,6},{5,7},{6,4},{7,5},{8,10},{9,11},{10,... | collective-permute-start | bytes 786440 | tf_op jit(solution)/shard_map/ppermute | solution.py:302
  72.8 12.0 %collective-permute-start.19 = (f32[512,128]{1,0:T(8,128)S(1)}, f32[512,128]{1,0:T(8,128)S(1)}, u32[]{:S(2)}, u32[]{:S(2)}) collective-permute-start(f32[512,128]{1,0:T(8,128)S(1)} %copy-done.6), channel_id=1, source_target_pairs={{0,8},{4,12},{8,0},{12,4},{16,24},{20,28},{24,16},{28,20},{1,9},{5... | collective-permute-start | bytes 786440 | tf_op jit(solution)/shard_map/ppermute | solution.py:294
  74.1 12.0 %collective-permute-start.20 = (f32[512,128]{1,0:T(8,128)S(1)}, f32[512,128]{1,0:T(8,128)S(1)}, u32[]{:S(2)}, u32[]{:S(2)}) collective-permute-start(f32[512,128]{1,0:T(8,128)S(1)} %copy-done.5), channel_id=1, source_target_pairs={{0,24},{4,28},{8,16},{12,20},{16,8},{20,12},{24,0},{28,4},{1,25},{... | collective-permute-start | bytes 786440 | tf_op jit(solution)/shard_map/ppermute | solution.py:294
  78.9 10.8 %collective-permute-start.21 = (f32[512,128]{1,0:T(8,128)S(1)}, f32[512,128]{1,0:T(8,128)S(1)}, u32[]{:S(2)}, u32[]{:S(2)}) collective-permute-start(f32[512,128]{1,0:T(8,128)S(1)} %copy-done.4), channel_id=1, source_target_pairs={{0,16},{4,20},{8,24},{12,28},{16,0},{20,4},{24,8},{28,12},{1,17},{... | collective-permute-start | bytes 786440 | tf_op jit(solution)/shard_map/ppermute | solution.py:294
  79.0 13.3 %collective-permute-start.17 = (f32[512,128]{1,0:T(8,128)S(1)}, f32[512,128]{1,0:T(8,128)S(1)}, u32[]{:S(2)}, u32[]{:S(2)}) collective-permute-start(f32[512,128]{1,0:T(8,128)S(1)} %squares.6.own_ref), channel_id=1, source_target_pairs={{0,1},{1,0},{2,3},{3,2},{4,5},{5,4},{6,7},{7,6},{8,9},{9,8},{10,11... | collective-permute-start | bytes 786440 | tf_op jit(solution)/shard_map/ppermute | solution.py:302
  83.5 22.8 %collective-permute-start.13 = (f32[1,512,128]{2,1,0:T(8,128)S(1)}, f32[1,512,128]{2,1,0:T(8,128)S(1)}, u32[]{:S(2)}, u32[]{:S(2)}) collective-permute-start(f32[1,512,128]{2,1,0:T(8,128)S(1)} %bitcast.30), channel_id=1, source_target_pairs={{0,2},{1,3},{2,0},{3,1},{4,6},{5,7},{6,4},{7,5},{8,10},{9,11},{10,... | collective-permute-start | bytes 786440 | tf_op jit(solution)/shard_map/ppermute | solution.py:302
  89.8 13.2 %collective-permute-start.22 = (f32[512,128]{1,0:T(8,128)S(1)}, f32[512,128]{1,0:T(8,128)S(1)}, u32[]{:S(2)}, u32[]{:S(2)}) collective-permute-start(f32[512,128]{1,0:T(8,128)S(1)} %squares.7.own_ref), channel_id=1, source_target_pairs={{0,1},{1,0},{2,3},{3,2},{4,5},{5,4},{6,7},{7,6},{8,9},{9,8},{10,11... | collective-permute-start | bytes 786440 | tf_op jit(solution)/shard_map/ppermute | solution.py:302
  93.1 22.0 %collective-permute-start.18 = (f32[1,512,128]{2,1,0:T(8,128)S(1)}, f32[1,512,128]{2,1,0:T(8,128)S(1)}, u32[]{:S(2)}, u32[]{:S(2)}) collective-permute-start(f32[1,512,128]{2,1,0:T(8,128)S(1)} %bitcast.32), channel_id=1, source_target_pairs={{0,2},{1,3},{2,0},{3,1},{4,6},{5,7},{6,4},{7,5},{8,10},{9,11},{10,... | collective-permute-start | bytes 786440 | tf_op jit(solution)/shard_map/ppermute | solution.py:302
  103.8 16.0 %collective-permute-start.23 = (f32[1,512,128]{2,1,0:T(8,128)S(1)}, f32[1,512,128]{2,1,0:T(8,128)S(1)}, u32[]{:S(2)}, u32[]{:S(2)}) collective-permute-start(f32[1,512,128]{2,1,0:T(8,128)S(1)} %bitcast.33), channel_id=1, source_target_pairs={{0,2},{1,3},{2,0},{3,1},{4,6},{5,7},{6,4},{7,5},{8,10},{9,11},{10,... | collective-permute-start | bytes 786440 | tf_op jit(solution)/shard_map/ppermute | solution.py:302

commit v4 on v2

--- a/solution.py
+++ b/solution.py
@@ -11,7 +11,7 @@
 F32 = jnp.float32
 WIDTHS = (128, 128, 128, 128)
 ORDER = (0, 1, 2, 3)
-HOLD = {0: (), 1: (), 2: ((0, 1),), 3: ((0, 1),)}
+HOLD = {0: (), 1: (), 2: ((0, 1),), 3: ((1, 1),)}
 AFTER = ((), (), (('got', 0),), (('got', 1), ('squared', 0)))
 
 

time: 121 us -> 122 us (level); the launches traced: 121 us -> 123 us
  starting transfers between devices: 26.3 us -> 35.2 us
  Pallas kernels: 34.8 us -> 29.2 us
    ppermute x15, starting transfers between devices: 16.3 us -> 24 us  [swapped(): return lax.ppermute(block, 'grid', [(i, i ^ mask) for i in range(count)])]
    ppermute x9, waiting for transfers between devices: 35.7 us -> 28.6 us  [turned(): return lax.ppermute(block, 'pts', [(i, i ^ distance) for i in range(count)])]
    ppermute x15, waiting for transfers between devices: 19.2 us -> 25.5 us  [swapped(): return lax.ppermute(block, 'grid', [(i, i ^ mask) for i in range(count)])]
    pallas_call x1, Pallas kernels: 9.44 us -> 3.87 us  [near_sums(): pl.pallas_call(functools.partial(near_kernel, base, widths), in_specs=[SM...]
  transfers between devices with their start and end apart: 24 -> 24, of which waited for: 11 -> 14; matrix products, arithmetic and copies ran while one was open for 0% -> 0% of each run, Pallas kernels for 22% -> 17%
where the time goes in v4:
time: 122 us; the launch traced here: 123 us
  waiting for transfers between devices  54.1 us (44%)
  starting transfers between devices  35.2 us (29%)
  Pallas kernels  29.2 us (24%)
  other arithmetic  2.48 us (2%)
  local copies, waits for them, and re-layouts  1.96 us (2%)
    ppermute x9, waiting for transfers between devices, turned(): return lax.ppermute(block, 'pts', [(i, i ^ distance) for i in range(count)])  28.6 us
    ppermute x15, waiting for transfers between devices, swapped(): return lax.ppermute(block, 'grid', [(i, i ^ mask) for i in range(count)])  25.5 us
    ppermute x15, starting transfers between devices, swapped(): return lax.ppermute(block, 'grid', [(i, i ^ mask) for i in range(count)])  24 us
    ppermute x9, starting transfers between devices, turned(): return lax.ppermute(block, 'pts', [(i, i ^ distance) for i in range(count)])  11.2 us
    pallas_call x1, Pallas kernels, fetched(): pl.pallas_call(functools.partial(fetched_kernel, count), in_specs=[SMEM,...  8.38 us
    pallas_call x1, Pallas kernels, held(): pl.pallas_call(functools.partial(held_kernel, base), in_specs=[SMEM, SMEM...  6.49 us
    pallas_call x2, Pallas kernels, picked(): pl.pallas_call(picked_kernel, grid_spec=pltpu.PrefetchScalarGridSpec(num_...  5.96 us
    pallas_call x1, Pallas kernels, near_sums(): pl.pallas_call(functools.partial(near_kernel, base, widths), in_specs=[SM...  3.87 us
  transfers between devices with their start and end apart: 24, of which 14 were waited for; matrix products, arithmetic and copies ran while one was open for 0% of the time, Pallas kernels for 17%

profile of v4, /device:TPU:0, one launch (start us, length us, event | category | flops | bytes accessed | tf_op | source)
XLA Modules:
  0.0 123.2 jit_solution(7086075223509743450)
XLA Ops:
  0.0 0.7 broadcast_xor_fusion
  0.7 0.8 fusion.5
  1.4 0.0 copy-start
  1.4 1.9 %copy-done = bf16[1,3200,512]{2,1,0:T(8,128)(2,1)S(1)} copy-done((bf16[1,3200,512]{2,1,0:T(8,128)(2,1)S(1)}, bf16[1,3200,512]{2,1,0:T(8,128)(2,1)}, u32[]{:S(2)}) %copy-start) | copy-done | bytes 3276824
  3.3 8.4 %fetched.1 = f32[3,512,512]{2,1,0:T(8,128)} custom-call(s32[16]{0:T(128)S(1)} %get-tuple-element.90.block_of, s32[16]{0:T(128)S(1)} %get-tuple-element.89.live, bf16[3200,512]{1,0:T(8,128)(2,1)S(1)} %bitcast.27, bf16[6,3200,512]{2,1,0:T(8,128)(2,1)} %bitcast.36), custom_call_target="tpu_custom_call" | custom-call | flops 7500000256 | bytes 22500000 | tf_op jit(solution)/shard_map/fetched/pallas_call | solution.py:91
  11.7 0.1 collective-permute-start
  11.8 0.0 copy-start.2
  11.8 0.0 copy-start.3
  11.9 6.5 %held.1 = (f32[512,512]{1,0:T(8,128)S(1)}, f32[512,512]{1,0:T(8,128)S(1)}) custom-call(s32[16]{0:T(128)S(1)} %get-tuple-element.90.block_of, s32[16]{0:T(128)S(1)} %get-tuple-element.89.live, bf16[3200,512]{1,0:T(8,128)(2,1)S(1)} %bitcast.28, bf16[6,3200,512]{2,1,0:T(8,128)(2,1)} %bitcast.37), custom_call_target="tpu_custom_call" | custom-call | flops 4000000000 | bytes 12000000 | tf_op jit(solution)/shard_map/held/pallas_call | solution.py:114
  18.3 0.1 pad_add_fusion.where
  18.4 2.4 %picked.3 = f32[256,1024]{1,0:T(8,128)S(1)} custom-call(s32[2]{0:T(128)S(1)} %pad_add_fusion.where, s32[1,2048]{1,0:T(1,128)S(1)} %bitcast.34, bf16[512,2048]{1,0:T(8,128)(2,1)S(1)} %copy-done.2), custom_call_target="tpu_custom_call" | custom-call | flops 3000000000 | bytes 9000000 | tf_op jit(solution)/shard_map/picked/pallas_call | solution.py:178
  20.9 1.2 collective-permute-start.1
  22.1 3.9 %near_sums.1 = (f32[512,128]{1,0:T(8,128)}, f32[512,128]{1,0:T(8,128)}, f32[512,128]{1,0:T(8,128)}, f32[512,128]{1,0:T(8,128)}, f32[512,128]{1,0:T(8,128)}, /*in...) custom-call(s32[16]{0:T(128)S(1)} %get-tuple-element.90.block_of, ...), custom_call_target="tpu_custom_call" | custom-call | flops 5000000000 | bytes 15000000 | tf_op jit(solution)/shard_map/near_sums/pallas_call | solution.py:146
  25.9 3.9 %collective-permute-start.6 = (f32[512,512]{1,0:T(8,128)S(1)}, f32[512,512]{1,0:T(8,128)S(1)}, u32[]{:S(2)}, u32[]{:S(2)}) collective-permute-start(f32[512,512]{1,0:T(8,128)S(1)} %get-tuple-element.66), channel_id=1, source_target_pairs={{0,4},{4,0},{8,12},{12,8},{16,20},{20,16},{24,28},{28,24},{1,5},{5... | collective-permute-start | bytes 3145736 | tf_op jit(solution)/shard_map/ppermute | solution.py:275
  29.8 4.1 %collective-permute-start.2 = (f32[512,128]{1,0:T(8,128)}, f32[512,128]{1,0:T(8,128)S(1)}, u32[]{:S(2)}, u32[]{:S(2)}) collective-permute-start(f32[512,128]{1,0:T(8,128)} %get-tuple-element.50), channel_id=1, source_target_pairs={{0,8},{4,12},{8,0},{12,4},{16,24},{20,28},{24,16},{28,20},{1,9},{5... | collective-permute-start | bytes 786440 | tf_op jit(solution)/shard_map/ppermute | solution.py:275
  33.9 4.0 %collective-permute-start.3 = (f32[512,128]{1,0:T(8,128)}, f32[512,128]{1,0:T(8,128)S(1)}, u32[]{:S(2)}, u32[]{:S(2)}) collective-permute-start(f32[512,128]{1,0:T(8,128)} %get-tuple-element.54), channel_id=1, source_target_pairs={{0,24},{4,28},{8,16},{12,20},{16,8},{20,12},{24,0},{28,4},{1,25},{... | collective-permute-start | bytes 786440 | tf_op jit(solution)/shard_map/ppermute | solution.py:275
  38.0 0.6 collective-permute-start.4
  38.5 5.4 %collective-permute-done.1.mine_ref = f32[256,1024]{1,0:T(8,128)S(1)} collective-permute-done((f32[256,1024]{1,0:T(8,128)S(1)}, f32[256,1024]{1,0:T(8,128)S(1)}, u32[]{:S(2)}, u32[]{:S(2)}) %collective-permute-start.1) | collective-permute-done | bytes 1048608 | tf_op jit(solution)/shard_map/ppermute | solution.py:283
  43.9 0.0 collective-permute-done.2.refs_2_
  43.9 6.5 %collective-permute-done.3.refs_3_ = f32[512,128]{1,0:T(8,128)S(1)} collective-permute-done((f32[512,128]{1,0:T(8,128)}, f32[512,128]{1,0:T(8,128)S(1)}, u32[]{:S(2)}, u32[]{:S(2)}) %collective-permute-start.3) | collective-permute-done | bytes 262176 | tf_op jit(solution)/shard_map/ppermute | solution.py:275
  50.5 1.4 %collective-permute-done.4.refs_4_ = f32[512,128]{1,0:T(8,128)S(1)} collective-permute-done((f32[512,128]{1,0:T(8,128)}, f32[512,128]{1,0:T(8,128)S(1)}, u32[]{:S(2)}, u32[]{:S(2)}) %collective-permute-start.4) | collective-permute-done | bytes 262176 | tf_op jit(solution)/shard_map/ppermute | solution.py:275
  51.9 0.0 collective-permute-start.5
  51.9 0.0 collective-permute-done.6.refs_1_
  51.9 1.7 %collective-permute-start.9 = (f32[512,128]{1,0:T(8,128)}, f32[512,128]{1,0:T(8,128)S(1)}, u32[]{:S(2)}, u32[]{:S(2)}) collective-permute-start(f32[512,128]{1,0:T(8,128)} %get-tuple-element.70), channel_id=1, source_target_pairs={{0,8},{4,12},{8,0},{12,4},{16,24},{20,28},{24,16},{28,20},{1,9},{5... | collective-permute-start | bytes 786440 | tf_op jit(solution)/shard_map/ppermute | solution.py:275
  53.6 0.3 collective-permute-start.10
  53.9 1.5 %collective-permute-start.11 = (f32[512,128]{1,0:T(8,128)}, f32[512,128]{1,0:T(8,128)S(1)}, u32[]{:S(2)}, u32[]{:S(2)}) collective-permute-start(f32[512,128]{1,0:T(8,128)} %get-tuple-element.72), channel_id=1, source_target_pairs={{0,16},{4,20},{8,24},{12,28},{16,0},{20,4},{24,8},{28,12},{1,17},{... | collective-permute-start | bytes 786440 | tf_op jit(solution)/shard_map/ppermute | solution.py:275
  55.4 0.1 squares.4.own_ref
  55.5 0.4 collective-permute-start.7
  55.9 3.5 %picked.2.kept_ref = bf16[512,1024]{1,0:T(8,128)(2,1)S(1)} custom-call(s32[2]{0:T(128)S(1)} %pad_add_fusion.where, s32[1,2048]{1,0:T(1,128)S(1)} %bitcast.35, bf16[512,2048]{1,0:T(8,128)(2,1)S(1)} %copy-done.2), custom_call_target="tpu_custom_call" | custom-call | flops 3000000000 | bytes 9000000 | tf_op jit(solution)/shard_map/picked/pallas_call | solution.py:178
  59.5 1.8 %collective-permute-done.9.refs_2_ = f32[512,128]{1,0:T(8,128)S(1)} collective-permute-done((f32[512,128]{1,0:T(8,128)}, f32[512,128]{1,0:T(8,128)S(1)}, u32[]{:S(2)}, u32[]{:S(2)}) %collective-permute-start.9) | collective-permute-done | bytes 262176 | tf_op jit(solution)/shard_map/ppermute | solution.py:275
  61.2 1.7 %collective-permute-start.14 = (f32[512,128]{1,0:T(8,128)S(1)}, f32[512,128]{1,0:T(8,128)S(1)}, u32[]{:S(2)}, u32[]{:S(2)}) collective-permute-start(f32[512,128]{1,0:T(8,128)S(1)} %copy-done.9), channel_id=1, source_target_pairs={{0,8},{4,12},{8,0},{12,4},{16,24},{20,28},{24,16},{28,20},{1,9},{5... | collective-permute-start | bytes 786440 | tf_op jit(solution)/shard_map/ppermute | solution.py:275
  62.9 3.9 %collective-permute-done.10.refs_3_ = f32[512,128]{1,0:T(8,128)S(1)} collective-permute-done((f32[512,128]{1,0:T(8,128)}, f32[512,128]{1,0:T(8,128)S(1)}, u32[]{:S(2)}, u32[]{:S(2)}) %collective-permute-start.10) | collective-permute-done | bytes 262176 | tf_op jit(solution)/shard_map/ppermute | solution.py:275
  66.8 2.6 %collective-permute-start.15 = (f32[512,128]{1,0:T(8,128)S(1)}, f32[512,128]{1,0:T(8,128)S(1)}, u32[]{:S(2)}, u32[]{:S(2)}) collective-permute-start(f32[512,128]{1,0:T(8,128)S(1)} %copy-done.8), channel_id=1, source_target_pairs={{0,24},{4,28},{8,16},{12,20},{16,8},{20,12},{24,0},{28,4},{1,25},{... | collective-permute-start | bytes 786440 | tf_op jit(solution)/shard_map/ppermute | solution.py:275
  69.4 0.0 collective-permute-done.11.refs_4_
  69.5 0.3 collective-permute-start.16
  69.7 0.1 squares.5.own_ref
  69.8 0.0 collective-permute-done.7.came_ref
  69.9 0.8 collective-permute-start.12
  70.6 0.8 joined.1.joined_ref
  71.5 0.8 shares.4
  72.3 2.7 %collective-permute-start.8 = (f32[1,512,128]{2,1,0:T(8,128)S(1)}, f32[1,512,128]{2,1,0:T(8,128)S(1)}, u32[]{:S(2)}, u32[]{:S(2)}) collective-permute-start(f32[1,512,128]{2,1,0:T(8,128)S(1)} %bitcast.31), channel_id=1, source_target_pairs={{0,2},{1,3},{2,0},{3,1},{4,6},{5,7},{6,4},{7,5},{8,10},{9,11},{10,... | collective-permute-start | bytes 786440 | tf_op jit(solution)/shard_map/ppermute | solution.py:283
  75.0 0.4 collective-permute-start.19
  75.4 2.7 %collective-permute-done.15.refs_3_ = f32[512,128]{1,0:T(8,128)S(1)} collective-permute-done((f32[512,128]{1,0:T(8,128)S(1)}, f32[512,128]{1,0:T(8,128)S(1)}, u32[]{:S(2)}, u32[]{:S(2)}) %collective-permute-start.15) | collective-permute-done | bytes 262176 | tf_op jit(solution)/shard_map/ppermute | solution.py:275
  78.1 2.6 %collective-permute-start.20 = (f32[512,128]{1,0:T(8,128)S(1)}, f32[512,128]{1,0:T(8,128)S(1)}, u32[]{:S(2)}, u32[]{:S(2)}) collective-permute-start(f32[512,128]{1,0:T(8,128)S(1)} %copy-done.5), channel_id=1, source_target_pairs={{0,24},{4,28},{8,16},{12,20},{16,8},{20,12},{24,0},{28,4},{1,25},{... | collective-permute-start | bytes 786440 | tf_op jit(solution)/shard_map/ppermute | solution.py:275
  80.7 1.6 %collective-permute-done.16.refs_4_ = f32[512,128]{1,0:T(8,128)S(1)} collective-permute-done((f32[512,128]{1,0:T(8,128)S(1)}, f32[512,128]{1,0:T(8,128)S(1)}, u32[]{:S(2)}, u32[]{:S(2)}) %collective-permute-start.16) | collective-permute-done | bytes 262176 | tf_op jit(solution)/shard_map/ppermute | solution.py:275
  82.3 0.3 collective-permute-start.21
  82.6 0.1 squares.6.own_ref
  82.8 0.6 collective-permute-start.17
  83.4 0.8 shares.5
  84.2 1.6 %collective-permute-done.8 = f32[1,512,128]{2,1,0:T(8,128)S(1)} collective-permute-done((f32[1,512,128]{2,1,0:T(8,128)S(1)}, f32[1,512,128]{2,1,0:T(8,128)S(1)}, u32[]{:S(2)}, u32[]{:S(2)}) %collective-permute-start.8) | collective-permute-done | bytes 262176 | tf_op jit(solution)/shard_map/ppermute | solution.py:283
  85.7 1.3 %collective-permute-start.13 = (f32[1,512,128]{2,1,0:T(8,128)S(1)}, f32[1,512,128]{2,1,0:T(8,128)S(1)}, u32[]{:S(2)}, u32[]{:S(2)}) collective-permute-start(f32[1,512,128]{2,1,0:T(8,128)S(1)} %bitcast.30), channel_id=1, source_target_pairs={{0,2},{1,3},{2,0},{3,1},{4,6},{5,7},{6,4},{7,5},{8,10},{9,11},{10,... | collective-permute-start | bytes 786440 | tf_op jit(solution)/shard_map/ppermute | solution.py:283
  87.0 2.0 %collective-permute-done.20.refs_3_ = f32[512,128]{1,0:T(8,128)S(1)} collective-permute-done((f32[512,128]{1,0:T(8,128)S(1)}, f32[512,128]{1,0:T(8,128)S(1)}, u32[]{:S(2)}, u32[]{:S(2)}) %collective-permute-start.20) | collective-permute-done | bytes 262176 | tf_op jit(solution)/shard_map/ppermute | solution.py:275
  89.0 5.5 %collective-permute-done.21.refs_4_ = f32[512,128]{1,0:T(8,128)S(1)} collective-permute-done((f32[512,128]{1,0:T(8,128)S(1)}, f32[512,128]{1,0:T(8,128)S(1)}, u32[]{:S(2)}, u32[]{:S(2)}) %collective-permute-start.21) | collective-permute-done | bytes 262176 | tf_op jit(solution)/shard_map/ppermute | solution.py:275
  94.5 0.1 squares.7.own_ref
  94.7 0.4 collective-permute-start.22
  95.1 0.4 collective-permute-done.17.came_ref
  95.5 0.8 shares.6
  96.3 1.9 %collective-permute-start.18 = (f32[1,512,128]{2,1,0:T(8,128)S(1)}, f32[1,512,128]{2,1,0:T(8,128)S(1)}, u32[]{:S(2)}, u32[]{:S(2)}) collective-permute-start(f32[1,512,128]{2,1,0:T(8,128)S(1)} %bitcast.32), channel_id=1, source_target_pairs={{0,2},{1,3},{2,0},{3,1},{4,6},{5,7},{6,4},{7,5},{8,10},{9,11},{10,... | collective-permute-start | bytes 786440 | tf_op jit(solution)/shard_map/ppermute | solution.py:283
  98.2 8.8 %collective-permute-done.22.came_ref = f32[512,128]{1,0:T(8,128)S(1)} collective-permute-done((f32[512,128]{1,0:T(8,128)S(1)}, f32[512,128]{1,0:T(8,128)S(1)}, u32[]{:S(2)}, u32[]{:S(2)}) %collective-permute-start.22) | collective-permute-done | bytes 262176 | tf_op jit(solution)/shard_map/ppermute | solution.py:283
  106.9 0.8 shares.7
  107.7 2.0 %collective-permute-start.23 = (f32[1,512,128]{2,1,0:T(8,128)S(1)}, f32[1,512,128]{2,1,0:T(8,128)S(1)}, u32[]{:S(2)}, u32[]{:S(2)}) collective-permute-start(f32[1,512,128]{2,1,0:T(8,128)S(1)} %bitcast.33), channel_id=1, source_target_pairs={{0,2},{1,3},{2,0},{3,1},{4,6},{5,7},{6,4},{7,5},{8,10},{9,11},{10,... | collective-permute-start | bytes 786440 | tf_op jit(solution)/shard_map/ppermute | solution.py:283
  109.8 0.7 collective-permute-done.18
  110.5 11.8 %collective-permute-done.23 = f32[1,512,128]{2,1,0:T(8,128)S(1)} collective-permute-done((f32[1,512,128]{2,1,0:T(8,128)S(1)}, f32[1,512,128]{2,1,0:T(8,128)S(1)}, u32[]{:S(2)}, u32[]{:S(2)}) %collective-permute-start.23) | collective-permute-done | bytes 262176 | tf_op jit(solution)/shard_map/ppermute | solution.py:283
  122.3 0.9 pad_maximum_fusion
  (26 shorter events, 0.2 us)
Async XLA Ops:
  1.4 1.9 %copy-start = (bf16[1,3200,512]{2,1,0:T(8,128)(2,1)S(1)}, bf16[1,3200,512]{2,1,0:T(8,128)(2,1)}, u32[]{:S(2)}) copy-start(bf16[1,3200,512]{2,1,0:T(8,128)(2,1)} %param.8) | copy-start | bytes 9830404
  3.3 8.5 %copy-start.1 = (bf16[1,3200,512]{2,1,0:T(8,128)(2,1)S(1)}, bf16[1,3200,512]{2,1,0:T(8,128)(2,1)}, u32[]{:S(2)}) copy-start(bf16[1,3200,512]{2,1,0:T(8,128)(2,1)} %param.8) | copy-start | bytes 9830404
  11.7 10.3 %collective-permute-start = (f32[3,512,512]{2,1,0:T(8,128)}, f32[3,512,512]{2,1,0:T(8,128)}, u32[]{:S(2)}, u32[]{:S(2)}) collective-permute-start(f32[3,512,512]{2,1,0:T(8,128)} %fetched.1), channel_id=1, source_target_pairs={{0,4},{4,0},{8,12},{12,8},{16,20},{20,16},{24,28},{28,24},{1,5},{5... | collective-permute-start | bytes 9437192 | tf_op jit(solution)/shard_map/ppermute | solution.py:275
  11.8 6.6 %copy-start.2 = (bf16[512,2048]{1,0:T(8,128)(2,1)S(1)}, bf16[512,2048]{1,0:T(8,128)(2,1)}, u32[]{:S(2)}) copy-start(bf16[512,2048]{1,0:T(8,128)(2,1)} %gram_ref.1) | copy-start | bytes 6291460
  11.8 6.6 %copy-start.3 = (s32[2048]{0:T(1024)S(1)}, s32[2048]{0:T(1024)}, u32[]{:S(2)}) copy-start(s32[2048]{0:T(1024)} %param.11) | copy-start | bytes 24580
  20.9 23.1 %collective-permute-start.1 = (f32[256,1024]{1,0:T(8,128)S(1)}, f32[256,1024]{1,0:T(8,128)S(1)}, u32[]{:S(2)}, u32[]{:S(2)}) collective-permute-start(f32[256,1024]{1,0:T(8,128)S(1)} %picked.3), channel_id=1, source_target_pairs={{0,1},{1,0},{2,3},{3,2},{4,5},{5,4},{6,7},{7,6},{8,9},{9,8},{10,11... | collective-permute-start | bytes 3145736 | tf_op jit(solution)/shard_map/ppermute | solution.py:283
  25.9 26.0 %collective-permute-start.6 = (f32[512,512]{1,0:T(8,128)S(1)}, f32[512,512]{1,0:T(8,128)S(1)}, u32[]{:S(2)}, u32[]{:S(2)}) collective-permute-start(f32[512,512]{1,0:T(8,128)S(1)} %get-tuple-element.66), channel_id=1, source_target_pairs={{0,4},{4,0},{8,12},{12,8},{16,20},{20,16},{24,28},{28,24},{1,5},{5... | collective-permute-start | bytes 3145736 | tf_op jit(solution)/shard_map/ppermute | solution.py:275
  29.8 14.1 %collective-permute-start.2 = (f32[512,128]{1,0:T(8,128)}, f32[512,128]{1,0:T(8,128)S(1)}, u32[]{:S(2)}, u32[]{:S(2)}) collective-permute-start(f32[512,128]{1,0:T(8,128)} %get-tuple-element.50), channel_id=1, source_target_pairs={{0,8},{4,12},{8,0},{12,4},{16,24},{20,28},{24,16},{28,20},{1,9},{5... | collective-permute-start | bytes 786440 | tf_op jit(solution)/shard_map/ppermute | solution.py:275
  33.9 16.5 %collective-permute-start.3 = (f32[512,128]{1,0:T(8,128)}, f32[512,128]{1,0:T(8,128)S(1)}, u32[]{:S(2)}, u32[]{:S(2)}) collective-permute-start(f32[512,128]{1,0:T(8,128)} %get-tuple-element.54), channel_id=1, source_target_pairs={{0,24},{4,28},{8,16},{12,20},{16,8},{20,12},{24,0},{28,4},{1,25},{... | collective-permute-start | bytes 786440 | tf_op jit(solution)/shard_map/ppermute | solution.py:275
  38.0 13.9 %collective-permute-start.4 = (f32[512,128]{1,0:T(8,128)}, f32[512,128]{1,0:T(8,128)S(1)}, u32[]{:S(2)}, u32[]{:S(2)}) collective-permute-start(f32[512,128]{1,0:T(8,128)} %get-tuple-element.58), channel_id=1, source_target_pairs={{0,16},{4,20},{8,24},{12,28},{16,0},{20,4},{24,8},{28,12},{1,17},{... | collective-permute-start | bytes 786440 | tf_op jit(solution)/shard_map/ppermute | solution.py:275
  51.9 18.7 %collective-permute-start.5 = (f32[256,1024]{1,0:T(8,128)S(1)}, f32[256,1024]{1,0:T(8,128)S(1)}, u32[]{:S(2)}, u32[]{:S(2)}) collective-permute-start(f32[256,1024]{1,0:T(8,128)S(1)} %collective-permute-done.1.mine_ref), channel_id=1, source_target_pairs={{0,4},{4,0},{8,12},{12,8},{16,20},{20,16},{24,28},{28,24},{1,5},{5... | collective-permute-start | bytes 3145736 | tf_op jit(solution)/shard_map/ppermute | solution.py:275
  51.9 9.3 %collective-permute-start.9 = (f32[512,128]{1,0:T(8,128)}, f32[512,128]{1,0:T(8,128)S(1)}, u32[]{:S(2)}, u32[]{:S(2)}) collective-permute-start(f32[512,128]{1,0:T(8,128)} %get-tuple-element.70), channel_id=1, source_target_pairs={{0,8},{4,12},{8,0},{12,4},{16,24},{20,28},{24,16},{28,20},{1,9},{5... | collective-permute-start | bytes 786440 | tf_op jit(solution)/shard_map/ppermute | solution.py:275
  53.6 13.2 %collective-permute-start.10 = (f32[512,128]{1,0:T(8,128)}, f32[512,128]{1,0:T(8,128)S(1)}, u32[]{:S(2)}, u32[]{:S(2)}) collective-permute-start(f32[512,128]{1,0:T(8,128)} %get-tuple-element.71), channel_id=1, source_target_pairs={{0,24},{4,28},{8,16},{12,20},{16,8},{20,12},{24,0},{28,4},{1,25},{... | collective-permute-start | bytes 786440 | tf_op jit(solution)/shard_map/ppermute | solution.py:275
  53.9 15.6 %collective-permute-start.11 = (f32[512,128]{1,0:T(8,128)}, f32[512,128]{1,0:T(8,128)S(1)}, u32[]{:S(2)}, u32[]{:S(2)}) collective-permute-start(f32[512,128]{1,0:T(8,128)} %get-tuple-element.72), channel_id=1, source_target_pairs={{0,16},{4,20},{8,24},{12,28},{16,0},{20,4},{24,8},{28,12},{1,17},{... | collective-permute-start | bytes 786440 | tf_op jit(solution)/shard_map/ppermute | solution.py:275
  55.5 5.7 %copy-start.9 = (f32[512,128]{1,0:T(8,128)S(1)}, f32[512,128]{1,0:T(8,128)}, u32[]{:S(2)}) copy-start(f32[512,128]{1,0:T(8,128)} %get-tuple-element.77) | copy-start | bytes 786436
  55.5 11.3 %copy-start.8 = (f32[512,128]{1,0:T(8,128)S(1)}, f32[512,128]{1,0:T(8,128)}, u32[]{:S(2)}) copy-start(f32[512,128]{1,0:T(8,128)} %get-tuple-element.78) | copy-start | bytes 786436
  55.5 13.9 %copy-start.7 = (f32[512,128]{1,0:T(8,128)S(1)}, f32[512,128]{1,0:T(8,128)}, u32[]{:S(2)}) copy-start(f32[512,128]{1,0:T(8,128)} %get-tuple-element.79) | copy-start | bytes 786436
  55.5 14.3 %collective-permute-start.7 = (f32[512,128]{1,0:T(8,128)S(1)}, f32[512,128]{1,0:T(8,128)S(1)}, u32[]{:S(2)}, u32[]{:S(2)}) collective-permute-start(f32[512,128]{1,0:T(8,128)S(1)} %squares.4.own_ref), channel_id=1, source_target_pairs={{0,1},{1,0},{2,3},{3,2},{4,5},{5,4},{6,7},{7,6},{8,9},{9,8},{10,11... | collective-permute-start | bytes 786440 | tf_op jit(solution)/shard_map/ppermute | solution.py:283
  61.2 13.8 %collective-permute-start.14 = (f32[512,128]{1,0:T(8,128)S(1)}, f32[512,128]{1,0:T(8,128)S(1)}, u32[]{:S(2)}, u32[]{:S(2)}) collective-permute-start(f32[512,128]{1,0:T(8,128)S(1)} %copy-done.9), channel_id=1, source_target_pairs={{0,8},{4,12},{8,0},{12,4},{16,24},{20,28},{24,16},{28,20},{1,9},{5... | collective-permute-start | bytes 786440 | tf_op jit(solution)/shard_map/ppermute | solution.py:275
  66.8 11.3 %collective-permute-start.15 = (f32[512,128]{1,0:T(8,128)S(1)}, f32[512,128]{1,0:T(8,128)S(1)}, u32[]{:S(2)}, u32[]{:S(2)}) collective-permute-start(f32[512,128]{1,0:T(8,128)S(1)} %copy-done.8), channel_id=1, source_target_pairs={{0,24},{4,28},{8,16},{12,20},{16,8},{20,12},{24,0},{28,4},{1,25},{... | collective-permute-start | bytes 786440 | tf_op jit(solution)/shard_map/ppermute | solution.py:275
  69.5 12.9 %collective-permute-start.16 = (f32[512,128]{1,0:T(8,128)S(1)}, f32[512,128]{1,0:T(8,128)S(1)}, u32[]{:S(2)}, u32[]{:S(2)}) collective-permute-start(f32[512,128]{1,0:T(8,128)S(1)} %copy-done.7), channel_id=1, source_target_pairs={{0,16},{4,20},{8,24},{12,28},{16,0},{20,4},{24,8},{28,12},{1,17},{... | collective-permute-start | bytes 786440 | tf_op jit(solution)/shard_map/ppermute | solution.py:275
  69.9 12.9 %collective-permute-start.12 = (f32[512,128]{1,0:T(8,128)S(1)}, f32[512,128]{1,0:T(8,128)S(1)}, u32[]{:S(2)}, u32[]{:S(2)}) collective-permute-start(f32[512,128]{1,0:T(8,128)S(1)} %squares.5.own_ref), channel_id=1, source_target_pairs={{0,1},{1,0},{2,3},{3,2},{4,5},{5,4},{6,7},{7,6},{8,9},{9,8},{10,11... | collective-permute-start | bytes 786440 | tf_op jit(solution)/shard_map/ppermute | solution.py:283
  71.5 3.5 %copy-start.6 = (f32[512,128]{1,0:T(8,128)S(1)}, f32[512,128]{1,0:T(8,128)}, u32[]{:S(2)}) copy-start(f32[512,128]{1,0:T(8,128)} %get-tuple-element.84) | copy-start | bytes 786436
  71.5 6.6 %copy-start.5 = (f32[512,128]{1,0:T(8,128)S(1)}, f32[512,128]{1,0:T(8,128)}, u32[]{:S(2)}) copy-start(f32[512,128]{1,0:T(8,128)} %get-tuple-element.85) | copy-start | bytes 786436
  71.5 10.9 %copy-start.4 = (f32[512,128]{1,0:T(8,128)S(1)}, f32[512,128]{1,0:T(8,128)}, u32[]{:S(2)}) copy-start(f32[512,128]{1,0:T(8,128)} %get-tuple-element.86) | copy-start | bytes 786436
  72.3 13.4 %collective-permute-start.8 = (f32[1,512,128]{2,1,0:T(8,128)S(1)}, f32[1,512,128]{2,1,0:T(8,128)S(1)}, u32[]{:S(2)}, u32[]{:S(2)}) collective-permute-start(f32[1,512,128]{2,1,0:T(8,128)S(1)} %bitcast.31), channel_id=1, source_target_pairs={{0,2},{1,3},{2,0},{3,1},{4,6},{5,7},{6,4},{7,5},{8,10},{9,11},{10,... | collective-permute-start | bytes 786440 | tf_op jit(solution)/shard_map/ppermute | solution.py:283
  75.0 12.0 %collective-permute-start.19 = (f32[512,128]{1,0:T(8,128)S(1)}, f32[512,128]{1,0:T(8,128)S(1)}, u32[]{:S(2)}, u32[]{:S(2)}) collective-permute-start(f32[512,128]{1,0:T(8,128)S(1)} %copy-done.6), channel_id=1, source_target_pairs={{0,8},{4,12},{8,0},{12,4},{16,24},{20,28},{24,16},{28,20},{1,9},{5... | collective-permute-start | bytes 786440 | tf_op jit(solution)/shard_map/ppermute | solution.py:275
  78.1 11.0 %collective-permute-start.20 = (f32[512,128]{1,0:T(8,128)S(1)}, f32[512,128]{1,0:T(8,128)S(1)}, u32[]{:S(2)}, u32[]{:S(2)}) collective-permute-start(f32[512,128]{1,0:T(8,128)S(1)} %copy-done.5), channel_id=1, source_target_pairs={{0,24},{4,28},{8,16},{12,20},{16,8},{20,12},{24,0},{28,4},{1,25},{... | collective-permute-start | bytes 786440 | tf_op jit(solution)/shard_map/ppermute | solution.py:275
  82.3 12.2 %collective-permute-start.21 = (f32[512,128]{1,0:T(8,128)S(1)}, f32[512,128]{1,0:T(8,128)S(1)}, u32[]{:S(2)}, u32[]{:S(2)}) collective-permute-start(f32[512,128]{1,0:T(8,128)S(1)} %copy-done.4), channel_id=1, source_target_pairs={{0,16},{4,20},{8,24},{12,28},{16,0},{20,4},{24,8},{28,12},{1,17},{... | collective-permute-start | bytes 786440 | tf_op jit(solution)/shard_map/ppermute | solution.py:275
  82.8 12.7 %collective-permute-start.17 = (f32[512,128]{1,0:T(8,128)S(1)}, f32[512,128]{1,0:T(8,128)S(1)}, u32[]{:S(2)}, u32[]{:S(2)}) collective-permute-start(f32[512,128]{1,0:T(8,128)S(1)} %squares.6.own_ref), channel_id=1, source_target_pairs={{0,1},{1,0},{2,3},{3,2},{4,5},{5,4},{6,7},{7,6},{8,9},{9,8},{10,11... | collective-permute-start | bytes 786440 | tf_op jit(solution)/shard_map/ppermute | solution.py:283
  85.7 12.4 %collective-permute-start.13 = (f32[1,512,128]{2,1,0:T(8,128)S(1)}, f32[1,512,128]{2,1,0:T(8,128)S(1)}, u32[]{:S(2)}, u32[]{:S(2)}) collective-permute-start(f32[1,512,128]{2,1,0:T(8,128)S(1)} %bitcast.30), channel_id=1, source_target_pairs={{0,2},{1,3},{2,0},{3,1},{4,6},{5,7},{6,4},{7,5},{8,10},{9,11},{10,... | collective-permute-start | bytes 786440 | tf_op jit(solution)/shard_map/ppermute | solution.py:283
  94.7 12.3 %collective-permute-start.22 = (f32[512,128]{1,0:T(8,128)S(1)}, f32[512,128]{1,0:T(8,128)S(1)}, u32[]{:S(2)}, u32[]{:S(2)}) collective-permute-start(f32[512,128]{1,0:T(8,128)S(1)} %squares.7.own_ref), channel_id=1, source_target_pairs={{0,1},{1,0},{2,3},{3,2},{4,5},{5,4},{6,7},{7,6},{8,9},{9,8},{10,11... | collective-permute-start | bytes 786440 | tf_op jit(solution)/shard_map/ppermute | solution.py:283
  96.3 14.2 %collective-permute-start.18 = (f32[1,512,128]{2,1,0:T(8,128)S(1)}, f32[1,512,128]{2,1,0:T(8,128)S(1)}, u32[]{:S(2)}, u32[]{:S(2)}) collective-permute-start(f32[1,512,128]{2,1,0:T(8,128)S(1)} %bitcast.32), channel_id=1, source_target_pairs={{0,2},{1,3},{2,0},{3,1},{4,6},{5,7},{6,4},{7,5},{8,10},{9,11},{10,... | collective-permute-start | bytes 786440 | tf_op jit(solution)/shard_map/ppermute | solution.py:283
  107.7 14.5 %collective-permute-start.23 = (f32[1,512,128]{2,1,0:T(8,128)S(1)}, f32[1,512,128]{2,1,0:T(8,128)S(1)}, u32[]{:S(2)}, u32[]{:S(2)}) collective-permute-start(f32[1,512,128]{2,1,0:T(8,128)S(1)} %bitcast.33), channel_id=1, source_target_pairs={{0,2},{1,3},{2,0},{3,1},{4,6},{5,7},{6,4},{7,5},{8,10},{9,11},{10,... | collective-permute-start | bytes 786440 | tf_op jit(solution)/shard_map/ppermute | solution.py:283
